TPU v7x, 32 devices: a whole 2x2x4 slice. The times are simulated.
32 devices in a mesh: dp: 8 (over z, x), pair: 4 (over y, core).
Axes of the slice: x: 2, y: 2, z: 4, core: 2. Of those that a mesh axis runs over, the one named last changes fastest.
Arguments:
- patches: bfloat16 [128, 196, 768], P(('dp', 'pair')), may hold values from -6 to 6
- patch_order: int32 [128, 196], P(('dp', 'pair')), may hold values from 0 to 195, each once within a row
- counts: int32 [128], P(('dp', 'pair')), may hold values from 40 to 60
- master: float32 [11608064], P(('dp', 'pair'))
- moment1: float32 [11608064], P(('dp', 'pair')), may hold values from -1.4901161e-07 to 1.4901161e-07
- moment2: float32 [11608064], P(('dp', 'pair')), may hold values from 4.1350566e-16 to 1.6367932e-15
- block_rates: float32 [2], replicated, may hold values from 0.01 to 0.04
- clip_limit: float32 [1], replicated, may hold values from 0.0002 to 0.0004
- step_count: int32 [1], replicated, may hold values from 1 to 20
Outputs:
- loss: float32 [1], replicated
- grad_norm: float32 [1], replicated
- moment1_new: float32 [11608064], P(('dp', 'pair'))
- moment2_new: float32 [11608064], P(('dp', 'pair'))
- master_new: float32 [11608064], P(('dp', 'pair'))
Inputs may be any that keep to these rules, and one draw needn't show every extreme that they name: `patch_order`: each row is a permutation; the first count entries name the image's visible patches.
All inputs are finite; a program needn't handle non-finite values.
Results may differ from a plain program's by a relative error of at most 0.00035.
The roundings to bfloat16 on the way count: a program that leaves them out, or rounds other values in their place, can miss the bound.
Values may be sent and summed in bfloat16 or wider, within the bound.
A program may use at most 256 MiB of HBM per device.

v0:
```python
import jax
import jax.numpy as jnp
from jax import lax
from jax.sharding import PartitionSpec as P

PIX = 768
HEADS = 12
F = 3072
DHEADS = 16
FD = 2048
GRID = 14
KEEP = 64
D = 768
DD = 512
PATCHES = 196
ENC_PARAMS = 7672320


NORM_EPS = 1e-06
ADAM_EPS = 1e-08
BETA_ONE = 0.9
BETA_TWO = 0.95
DECAY = 0.05
NEG_FILL = -1000000000.0


def shapes():
    return [
        (PIX, D),
        (D, 3 * D),
        (D, D),
        (D, F),
        (F, D),
        (6, D),
        (D, DD),
        (DD, 3 * DD),
        (DD, DD),
        (DD, FD),
        (FD, DD),
        (DD, PIX),
        (6, DD),
        (1, DD),
    ]


def unpack(flat):
    parts = []
    offset = 0
    for shape in shapes():
        amount = shape[0] * shape[1]
        parts.append(flat[offset : offset + amount].reshape(shape))
        offset += amount
    return parts


def mult(left, right):
    return jnp.einsum("bsi,ij->bsj", left, right, preferred_element_type=jnp.float32)


def mult_back(grad, right):
    return jnp.einsum("bsj,ij->bsi", grad, right, preferred_element_type=jnp.float32)


def outer(left, grad):
    return jnp.einsum("bsi,bsj->ij", left, grad, preferred_element_type=jnp.float32)


def layer_norm(x, gain, shift):
    centered = x - jnp.mean(x, axis=-1, keepdims=True)
    scale = lax.rsqrt(jnp.mean(centered * centered, axis=-1, keepdims=True) + NORM_EPS)
    normed = centered * scale
    return (normed * gain + shift, normed, scale)


def norm_back(grad, normed, scale, gain):
    inner = grad * gain
    back = scale * (
        inner
        - jnp.mean(inner, axis=-1, keepdims=True)
        - normed * jnp.mean(inner * normed, axis=-1, keepdims=True)
    )
    return (back, jnp.sum(grad * normed, axis=(0, 1)), jnp.sum(grad, axis=(0, 1)))


def positions(width):
    index = jnp.arange(PATCHES)
    quarter = width // 4
    freq = 10000.0 ** (-jnp.arange(quarter).astype(jnp.float32) / quarter)
    row = (index // GRID).astype(jnp.float32)[:, None] * freq[None, :]
    column = (index % GRID).astype(jnp.float32)[:, None] * freq[None, :]
    return jnp.concatenate([jnp.sin(row), jnp.cos(row), jnp.sin(column), jnp.cos(column)], axis=1)


def attention_scores(query, keys, bias, size):
    scores = jnp.einsum("bqhd,bkhd->bhqk", query, keys, preferred_element_type=jnp.float32)
    return scores * size ** (-0.5) + bias[:, None, None, :]


def block_forward(x, weights, gains, heads, bias):
    triple_w, proj_w, up_w, down_w = weights
    batch, length, width = x.shape
    size = width // heads
    normed_one, plain_one, scale_one = layer_norm(x, gains[0], gains[1])
    entry = normed_one.astype(jnp.bfloat16)
    triple = mult(entry, triple_w).astype(jnp.bfloat16).reshape(batch, length, 3, heads, size)
    query, keys, values = (triple[:, :, 0], triple[:, :, 1], triple[:, :, 2])
    scores = attention_scores(query, keys, bias, size)
    top = jnp.max(scores, axis=-1, keepdims=True)
    log_total = top + jnp.log(jnp.sum(jnp.exp(scores - top), axis=-1, keepdims=True))
    attend = jnp.exp(scores - log_total).astype(jnp.bfloat16)
    mixed = jnp.einsum("bhqk,bkhd->bqhd", attend, values, preferred_element_type=jnp.float32)
    mixed = mixed.astype(jnp.bfloat16).reshape(batch, length, width)
    middle = x + mult(mixed, proj_w)
    normed_two, plain_two, scale_two = layer_norm(middle, gains[2], gains[3])
    inner = normed_two.astype(jnp.bfloat16)
    hidden = mult(inner, up_w)
    activated = jax.nn.gelu(hidden, approximate=False).astype(jnp.bfloat16)
    result = middle + mult(activated, down_w)
    saved = (
        entry,
        plain_one,
        scale_one,
        query,
        keys,
        values,
        log_total,
        mixed,
        plain_two,
        scale_two,
        inner,
        hidden,
        activated,
    )
    return (result, saved)


def block_backward(grad, weights, gains, heads, bias, saved):
    triple_w, proj_w, up_w, down_w = weights
    (
        entry,
        plain_one,
        scale_one,
        query,
        keys,
        values,
        log_total,
        mixed,
        plain_two,
        scale_two,
        inner,
        hidden,
        activated,
    ) = saved
    batch, length, width = grad.shape
    size = width // heads
    low_grad = grad.astype(jnp.bfloat16)
    grad_down = outer(activated, low_grad)
    grad_act = mult_back(low_grad, down_w)
    density = jnp.exp(-0.5 * hidden * hidden) * 0.3989422804014327
    cumulative = 0.5 * (1.0 + lax.erf(hidden * 0.7071067811865476))
    grad_hidden = (grad_act * (cumulative + hidden * density)).astype(jnp.bfloat16)
    grad_up = outer(inner, grad_hidden)
    back_two, gain_two, shift_two = norm_back(
        mult_back(grad_hidden, up_w), plain_two, scale_two, gains[2]
    )
    grad_mid = grad + back_two
    mid_low = grad_mid.astype(jnp.bfloat16)
    grad_proj = outer(mixed, mid_low)
    grad_mixed = mult_back(mid_low, proj_w).astype(jnp.bfloat16).reshape(batch, length, heads, size)
    attend = jnp.exp(attention_scores(query, keys, bias, size) - log_total)
    grad_att = jnp.einsum("bqhd,bkhd->bhqk", grad_mixed, values, preferred_element_type=jnp.float32)
    grad_values = jnp.einsum(
        "bhqk,bqhd->bkhd",
        attend.astype(jnp.bfloat16),
        grad_mixed,
        preferred_element_type=jnp.float32,
    )
    grad_scores = attend * (grad_att - jnp.sum(attend * grad_att, axis=-1, keepdims=True))
    grad_scores = grad_scores.astype(jnp.bfloat16)
    grad_query = jnp.einsum(
        "bhqk,bkhd->bqhd", grad_scores, keys, preferred_element_type=jnp.float32
    ) * size ** (-0.5)
    grad_keys = jnp.einsum(
        "bhqk,bqhd->bkhd", grad_scores, query, preferred_element_type=jnp.float32
    ) * size ** (-0.5)
    grad_triple = jnp.stack([grad_query, grad_keys, grad_values], axis=2)
    grad_triple = grad_triple.astype(jnp.bfloat16).reshape(batch, length, 3 * width)
    grad_triple_w = outer(entry, grad_triple)
    back_one, gain_one, shift_one = norm_back(
        mult_back(grad_triple, triple_w), plain_one, scale_one, gains[0]
    )
    grad_in = grad_mid + back_one
    gain_grads = jnp.stack([gain_one, shift_one, gain_two, shift_two])
    return (grad_in, (grad_triple_w, grad_proj, grad_up, grad_down), gain_grads)


def body(
    patches, patch_order, counts, master, moment1, moment2, block_rates, clip_limit, step_count
):
    local_masked = jnp.sum(PATCHES - counts).astype(jnp.float32)
    masked = lax.psum(local_masked, ("dp", "pair"))
    low_master = master.astype(jnp.bfloat16)
    parts = unpack(lax.all_gather(low_master, ("dp", "pair"), axis=0, tiled=True))
    enc_gains = parts[5].astype(jnp.float32)
    dec_gains = parts[12].astype(jnp.float32)
    slots = patch_order[:, :KEEP]
    live = jnp.arange(KEEP)[None, :] < counts[:, None]
    enc_bias = jnp.where(live, 0.0, NEG_FILL).astype(jnp.float32)
    seen = jnp.take_along_axis(patches, slots[:, :, None], axis=1)
    x_start = mult(seen, parts[0]) + jnp.take(positions(D), slots, axis=0)
    x_end, enc_saved = block_forward(x_start, tuple(parts[1:5]), enc_gains, HEADS, enc_bias)
    enc_normed, enc_plain, enc_scale = layer_norm(x_end, enc_gains[4], enc_gains[5])
    encoded = enc_normed.astype(jnp.bfloat16)
    entering = mult(encoded, parts[6])
    rank = jnp.argsort(patch_order, axis=1)
    shown = rank < counts[:, None]
    picked = jnp.take_along_axis(entering, jnp.minimum(rank, KEEP - 1)[:, :, None], axis=1)
    token = parts[13][0].astype(jnp.float32)
    y_start = jnp.where(shown[:, :, None], picked, token) + positions(DD)[None]
    dec_bias = jnp.zeros(shown.shape, jnp.float32)
    y_end, dec_saved = block_forward(y_start, tuple(parts[7:11]), dec_gains, DHEADS, dec_bias)
    final_normed, final_plain, final_scale = layer_norm(y_end, dec_gains[4], dec_gains[5])
    final = final_normed.astype(jnp.bfloat16)
    pred = mult(final, parts[11])
    pixels = patches.astype(jnp.float32)
    centered = pixels - jnp.mean(pixels, axis=-1, keepdims=True)
    target = centered * lax.rsqrt(jnp.mean(centered * centered, axis=-1, keepdims=True) + NORM_EPS)
    diff = pred - target
    hidden_mask = jnp.where(shown, 0.0, 1.0).astype(jnp.float32)
    loss_local = jnp.sum(jnp.mean(diff * diff, axis=-1) * hidden_mask)
    grad_pred = (diff * (hidden_mask[:, :, None] * (2.0 / PIX)) / masked).astype(jnp.bfloat16)
    again = unpack(lax.all_gather(low_master, ("dp", "pair"), axis=0, tiled=True))
    enc_back_gains = again[5].astype(jnp.float32)
    dec_back_gains = again[12].astype(jnp.float32)
    grad_head = outer(final, grad_pred)
    back_final, gain_final, shift_final = norm_back(
        mult_back(grad_pred, again[11]), final_plain, final_scale, dec_back_gains[4]
    )
    grad_y, dec_grads, dec_gain_grads = block_backward(
        back_final, tuple(again[7:11]), dec_back_gains, DHEADS, dec_bias, dec_saved
    )
    grad_token = jnp.sum(grad_y * hidden_mask[:, :, None], axis=(0, 1))
    grad_entering = jnp.take_along_axis(grad_y, slots[:, :, None], axis=1)
    grad_entering = jnp.where(live[:, :, None], grad_entering, 0.0).astype(jnp.bfloat16)
    grad_dec_embed = outer(encoded, grad_entering)
    back_enc, gain_enc, shift_enc = norm_back(
        mult_back(grad_entering, again[6]), enc_plain, enc_scale, enc_back_gains[4]
    )
    grad_x, enc_grads, enc_gain_grads = block_backward(
        back_enc, tuple(again[1:5]), enc_back_gains, HEADS, enc_bias, enc_saved
    )
    grad_embed = outer(seen, grad_x.astype(jnp.bfloat16))
    enc_norm_grads = jnp.concatenate([enc_gain_grads, jnp.stack([gain_enc, shift_enc])])
    dec_norm_grads = jnp.concatenate([dec_gain_grads, jnp.stack([gain_final, shift_final])])
    pieces = [
        grad_embed,
        enc_grads[0],
        enc_grads[1],
        enc_grads[2],
        enc_grads[3],
        enc_norm_grads,
        grad_dec_embed,
        dec_grads[0],
        dec_grads[1],
        dec_grads[2],
        dec_grads[3],
        grad_head,
        dec_norm_grads,
        grad_token[None],
    ]
    shard = master.shape[0]
    filled = sum((shape[0] * shape[1] for shape in shapes()))
    padding = jnp.zeros((shard * lax.axis_size(("dp", "pair")) - filled,), jnp.float32)
    flat = jnp.concatenate([piece.reshape(-1) for piece in pieces] + [padding])
    grad_share = lax.psum_scatter(flat, ("dp", "pair"), scatter_dimension=0, tiled=True)
    squares, loss_sum = lax.psum((jnp.sum(grad_share * grad_share), loss_local), ("dp", "pair"))
    grad_norm = jnp.sqrt(squares)
    loss = loss_sum / masked
    clipped = grad_share * (clip_limit[0] / (grad_norm + NORM_EPS))
    first = BETA_ONE * moment1 + (1.0 - BETA_ONE) * clipped
    second = BETA_TWO * moment2 + (1.0 - BETA_TWO) * clipped * clipped
    steps_done = step_count[0].astype(jnp.float32)
    position = lax.axis_index(("dp", "pair")) * shard + jnp.arange(shard)
    rate = jnp.where(position < ENC_PARAMS, block_rates[0], block_rates[1])
    update = (
        first
        / (1.0 - BETA_ONE**steps_done)
        / (jnp.sqrt(second / (1.0 - BETA_TWO**steps_done)) + ADAM_EPS)
    )
    master_new = master - rate * (update + DECAY * master)
    return (loss.reshape(1), grad_norm.reshape(1), first, second, master_new)


def solution(mesh):
    in_specs = (
        P(("dp", "pair"), None, None),
        P(("dp", "pair"), None),
        P(("dp", "pair")),
        P(("dp", "pair")),
        P(("dp", "pair")),
        P(("dp", "pair")),
        P(),
        P(),
        P(),
    )
    out_specs = (P(), P(), P(("dp", "pair")), P(("dp", "pair")), P(("dp", "pair")))
    return jax.shard_map(body, mesh=mesh, in_specs=in_specs, out_specs=out_specs, check_vma=False)
```

profile of v0, /device:TPU:0, one launch (start us, length us, event | category | flops | bytes accessed | tf_op | source)
XLA Modules:
  0.0 2068.6 jit_solution(8376311458875155277)
XLA Ops:
  8.7 9.0 reshape.529
  19.1 44.6 %psum.22 = f32[]{:T(128)} all-reduce(f32[]{:T(128)S(6)} %convert_element_type.222), channel_id=1, replica_groups=mesh['dp'=8,'pair'=4] {'dp','pair'}, use_global_device_ids=true, to_apply=%region_23.24 | all-reduce | flops 1 | bytes 8 | tf_op jit(solution)/shard_map/psum | solution.py:201
  80.1 199.0 %all-gather.3.cloned.1.call-done = bf16[32,1,362752]{2,1,0:T(2,128)(2,1)} async-done(((bf16[1,1,362752]{2,1,0:T(2,128)(2,1)}), bf16[32,1,362752]{2,1,0:T(2,128)(2,1)}) %all-gather.3.cloned.1.call-update) | async-done | bytes 23216144 | tf_op jit(solution)/shard_map/all_gather | solution.py:203
  279.1 489.9 %reduce = bf16[32,362752]{1,0:T(8,128)(2,1)} reduce(bf16[32,1,362752]{2,1,0:T(2,128)(2,1)} %all-gather.3.cloned.1.call-done, bf16[]{:T(256)} %constant.311), dimensions={1}, to_apply=%all-gather.reduce_sub_computation | reduce | bytes 46432256 | tf_op jit(solution)/shard_map/all_gather | solution.py:203
  769.0 55.4 %reshape.530 = bf16[11608064]{0:T(1024)(128)(2,1)} reshape(bf16[32,362752]{1,0:T(8,128)(2,1)} %reduce) | data formatting | bytes 46432256
  836.6 8.8 fusion.84
  889.9 8.2 reshape.534
  901.6 9.5 reshape.535
  916.2 7.1 fusion.19
  926.2 14.3 gather_fusion.2
  987.9 15.0 fusion.3
  1023.2 8.3 convolution_bitcast_fusion.8
  1031.5 10.4 multiply_reduce_fusion
  1042.0 6.8 multiply_convert_fusion
  1136.8 8.1 reshape.478
  1146.5 9.4 copy.139
  1155.9 10.8 reshape.481
  1205.3 14.6 dynamic-update-slice.6
  1219.9 26.4 %dynamic-update-slice.7 = f32[11608064]{0:T(1024)} dynamic-update-slice(f32[11608064]{0:T(1024)} %dynamic-update-slice.6, f32[786432]{0:T(1024)S(1)} %copy-done.18, s32[]{} %constant.319) | dynamic-update-slice | bytes 6291460
  1248.9 36.4 %dynamic-update-slice.9 = f32[11608064]{0:T(1024)} dynamic-update-slice(f32[11608064]{0:T(1024)} %constant_dynamic-update-slice_fusion.2, f32[1048576]{0:T(1024)} %bitcast.192, s32[]{} %constant.321) | dynamic-update-slice | bytes 8388612
  1285.3 36.6 %dynamic-update-slice.10 = f32[11608064]{0:T(1024)} dynamic-update-slice(f32[11608064]{0:T(1024)} %dynamic-update-slice.9, f32[1048576]{0:T(1024)} %bitcast.191, s32[]{} %constant.322) | dynamic-update-slice | bytes 8388612
  1321.9 13.8 dynamic-update-slice.11
  1340.5 667.5 %all-reduce.4.cloned.1.call-done = f32[11608064]{0:T(1024)} async-done(((f32[11608064]{0:T(1024)}), f32[11608064]{0:T(1024)}) %all-reduce.4.cloned.1.call-update) | async-done | bytes 46432272
  2010.4 40.1 %all-reduce.1 = (f32[]{:T(128)}, f32[]{:T(128)}) all-reduce(f32[]{:T(128)} %get-tuple-element.76, f32[]{:T(128)} %multiply_reduce_fusion.14), channel_id=1, replica_groups=mesh['dp'=8,'pair'=4] {'dp','pair'}, use_global_device_ids=true, to_apply=%region_21.22 | all-reduce | flops 2 | bytes 16 | tf_op jit(solution)/shard_map/psum | solution.py:276
  (509 shorter events, 295.7 us)
Async XLA Ops:
  7.2 56.5 %copy-start.91 = (s32[4,196]{1,0:T(4,128)S(1)}, s32[4,196]{1,0:T(4,128)}, u32[]{:S(2)}) copy-start(s32[4,196]{1,0:T(4,128)} %param.10) | copy-start | bytes 9412
  7.2 271.9 %all-gather.3.cloned.1.call-start = ((), (), s32[]{:S(2)}) async-start(), calls=%async_computation | async-start | bytes 47883264 | tf_op jit(solution)/shard_map/all_gather | solution.py:203
  17.7 1990.2 %all-reduce.4.cloned.1.call-start = ((), (), s32[]{:S(2)}) async-start(), calls=%async_computation.1 | async-start | bytes 92864512
  75.9 693.1 %copy-start.108 = (f32[4,196]{1,0:T(4,128)}, f32[4,196]{1,0:T(4,128)S(1)}, u32[]{:S(2)}) copy-start(f32[4,196]{1,0:T(4,128)S(1)} %broadcast_multiply_fusion) | copy-start | bytes 9412
  831.9 140.9 %copy-start.89 = (f32[512]{0:T(512)}, f32[512]{0:T(512)S(1)}, u32[]{:S(2)}) copy-start(f32[512]{0:T(512)S(1)} %slice_convert_fusion.2) | copy-start | bytes 6148
  835.1 13.8 copy-start.1
  860.2 121.2 %copy-start.79 = (f32[512]{0:T(512)}, f32[512]{0:T(512)S(1)}, u32[]{:S(2)}) copy-start(f32[512]{0:T(512)S(1)} %get-tuple-element.63) | copy-start | bytes 6148
  860.2 157.2 %copy-start.77 = (f32[512]{0:T(512)}, f32[512]{0:T(512)S(1)}, u32[]{:S(2)}) copy-start(f32[512]{0:T(512)S(1)} %get-tuple-element.64) | copy-start | bytes 6148
  872.0 39.1 %copy-start.104 = (f32[768]{0:T(1024)}, f32[768]{0:T(1024)S(1)}, u32[]{:S(2)}) copy-start(f32[768]{0:T(1024)S(1)} %get-tuple-element.58) | copy-start | bytes 9220
  872.0 39.1 %copy-start.125 = (f32[768]{0:T(1024)}, f32[768]{0:T(1024)S(1)}, u32[]{:S(2)}) copy-start(f32[768]{0:T(1024)S(1)} %get-tuple-element.57) | copy-start | bytes 9220
  872.0 53.1 %copy-start.81 = (f32[768]{0:T(1024)}, f32[768]{0:T(1024)S(1)}, u32[]{:S(2)}) copy-start(f32[768]{0:T(1024)S(1)} %get-tuple-element.55) | copy-start | bytes 9220
  872.0 53.1 %copy-start.102 = (f32[768]{0:T(1024)}, f32[768]{0:T(1024)S(1)}, u32[]{:S(2)}) copy-start(f32[768]{0:T(1024)S(1)} %get-tuple-element.56) | copy-start | bytes 9220
  911.1 12.2 slice-start.13
  911.1 12.2 slice-start.14
  924.8 15.7 copy-start.87
  977.1 40.3 %copy-start.75 = (f32[4,196]{1,0:T(4,128)}, f32[4,196]{1,0:T(4,128)S(1)}, u32[]{:S(2)}) copy-start(f32[4,196]{1,0:T(4,128)S(1)} %add_rsqrt_fusion.2) | copy-start | bytes 9412
  987.9 15.0 copy-start.14
  987.9 15.0 copy-start.64
  1023.2 18.8 slice-start
  1023.2 18.8 slice-start.1
  1203.8 16.1 copy-start.18
  1285.3 36.6 %copy-start.43 = (f32[393216]{0:T(1024)S(1)}, f32[393216]{0:T(1024)}, u32[]{:S(2)}) copy-start(f32[393216]{0:T(1024)} %reshape.488) | copy-start | bytes 4718596
  1338.3 714.3 %copy-start.44 = (f32[362752]{0:T(1024)S(1)}, f32[362752]{0:T(1024)}, u32[]{:S(2)}) copy-start(f32[362752]{0:T(1024)} %param.12) | copy-start | bytes 4353028
  1338.3 714.3 %copy-start.71 = (f32[362752]{0:T(1024)S(1)}, f32[362752]{0:T(1024)}, u32[]{:S(2)}) copy-start(f32[362752]{0:T(1024)} %param.14) | copy-start | bytes 4353028
  (140 other events, 585.1 us)
Sparse Core Ops, SparseCore 0:
  17.9 261.1 all-gather.2
  1338.4 669.4 all-reduce.3
where the time goes:
time: 2080 us; the launch traced here: 2070 us
  waiting for transfers between devices  867 us (42%)
  other arithmetic  558 us (27%)
  local copies, waits for them, and re-layouts  406 us (20%)
  matrix products  131 us (6%)
  blocking collectives  84.6 us (4%)
  between operations  22.9 us (1%)
    unnamed x3, waiting for transfers between devices  668 us
    all_gather x1, other arithmetic, body(): lax.all_gather(low_master, ('dp', 'pair'), axis=0, tiled=True)  490 us
    unnamed x343, local copies, waits for them, and re-layouts  257 us
    all_gather x1, waiting for transfers between devices, body(): lax.all_gather(low_master, ('dp', 'pair'), axis=0, tiled=True)  199 us
    psum x1, blocking collectives, body(): masked = lax.psum(local_masked, ('dp', 'pair'))  44.6 us
  transfers between devices with their start and end apart: 2, of which 2 were waited for; matrix products, arithmetic and copies ran while one was open for 1% of the time, Pallas kernels for 0%

commit v1 on v0

--- a/solution.py
+++ b/solution.py
@@ -1,19 +1,663 @@
+import functools
+
 import jax
 import jax.numpy as jnp
 from jax import lax
+from jax.experimental import pallas as pl
+from jax.experimental.pallas import tpu as pltpu
 from jax.sharding import PartitionSpec as P
 
-PIX = 768
-HEADS = 12
-F = 3072
-DHEADS = 16
-FD = 2048
-GRID = 14
-KEEP = 64
-D = 768
-DD = 512
-PATCHES = 196
+MESH = pl.DeviceIdType.MESH
+LANES = 128
+TILE = 16 * LANES
+
+
+def place():
+    dp, pair = lax.axis_index("dp"), lax.axis_index("pair")
+    return dp // 2, dp % 2, pair // 2, pair % 2
+
+
+def slot_of(z, x, y, c):
+    return (z * 2 + x) * 4 + y * 2 + c
+
+
+def partners(z, x, y, c):
+    return {
+        "x": {"dp": z * 2 + (1 - x)},
+        "y": {"pair": (1 - y) * 2 + c},
+        "c": {"pair": y * 2 + (1 - c)},
+        "up": {"dp": (z + 1) * 2 + x},
+        "down": {"dp": (z - 1) * 2 + x},
+    }
+
+
+def greet(n_z, z, to):
+    barrier = pltpu.get_barrier_semaphore()
+    for name in ("x", "y", "c"):
+        pl.semaphore_signal(barrier, inc=1, device_id=to[name], device_id_type=MESH)
+
+    @pl.when(z < n_z - 1)
+    def _():
+        pl.semaphore_signal(barrier, inc=1, device_id=to["up"], device_id_type=MESH)
+
+    @pl.when(z > 0)
+    def _():
+        pl.semaphore_signal(barrier, inc=1, device_id=to["down"], device_id_type=MESH)
+
+    pl.semaphore_wait(barrier, 3 + jnp.where(z < n_z - 1, 1, 0) + jnp.where(z > 0, 1, 0))
+
+
+def gather_kernel(n_z, slab_ref, out_ref, own_sem, send_sem, recv_sem):
+    half = slab_ref.shape[0] // 2
+    z, x, y, c = place()
+    to = partners(z, x, y, c)
+    me = slot_of(z, x, y, c)
+    local = pltpu.make_async_copy(slab_ref, out_ref.at[me], own_sem)
+    local.start()
+    greet(n_z, z, to)
+    local.wait()
+    pending = []
+
+    def copy(slot, part, name, index):
+        rows = pl.ds(part * half, half)
+        return pltpu.make_async_remote_copy(
+            out_ref.at[slot, rows],
+            out_ref.at[slot, rows],
+            send_sem.at[index],
+            recv_sem.at[slot, part],
+            device_id=to[name],
+            device_id_type=MESH,
+        )
+
+    def send(slot, part, name, where):
+        index = len(pending)
+        pending.append((slot, part, name, index, where))
+        if where is None:
+            copy(slot, part, name, index).start()
+        else:
+            pl.when(where)(lambda: copy(slot, part, name, index).start())
+
+    def arrived(slot, part, where):
+        if where is None:
+            copy(slot, part, "c", 0).wait_recv()
+        else:
+            pl.when(where)(lambda: copy(slot, part, "c", 0).wait_recv())
+
+    def both(one, two):
+        return two if one is None else jnp.logical_and(one, two)
+
+    levels = [[(z, None, None)]]
+    for t in range(1, n_z):
+        levels.append([(z - t, z >= t, "up"), (z + t, z + t < n_z, "down")])
+
+    def first(level):
+        for zz, where, onward in level:
+            slot = slot_of(zz, x, y, c)
+            for part in (0, 1):
+                if onward is None:
+                    send(slot, part, "up", z < n_z - 1)
+                    send(slot, part, "down", z > 0)
+                else:
+                    arrived(slot, part, where)
+                    more = z < n_z - 1 if onward == "up" else z > 0
+                    send(slot, part, onward, both(where, more))
+            for part in (0, 1):
+                send(slot, part, ("x", "y")[part], where)
+            for part in (0, 1):
+                send(slot, part, ("y", "x")[part], where)
+            for part in (0, 1):
+                send(slot, part, "c", where)
+
+    def second(level):
+        for zz, where, _ in level:
+            for part, slot in ((0, slot_of(zz, 1 - x, y, c)), (1, slot_of(zz, x, 1 - y, c))):
+                arrived(slot, part, where)
+                send(slot, part, ("y", "x")[part], where)
+                send(slot, part, "c", where)
+
+    def third(level):
+        for zz, where, _ in level:
+            for part, ox, oy in ((0, x, 1 - y), (1, 1 - x, y), (0, 1 - x, 1 - y), (1, 1 - x, 1 - y)):
+                slot = slot_of(zz, ox, oy, c)
+                arrived(slot, part, where)
+                send(slot, part, "c", where)
+
+    for t in range(n_z + 2):
+        if t < n_z:
+            first(levels[t])
+        if 1 <= t < n_z + 1:
+            second(levels[t - 1])
+        if t >= 2:
+            third(levels[t - 2])
+    for level in levels:
+        for zz, where, _ in level:
+            for ox in (0, 1):
+                for oy in (0, 1):
+                    for part in (0, 1):
+                        arrived(slot_of(zz, ox, oy, 1 - c), part, where)
+    for slot, part, name, index, where in pending:
+        if where is None:
+            copy(slot, part, name, index).wait_send()
+        else:
+            pl.when(where)(lambda s=slot, p=part, n=name, i=index: copy(s, p, n, i).wait_send())
+
+
+def gather(slab, n_dp, n_pair):
+    n_z = n_dp // 2
+    n = n_dp * n_pair
+    sends = (2 * n_z - 1) * 16 + 8
+    return pl.pallas_call(
+        functools.partial(gather_kernel, n_z),
+        name="gather",
+        out_shape=jax.ShapeDtypeStruct((n,) + slab.shape, slab.dtype),
+        in_specs=[pl.BlockSpec(memory_space=pl.ANY)],
+        out_specs=pl.BlockSpec(memory_space=pl.ANY),
+        scratch_shapes=[
+            pltpu.SemaphoreType.DMA,
+            pltpu.SemaphoreType.DMA((sends,)),
+            pltpu.SemaphoreType.DMA((n, 2)),
+        ],
+        compiler_params=pltpu.CompilerParams(collective_id=0, has_side_effects=True),
+    )(slab)
+
+
+PIX, HEADS, F, DHEADS, FD, GRID, KEEP, D, DD, PATCHES = 768, 12, 3072, 16, 2048, 14, 64, 768, 512, 196
+SHAPES = [(PIX, D), (D, 3 * D), (D, D), (D, F), (F, D), (6, D), (D, DD), (DD, 3 * DD), (DD, DD), (DD, FD), (FD, DD), (DD, PIX), (7, DD)]
+SMALL = (5, 12)
 ENC_PARAMS = 7672320
+MB = 1 << 20
+CELL = 8 * LANES
+BLOCK = 96
+
+
+def make_entries():
+    entries, row, tile = [], 0, 0
+    for number, (rows, width) in enumerate(SHAPES):
+        lines = rows * width // LANES
+        cols = 1 if number in SMALL else width // LANES
+        groups = -(-lines // (8 * cols))
+        entries.append((row, lines, cols, tile, groups))
+        row += lines
+        tile += groups * cols
+    return entries, row, tile
+
+
+ENTRIES, ROWS, TILES = make_entries()
+MARGIN = 8 * max(cols for _, _, cols, _, _ in ENTRIES)
+
+
+def first_tile(share, k):
+    lo = share * k
+    total = 0
+    for row, lines, cols, tile, _ in ENTRIES:
+        inside = jnp.logical_and(lo >= row * LANES, lo < (row + lines) * LANES)
+        total = total + jnp.where(inside, tile + (lo - row * LANES) // (CELL * cols) * cols, 0)
+    return total
+
+
+def ranges(share, n):
+    found = []
+    for k in range(n):
+        lo, hi = share * k, share * (k + 1)
+        spans = []
+        for row, lines, cols, tile, _ in ENTRIES:
+            low, high = max(lo, row * LANES), min(hi, (row + lines) * LANES)
+            if low < high:
+                size = CELL * cols
+                spans.append((tile + (low - row * LANES) // size * cols, tile + -(-(high - row * LANES) // size) * cols))
+        found.append((spans[0][0], spans[-1][1]))
+    return found
+
+
+def slab_tiles(share, n):
+    longest = max(b - a for a, b in ranges(share, n))
+    return -(-longest // 24) * 24
+
+
+def line_span(share, k):
+    return share * k // LANES, (share * (k + 1) + LANES - 1) // LANES
+
+
+def tiled(share, k, body):
+    lo, hi = line_span(share, k)
+    begin = first_tile(share, k)
+    for number in SMALL + tuple(i for i in range(len(ENTRIES)) if i not in SMALL):
+        row, lines, cols, tile, _ = ENTRIES[number]
+        low = jnp.maximum(lo, row) - row
+        high = jnp.minimum(hi, row + lines) - row
+        size = 8 * cols
+
+        def group(g, _, row=row, cols=cols, tile=tile, size=size):
+            body(row + g * size - lo + MARGIN, tile + g * cols - begin, cols)
+            return 0
+
+        lax.fori_loop(jnp.where(low < high, low // size, 0), jnp.where(low < high, (high + size - 1) // size, 0), group, 0)
+
+
+def tile_kernel(share, n_pair, lines_ref, extra_ref, out_ref, wide):
+    k = lax.axis_index("dp") * n_pair + lax.axis_index("pair")
+    rows = lines_ref.shape[0]
+    wide[0:MARGIN, :] = jnp.zeros((MARGIN, LANES), jnp.float32)
+    wide[MARGIN + rows :, :] = jnp.zeros((wide.shape[0] - MARGIN - rows, LANES), jnp.float32)
+    wide[MARGIN : MARGIN + rows, :] = lines_ref[...]
+
+    def body(line, tile, cols):
+        for col in range(cols):
+            out_ref[tile + col] = wide[pl.ds(line + col, 8, stride=cols), :].astype(out_ref.dtype)
+
+    tiled(share, k, body)
+    out_ref[out_ref.shape[0] - 2] = extra_ref[...].astype(out_ref.dtype)
+
+
+def wide_rows(rows):
+    return -(-(rows + 2 * MARGIN) // 8) * 8
+
+
+def to_tiles(lines, extra, share, n, n_pair):
+    rows = lines.shape[0]
+    count = slab_tiles(share, n) + 2
+    spec = pl.BlockSpec(memory_space=pltpu.VMEM)
+    return pl.pallas_call(
+        functools.partial(tile_kernel, share, n_pair),
+        name="to_tiles",
+        out_shape=jax.ShapeDtypeStruct((count, 8, LANES), jnp.bfloat16),
+        in_specs=[spec, spec],
+        out_specs=spec,
+        scratch_shapes=[pltpu.VMEM((wide_rows(rows), LANES), jnp.float32)],
+    )(lines, extra)
+
+
+def line_kernel(share, n_pair, slab_ref, out_ref, wide):
+    k = lax.axis_index("dp") * n_pair + lax.axis_index("pair")
+
+    def body(line, tile, cols):
+        for col in range(cols):
+            wide[pl.ds(line + col, 8, stride=cols), :] = slab_ref[pl.ds(pl.multiple_of((tile + col) * 8, 8), 8), :]
+
+    tiled(share, k, body)
+    out_ref[...] = wide[MARGIN : MARGIN + out_ref.shape[0], :]
+
+
+def to_lines(slab, rows, share, n_pair):
+    spec = pl.BlockSpec(memory_space=pltpu.VMEM)
+    return pl.pallas_call(
+        functools.partial(line_kernel, share, n_pair),
+        name="to_lines",
+        out_shape=jax.ShapeDtypeStruct((rows, LANES), jnp.float32),
+        in_specs=[spec],
+        out_specs=spec,
+        scratch_shapes=[pltpu.VMEM((wide_rows(rows), LANES), jnp.float32)],
+    )(slab)
+
+
+def pieces(share, n):
+    spans = ranges(share, n)
+    shared = [spans[k][1] > spans[k + 1][0] for k in range(n - 1)]
+    plain, seams = [], []
+    for number, (_, _, cols, tile, groups) in enumerate(ENTRIES):
+        end = tile + groups * cols
+        for k, (a, b) in enumerate(spans):
+            low, high = max(a, tile), min(b, end)
+            if low >= high:
+                continue
+            inner_low, inner_high = low, high
+            if k > 0 and spans[k - 1][1] > low:
+                inner_low = spans[k - 1][1]
+            if k < n - 1 and spans[k + 1][0] < high:
+                inner_high = spans[k + 1][0]
+                seams.append((number, k, inner_high, high))
+            if inner_low < inner_high:
+                plain.append((number, k, inner_low, inner_high))
+    return spans, plain, seams
+
+
+def assemble_kernel(share, n, slots_ref, *refs):
+    outs = refs[: len(ENTRIES)]
+    whole, right, plain_sem, left_sem, right_sem, out_sem = refs[len(ENTRIES) :]
+    spans, plain, seams = pieces(share, n)
+    waits = [[] for _ in ENTRIES]
+    for i, (number, k, low, high) in enumerate(plain):
+        copy = pltpu.make_async_copy(slots_ref.at[k, pl.ds(low - spans[k][0], high - low)], whole.at[pl.ds(low, high - low)], plain_sem.at[i])
+        copy.start()
+        waits[number].append(copy)
+    for i, (number, k, low, high) in enumerate(seams):
+        one = pltpu.make_async_copy(slots_ref.at[k, pl.ds(low - spans[k][0], high - low)], whole.at[pl.ds(low, high - low)], left_sem.at[i])
+        two = pltpu.make_async_copy(
+            slots_ref.at[k + 1, pl.ds(low - spans[k + 1][0], high - low)], right.at[i, pl.ds(0, high - low)], right_sem.at[i]
+        )
+        one.start()
+        two.start()
+        waits[number] += [one, two]
+    ended = []
+    for number, (_, _, cols, tile, groups) in enumerate(ENTRIES):
+        for copy in waits[number]:
+            copy.wait()
+        for i, (owner, k, low, high) in enumerate(seams):
+            if owner == number:
+                total = whole[low:high].astype(jnp.float32) + right[i, 0 : high - low].astype(jnp.float32)
+                whole[low:high] = total.astype(jnp.bfloat16)
+        copy = pltpu.make_async_copy(whole.at[pl.ds(tile, groups * cols)], outs[number], out_sem.at[number])
+        copy.start()
+        ended.append(copy)
+    for copy in ended:
+        copy.wait()
+
+
+def assemble(slots, share):
+    n = slots.shape[0]
+    _, plain, seams = pieces(share, n)
+    anyspec = pl.BlockSpec(memory_space=pl.ANY)
+    dma = pltpu.SemaphoreType.DMA
+    return pl.pallas_call(
+        functools.partial(assemble_kernel, share, n),
+        name="assemble",
+        out_shape=[jax.ShapeDtypeStruct((groups * cols, 8, LANES), jnp.bfloat16) for _, _, cols, _, groups in ENTRIES],
+        in_specs=[anyspec],
+        out_specs=[anyspec] * len(ENTRIES),
+        scratch_shapes=[
+            pltpu.VMEM((TILES, 8, LANES), jnp.bfloat16),
+            pltpu.VMEM((len(seams), MARGIN // 8, 8, LANES), jnp.bfloat16),
+            dma((len(plain),)),
+            dma((len(seams),)),
+            dma((len(seams),)),
+            dma((len(ENTRIES),)),
+        ],
+        compiler_params=pltpu.CompilerParams(vmem_limit_bytes=40 * MB),
+    )(slots)
+
+
+def matrix(tiles_, number):
+    rows, width = SHAPES[number]
+    cols = width // LANES
+    return tiles_.reshape(rows // 8, cols, 8, LANES).transpose(0, 2, 1, 3).reshape(rows, width)
+
+
+def matrix_tiles(value):
+    rows, width = value.shape
+    cols = width // LANES
+    return value.reshape(rows // 8, 8, cols, LANES).transpose(0, 2, 1, 3).reshape(rows * cols, LANES)
+
+
+def reduce_kernel(n_z, share, grad_ref, out_ref, sib_ref, gbuf, rbuf, keep, q1s, q1r, q2s, q2r, zs, zr, t1s, t1r, t2s, t2r, tzs, tzr, sib_sem, load_sem, s1_sem, s2_sem, z_sem):
+    z, x, y, c = place()
+    to = partners(z, x, y, c)
+    rows = out_ref.shape[0]
+    half = rows // 2
+    count = half // BLOCK
+
+    def start_of(k):
+        return pl.multiple_of(first_tile(share, k) * 8, 8)
+
+    def order(j):
+        low = z < n_z // 2
+        far = jnp.where(low, n_z - 1 - j, j)
+        moved = jnp.where(low, jnp.where(far > z, far, far - 1), jnp.where(far < z, far, far + 1))
+        return jnp.where(j == n_z - 1, z, moved)
+
+    def sibling(j, xx, yy, core):
+        k = slot_of(order(j), xx, yy, core)
+        return pltpu.make_async_remote_copy(
+            grad_ref.at[pl.ds(start_of(k), rows)],
+            sib_ref.at[j, xx * 2 + yy],
+            sib_sem.at[0, j, xx * 2 + yy],
+            sib_sem.at[1, j, xx * 2 + yy],
+            device_id=to["c"],
+            device_id_type=MESH,
+        )
+
+    def loads(j, s, q):
+        k = slot_of(order(j), q // 2, q % 2, c)
+        return (
+            pltpu.make_async_copy(grad_ref.at[pl.ds(start_of(k), rows)], gbuf.at[s, q], load_sem.at[0, s, q]),
+            pltpu.make_async_copy(sib_ref.at[j, q], rbuf.at[s, q], load_sem.at[1, s, q]),
+        )
+
+    def load(j):
+        s = lax.rem(j, 2)
+        for q in range(4):
+            sibling(j, q // 2, q % 2, 1 - c).wait_recv()
+            for one in loads(j, s, q):
+                one.start()
+
+    def pack(value, q_ref, t_ref, b):
+        top = jnp.max(jnp.abs(value), axis=0, keepdims=True)
+        inverse = jnp.where(top > 1e-30, 32767.0 / jnp.maximum(top, 1e-30), 0.0)
+        q_ref[pl.ds(pl.multiple_of(b * BLOCK, BLOCK), BLOCK), :] = jnp.round(value * inverse).astype(jnp.int32).astype(jnp.int16)
+        t_ref[pl.ds(b, 1), :] = top * (1.0 / 32767.0)
+
+    def unpack(q_ref, t_ref, b):
+        return q_ref[pl.ds(pl.multiple_of(b * BLOCK, BLOCK), BLOCK), :].astype(jnp.int32).astype(jnp.float32) * t_ref[pl.ds(b, 1), :]
+
+    def each(body):
+        def one(b, _):
+            body(b)
+            return 0
+
+        lax.fori_loop(0, count, one, 0)
+
+    def own(s, q, part, b):
+        at = pl.ds(pl.multiple_of(part * half + b * BLOCK, BLOCK), BLOCK)
+        return gbuf[s, q, at, :] + rbuf[s, q, at, :]
+
+    def message(qs, ts, qr, tr, sem, name):
+        return (
+            pltpu.make_async_remote_copy(qs, qr, sem.at[0, 0], sem.at[0, 1], device_id=to[name], device_id_type=MESH),
+            pltpu.make_async_remote_copy(ts, tr, sem.at[1, 0], sem.at[1, 1], device_id=to[name], device_id_type=MESH),
+        )
+
+    def first_message(j, part, other):
+        i = part * 2 + other
+        return message(q1s.at[j, i], t1s.at[j, i], q1r.at[j, i], t1r.at[j, i], s1_sem.at[j, i], ("x", "y")[part])
+
+    def second_message(j, part):
+        return message(q2s.at[j, part], t2s.at[j, part], q2r.at[j, part], t2r.at[j, part], s2_sem.at[j, part], ("y", "x")[part])
+
+    def z_message(zz, part, name):
+        d = 0 if name == "up" else 1
+        return message(zs.at[zz, part], tzs.at[zz, part], zr.at[d, zz, part], tzr.at[d, zz, part], z_sem.at[d, zz, part], name)
+
+    def quarter(part, other, mine):
+        if part == 0:
+            return (x if mine else 1 - x) * 2 + other
+        return other * 2 + (y if mine else 1 - y)
+
+    def stage_one(j):
+        s = lax.rem(j, 2)
+        for q in range(4):
+            for one in loads(j, s, q):
+                one.wait()
+        for part in (0, 1):
+            for other in (0, 1):
+                q = quarter(part, other, False)
+                i = part * 2 + other
+                each(lambda b: pack(own(s, q, part, b), q1s.at[j, i], t1s.at[j, i], b))
+                for one in first_message(j, part, other):
+                    one.start()
+
+    def stage_two(j):
+        s = lax.rem(j, 2)
+        for part in (0, 1):
+            for other in (0, 1):
+                for one in first_message(j, part, other):
+                    one.wait_recv()
+            here = (y, x)[part]
+            away = quarter(part, 1 - here, True)
+            i = part * 2 + 1 - here
+            each(lambda b: pack(own(s, away, part, b) + unpack(q1r.at[j, i], t1r.at[j, i], b), q2s.at[j, part], t2s.at[j, part], b))
+            for one in second_message(j, part):
+                one.start()
+        for part in (0, 1):
+            here = (y, x)[part]
+            mine = x * 2 + y
+            k = part * 2 + here
+
+            def store(b, part=part, k=k):
+                at = pl.ds(pl.multiple_of(part * half + b * BLOCK, BLOCK), BLOCK)
+                keep[j, at, :] = own(s, mine, part, b) + unpack(q1r.at[j, k], t1r.at[j, k], b)
+
+            each(store)
+
+    def add_to_keep(j, part, q_ref, t_ref):
+        def body(b):
+            at = pl.ds(pl.multiple_of(part * half + b * BLOCK, BLOCK), BLOCK)
+            keep[j, at, :] += unpack(q_ref, t_ref, b)
+
+        each(body)
+
+    def stage_three(j):
+        for part in (0, 1):
+            for one in second_message(j, part):
+                one.wait_recv()
+            add_to_keep(j, part, q2r.at[j, part], t2r.at[j, part])
+
+    def pass_on(j, zz, part, name):
+        def body(b):
+            at = pl.ds(pl.multiple_of(part * half + b * BLOCK, BLOCK), BLOCK)
+            pack(keep[j, at, :], zs.at[zz, part], tzs.at[zz, part], b)
+
+        each(body)
+        for one in z_message(zz, part, name):
+            one.start()
+
+    def stage_four(j):
+        zz = order(j)
+        for part in (0, 1):
+            for d, name, has, onward in ((0, "up", z > 0, zz > z), (1, "down", z < n_z - 1, zz < z)):
+                back = zz >= z if d == 0 else zz <= z
+
+                @pl.when(jnp.logical_and(has, back))
+                def _():
+                    for one in z_message(zz, part, name):
+                        one.wait_recv()
+                    add_to_keep(j, part, zr.at[d, zz, part], tzr.at[d, zz, part])
+
+                @pl.when(onward)
+                def _():
+                    pass_on(j, zz, part, name)
+
+    greet(n_z, z, to)
+
+    def begin(j, _):
+        for q in range(4):
+            sibling(j, q // 2, q % 2, 1 - c).start()
+        return 0
+
+    lax.fori_loop(0, n_z, begin, 0)
+    load(0)
+
+    def turn(t, _):
+        pl.when(t < n_z)(lambda: stage_one(t))
+        pl.when(jnp.logical_and(t >= 1, t <= n_z))(lambda: stage_two(t - 1))
+        pl.when(t + 1 < n_z)(lambda: load(t + 1))
+        pl.when(jnp.logical_and(t >= 2, t <= n_z + 1))(lambda: stage_three(t - 2))
+        pl.when(t >= 3)(lambda: stage_four(t - 3))
+        return 0
+
+    lax.fori_loop(0, n_z + 3, turn, 0)
+    out_ref[...] = keep[n_z - 1]
+
+    def finish(j, _):
+        zz = order(j)
+        for q in range(4):
+            sibling(j, q // 2, q % 2, 1 - c).wait_send()
+        for part in (0, 1):
+            for other in (0, 1):
+                for one in first_message(j, part, other):
+                    one.wait_send()
+            for one in second_message(j, part):
+                one.wait_send()
+
+            @pl.when(zz > z)
+            def _():
+                for one in z_message(zz, part, "up"):
+                    one.wait_send()
+
+            @pl.when(zz < z)
+            def _():
+                for one in z_message(zz, part, "down"):
+                    one.wait_send()
+
+        return 0
+
+    lax.fori_loop(0, n_z, finish, 0)
+
+
+def reduce(flat, share, n_dp, n_pair):
+    n_z, n = n_dp // 2, n_dp * n_pair
+    rows = slab_tiles(share, n) * 8
+    half = rows // 2
+    marks = (half // BLOCK + 7) // 8 * 8
+    anyspec = pl.BlockSpec(memory_space=pl.ANY)
+
+    def q(*lead):
+        return pltpu.VMEM(lead + (half, LANES), jnp.int16)
+
+    def t(*lead):
+        return pltpu.VMEM(lead + (marks, LANES), jnp.float32)
+
+    dma = pltpu.SemaphoreType.DMA
+    return pl.pallas_call(
+        functools.partial(reduce_kernel, n_z, share),
+        name="reduce_scatter",
+        out_shape=[jax.ShapeDtypeStruct((rows, LANES), jnp.float32), jax.ShapeDtypeStruct((n_z, 4, rows, LANES), jnp.float32)],
+        in_specs=[anyspec],
+        out_specs=[pl.BlockSpec(memory_space=pltpu.VMEM), anyspec],
+        scratch_shapes=[
+            pltpu.VMEM((2, 4, rows, LANES), jnp.float32),
+            pltpu.VMEM((2, 4, rows, LANES), jnp.float32),
+            pltpu.VMEM((n_z, rows, LANES), jnp.float32),
+            q(n_z, 4), q(n_z, 4), q(n_z, 2), q(n_z, 2), q(n_z, 2), q(2, n_z, 2),
+            t(n_z, 4), t(n_z, 4), t(n_z, 2), t(n_z, 2), t(n_z, 2), t(2, n_z, 2),
+            dma((2, n_z, 4)), dma((2, 2, 4)), dma((n_z, 4, 2, 2)), dma((n_z, 2, 2, 2)), dma((2, n_z, 2, 2, 2)),
+        ],
+        compiler_params=pltpu.CompilerParams(collective_id=1, has_side_effects=True, vmem_limit_bytes=60 * MB),
+    )(flat)[0]
+
+
+def share_kernel(n_dp, n_pair, in_ref, out_ref, send_sem, recv_sem):
+    n = n_dp * n_pair
+    me = lax.axis_index("dp") * n_pair + lax.axis_index("pair")
+    barrier = pltpu.get_barrier_semaphore()
+
+    def other(d):
+        k = lax.rem(me + d, n)
+        return {"dp": k // n_pair, "pair": lax.rem(k, n_pair)}
+
+    def hello(d, _):
+        pl.semaphore_signal(barrier, inc=1, device_id=other(d), device_id_type=MESH)
+        return 0
+
+    lax.fori_loop(1, n, hello, 0)
+    pl.semaphore_wait(barrier, n - 1)
+    out_ref[me] = in_ref[...]
+
+    def copy(d):
+        return pltpu.make_async_remote_copy(in_ref, out_ref.at[me], send_sem.at[d], recv_sem.at[d], device_id=other(d), device_id_type=MESH)
+
+    def go(d, _):
+        copy(d).start()
+        return 0
+
+    def stop(d, _):
+        copy(d).wait()
+        return 0
+
+    lax.fori_loop(1, n, go, 0)
+    lax.fori_loop(1, n, stop, 0)
+
+
+def share_all(value, n_dp, n_pair, ident):
+    n = n_dp * n_pair
+    spec = pl.BlockSpec(memory_space=pltpu.VMEM)
+    return pl.pallas_call(
+        functools.partial(share_kernel, n_dp, n_pair),
+        name="share_all",
+        out_shape=jax.ShapeDtypeStruct((n,) + value.shape, value.dtype),
+        in_specs=[spec],
+        out_specs=spec,
+        scratch_shapes=[pltpu.SemaphoreType.DMA((n,)), pltpu.SemaphoreType.DMA((n,))],
+        compiler_params=pltpu.CompilerParams(collective_id=ident, has_side_effects=True),
+    )(value)
 
 
 NORM_EPS = 1e-06
@@ -22,35 +666,6 @@
 BETA_TWO = 0.95
 DECAY = 0.05
 NEG_FILL = -1000000000.0
-
-
-def shapes():
-    return [
-        (PIX, D),
-        (D, 3 * D),
-        (D, D),
-        (D, F),
-        (F, D),
-        (6, D),
-        (D, DD),
-        (DD, 3 * DD),
-        (DD, DD),
-        (DD, FD),
-        (FD, DD),
-        (DD, PIX),
-        (6, DD),
-        (1, DD),
-    ]
-
-
-def unpack(flat):
-    parts = []
-    offset = 0
-    for shape in shapes():
-        amount = shape[0] * shape[1]
-        parts.append(flat[offset : offset + amount].reshape(shape))
-        offset += amount
-    return parts
 
 
 def mult(left, right):
@@ -194,13 +809,31 @@
     return (grad_in, (grad_triple_w, grad_proj, grad_up, grad_down), gain_grads)
 
 
+def own_lines(flat, share, index):
+    if share % LANES == 0:
+        return flat.reshape(-1, LANES)
+    rows = (share + LANES - 1) // LANES + 1
+    return lax.dynamic_update_slice(jnp.zeros((rows * LANES,), flat.dtype), flat, (share * index % LANES,)).reshape(rows, LANES)
+
+
+def own_flat(lines, share, index):
+    if share % LANES == 0:
+        return lines.reshape(-1)
+    return lax.dynamic_slice(lines.reshape(-1), (share * index % LANES,), (share,))
+
+
 def body(
-    patches, patch_order, counts, master, moment1, moment2, block_rates, clip_limit, step_count
+    n_dp, n_pair, patches, patch_order, counts, master, moment1, moment2, block_rates, clip_limit, step_count
 ):
-    local_masked = jnp.sum(PATCHES - counts).astype(jnp.float32)
-    masked = lax.psum(local_masked, ("dp", "pair"))
-    low_master = master.astype(jnp.bfloat16)
-    parts = unpack(lax.all_gather(low_master, ("dp", "pair"), axis=0, tiled=True))
+    n = n_dp * n_pair
+    share = master.shape[0]
+    index = lax.axis_index("dp") * n_pair + lax.axis_index("pair")
+    extra = jnp.zeros((8, LANES), jnp.float32).at[0, : counts.shape[0]].set((PATCHES - counts).astype(jnp.float32))
+    slab = to_tiles(own_lines(master, share, index), extra, share, n, n_pair)
+    slots = gather(slab, n_dp, n_pair)
+    masked = jnp.sum(slots[:, slab.shape[0] - 2, 0, :].astype(jnp.float32))
+    held = assemble(slots, share)
+    parts = [held[i].reshape(-1)[: SHAPES[i][0] * SHAPES[i][1]].reshape(SHAPES[i]) if i in SMALL else matrix(held[i], i) for i in range(len(SHAPES))]
     enc_gains = parts[5].astype(jnp.float32)
     dec_gains = parts[12].astype(jnp.float32)
     slots = patch_order[:, :KEEP]
@@ -215,7 +848,7 @@
     rank = jnp.argsort(patch_order, axis=1)
     shown = rank < counts[:, None]
     picked = jnp.take_along_axis(entering, jnp.minimum(rank, KEEP - 1)[:, :, None], axis=1)
-    token = parts[13][0].astype(jnp.float32)
+    token = parts[12][6].astype(jnp.float32)
     y_start = jnp.where(shown[:, :, None], picked, token) + positions(DD)[None]
     dec_bias = jnp.zeros(shown.shape, jnp.float32)
     y_end, dec_saved = block_forward(y_start, tuple(parts[7:11]), dec_gains, DHEADS, dec_bias)
@@ -229,7 +862,7 @@
     hidden_mask = jnp.where(shown, 0.0, 1.0).astype(jnp.float32)
     loss_local = jnp.sum(jnp.mean(diff * diff, axis=-1) * hidden_mask)
     grad_pred = (diff * (hidden_mask[:, :, None] * (2.0 / PIX)) / masked).astype(jnp.bfloat16)
-    again = unpack(lax.all_gather(low_master, ("dp", "pair"), axis=0, tiled=True))
+    again = parts
     enc_back_gains = again[5].astype(jnp.float32)
     dec_back_gains = again[12].astype(jnp.float32)
     grad_head = outer(final, grad_pred)
@@ -252,7 +885,7 @@
     grad_embed = outer(seen, grad_x.astype(jnp.bfloat16))
     enc_norm_grads = jnp.concatenate([enc_gain_grads, jnp.stack([gain_enc, shift_enc])])
     dec_norm_grads = jnp.concatenate([dec_gain_grads, jnp.stack([gain_final, shift_final])])
-    pieces = [
+    grads = [
         grad_embed,
         enc_grads[0],
         enc_grads[1],
@@ -265,22 +898,30 @@
         dec_grads[2],
         dec_grads[3],
         grad_head,
-        dec_norm_grads,
-        grad_token[None],
+        jnp.concatenate([dec_norm_grads, grad_token[None]]),
     ]
-    shard = master.shape[0]
-    filled = sum((shape[0] * shape[1] for shape in shapes()))
-    padding = jnp.zeros((shard * lax.axis_size(("dp", "pair")) - filled,), jnp.float32)
-    flat = jnp.concatenate([piece.reshape(-1) for piece in pieces] + [padding])
-    grad_share = lax.psum_scatter(flat, ("dp", "pair"), scatter_dimension=0, tiled=True)
-    squares, loss_sum = lax.psum((jnp.sum(grad_share * grad_share), loss_local), ("dp", "pair"))
+    total = max(a for a, _ in ranges(share, n)) + slab_tiles(share, n)
+    pieces_ = []
+    for i, grad in enumerate(grads):
+        if i in SMALL:
+            lines = grad.reshape(-1, LANES)
+            pieces_.append(jnp.pad(lines, ((0, ENTRIES[i][4] * 8 - lines.shape[0]), (0, 0))))
+        else:
+            pieces_.append(matrix_tiles(grad))
+    pieces_.append(jnp.zeros(((total - TILES) * 8, LANES), jnp.float32))
+    slab_sum = reduce(jnp.concatenate(pieces_), share, n_dp, n_pair)
+    rows = share // LANES if share % LANES == 0 else (share + LANES - 1) // LANES + 1
+    grad_share = own_flat(to_lines(slab_sum, rows, share, n_pair), share, index)
+    scalars = jnp.stack([jnp.sum(grad_share * grad_share), loss_local])
+    shared = share_all(jnp.zeros((8, LANES), jnp.float32).at[0, :2].set(scalars), n_dp, n_pair, 2)
+    squares, loss_sum = jnp.sum(shared[:, 0, 0]), jnp.sum(shared[:, 0, 1])
     grad_norm = jnp.sqrt(squares)
     loss = loss_sum / masked
     clipped = grad_share * (clip_limit[0] / (grad_norm + NORM_EPS))
     first = BETA_ONE * moment1 + (1.0 - BETA_ONE) * clipped
     second = BETA_TWO * moment2 + (1.0 - BETA_TWO) * clipped * clipped
     steps_done = step_count[0].astype(jnp.float32)
-    position = lax.axis_index(("dp", "pair")) * shard + jnp.arange(shard)
+    position = index * share + jnp.arange(share)
     rate = jnp.where(position < ENC_PARAMS, block_rates[0], block_rates[1])
     update = (
         first
@@ -304,4 +945,4 @@
         P(),
     )
     out_specs = (P(), P(), P(("dp", "pair")), P(("dp", "pair")), P(("dp", "pair")))
-    return jax.shard_map(body, mesh=mesh, in_specs=in_specs, out_specs=out_specs, check_vma=False)
+    return jax.shard_map(functools.partial(body, mesh.shape["dp"], mesh.shape["pair"]), mesh=mesh, in_specs=in_specs, out_specs=out_specs, check_vma=False)

time: 2080 us -> 649 us (0.31)
  waiting for transfers between devices: 867 us -> 0 us
  other arithmetic: 558 us -> 75.9 us
  Pallas kernels: 0 us -> 321 us
  local copies, waits for them, and re-layouts: 406 us -> 112 us
  blocking collectives: 84.6 us -> 0 us
    unnamed x3 -> x0, waiting for transfers between devices: 668 us -> none
    all_gather x1 -> x0, other arithmetic: 490 us -> none  [body(): lax.all_gather(low_master, ('dp', 'pair'), axis=0, tiled=True)]
    pallas_call x0 -> x6, Pallas kernels: none -> 321 us  [the longest x1 154 us: reduce(): pl.pallas_call(functools.partial(reduce_kernel, n_z, share), name='reduce...]
    unnamed x343 -> x288, local copies, waits for them, and re-layouts: 257 us -> 52.7 us
    all_gather x1 -> x0, waiting for transfers between devices: 199 us -> none  [body(): lax.all_gather(low_master, ('dp', 'pair'), axis=0, tiled=True)]
    psum x2 -> x0, blocking collectives: 84.6 us -> none  [the longest x1 44.6 us: body(): masked = lax.psum(local_masked, ('dp', 'pair'))]
    reshape x16 -> x2, local copies, waits for them, and re-layouts: 66.8 us -> 0.61 us  [body(): lines = grad.reshape(-1, LANES)]
    slice x11 -> x1, local copies, waits for them, and re-layouts: 29.5 us -> 0.02 us  [body(): held[i].reshape(-1)[:SHAPES[i][0] * SHAPES[i][1]].reshape(SHAPES[i])]
  transfers between devices with their start and end apart: 2 -> 0, of which waited for: 2 -> 0; matrix products, arithmetic and copies ran while one was open for 1% -> 0% of each run, Pallas kernels for 0% -> 0%
where the time goes in v1:
time: 649 us; the launch traced here: 644 us
  Pallas kernels  321 us (49%)
  matrix products  126 us (19%)
  local copies, waits for them, and re-layouts  112 us (17%)
  other arithmetic  75.9 us (12%)
  between operations  8.58 us (1%)
    pallas_call x1, Pallas kernels, reduce(): pl.pallas_call(functools.partial(reduce_kernel, n_z, share), name='reduce...  154 us
    pallas_call x1, Pallas kernels, gather(): pl.pallas_call(functools.partial(gather_kernel, n_z), name='gather', out_...  137 us
    unnamed x288, local copies, waits for them, and re-layouts  52.7 us
    dot_general x11, matrix products, outer(): jnp.einsum('bsi,bsj->ij', left, grad, preferred_element_type=jnp.float32)  27.3 us
    dot_general x11, matrix products, mult(): jnp.einsum('bsi,ij->bsj', left, right, preferred_element_type=jnp.float32)  27.3 us
    dot_general x10, matrix products, mult_back(): jnp.einsum('bsj,ij->bsi', grad, right, preferred_element_type=jnp.float32)  24.7 us
    convert_element_type x2, other arithmetic, block_forward(): activated = jax.nn.gelu(hidden, approximate=False).astype(jnp.bfloat16)  22.7 us
    gather x3, local copies, waits for them, and re-layouts, body(): jnp.take_along_axis(entering, jnp.minimum(rank, KEEP - 1)[:, :, None], ax...  17.2 us

profile of v1, /device:TPU:0, one launch (start us, length us, event | category | flops | bytes accessed | tf_op | source)
XLA Modules:
  0.0 643.9 jit_solution(16991592806632540831)
XLA Ops:
  8.7 136.7 %gather.29.slots_ref = bf16[32,386,8,128]{3,2,1,0:T(8,128)(2,1)} custom-call(bf16[386,8,128]{2,1,0:T(8,128)(2,1)} %to_tiles.1.slab_ref), custom_call_target="tpu_custom_call" | custom-call | tf_op jit(solution)/shard_map/gather/pallas_call | solution.py:149
  145.4 13.3 %assemble.1 = (bf16[576,8,128]{2,1,0:T(8,128)(2,1)S(1)}, bf16[1728,8,128]{2,1,0:T(8,128)(2,1)S(1)}, bf16[576,8,128]{2,1,0:T(8,128)(2,1)S(1)}, bf16[2304,8,128]{2...) custom-call(bf16[32,386,8,128]{3,2,1,0:T(8,128)(2,1)} %gather.29.slo, ...), custom_call_target="tpu_custom_call" | custom-call | tf_op jit(solution)/shard_map/assemble/pallas_call | solution.py:351
  188.8 5.1 fusion.70
  193.9 7.5 %fusion.19 = bf16[4,64,3072]{2,1,0:T(8,128)(2,1)S(1)} fusion(f32[4,64,3072]{2,1,0:T(8,128)S(1)} %get-tuple-element.142, u8[64,3072]{1,0:T(8,128)(4,1)S(1)} %get-tuple-element.68, u8[64,3072]{1,0:T(8,128)(4,1)S(1)} %get-tuple-element.67), kind=kLoop, calls=%fused_computation.49 | loop fusion | flops 55050240 | bytes 5111808 | tf_op jit(solution)/shard_map/convert_element_type | solution.py:732
  207.7 14.3 %gather_fusion.2 = f32[784,512]{1,0:T(8,128)} fusion(f32[4,64,512]{2,1,0:T(8,128)S(1)} %fusion.97, s32[784]{0:T(1024)S(1)} %reshape.620), kind=kCustom, calls=%fused_computation.2 | custom fusion | bytes 3217536 | tf_op jit(solution)/shard_map/jit(take_along_axis)/gather | solution.py:850
  227.8 5.1 convolution_convert_fusion.1
  232.9 4.7 copy.53
  237.6 8.2 %multiply_reduce_fusion.1 = (f32[4,16,196]{2,1,0:T(8,128)S(1)}, f32[4,16,196,196]{2,3,1,0:T(8,128)}) fusion(bf16[4,196,3,16,32]{1,4,3,2,0:T(8,128)(2,1)} %bitcast.433), kind=kOutput, calls=%fused_computation.8 | convolution fusion | flops 162256640 | bytes 11981824 | tf_op jit(solution)/shard_map/bqhd,bkhd->bhqk/dot_general | solution.py:710
  245.8 7.5 %exponential_reduce_fusion = f32[4,16,196]{2,1,0:T(8,128)S(1)} fusion(f32[4,16,196,196]{2,3,1,0:T(8,128)} %get-tuple-element.146, f32[4,16,196]{2,1,0:T(8,128)S(1)} %get-tuple-element.145), kind=kLoop, calls=%fused_computation.7 | loop fusion | flops 7363328 | bytes 9934848 | tf_op jit(solution)/shard_map/reduce_sum | solution.py:724
  253.4 7.7 %convolution_convert_fusion.2 = bf16[4,16,32,196]{3,2,1,0:T(8,128)(2,1)S(1)} fusion(bf16[4,196,3,16,32]{1,4,3,2,0:T(8,128)(2,1)} %bitcast.434, f32[4,16,196,196]{2,3,1,0:T(8,128)} %get-tuple-element.146, f32[4,16,196]{2,1,0:T(8,128)S(1)} %log_add_fusion), kind=kOutput, calls=%fused_computation.129 | convolution fusion | flops 165129216 | bytes 15008768 | tf_op jit(solution)/shard_map/bhqk,bkhd->bqhd/dot_general | solution.py:726
  267.3 15.2 %fusion.3 = bf16[4,196,2048]{2,1,0:T(8,128)(2,1)S(1)} fusion(f32[4,196,2048]{2,1,0:T(8,128)S(1)} %get-tuple-element.148, u8[196,2048]{1,0:T(8,128)(4,1)S(1)} %get-tuple-element.60, u8[196,2048]{1,0:T(8,128)(4,1)S(1)} %get-tuple-element.59), kind=kLoop, calls=%fused_computation.14 | loop fusion | flops 112394240 | bytes 10436608 | tf_op jit(solution)/shard_map/convert_element_type | solution.py:732
  306.7 13.5 %multiply_reduce_fusion = (f32[4,16,196]{2,1,0:T(8,128)S(1)}, f32[4,16,196,196]{2,3,1,0:T(8,128)}) fusion(f32[4,16,196,196]{2,3,1,0:T(8,128)} %get-tuple-element.146, f32[4,16,196]{2,1,0:T(8,128)S(1)} %log_add_fusion, bf16[4,196,16,32]{1,3,2,0:T(8,128)(2,1)} %bitcast.441, bf16[4,196,3,16,32]{1,4,3,2,0:T(8,128)(2,1)} %bitcast.435), kind=kOutput, calls=%fused_computation.5 | convolution fusion | flops 167173888 | bytes 25139200 | tf_op jit(solution)/shard_map/bqhd,bkhd->bhqk/dot_general | solution.py:786
  320.2 8.9 %multiply_convert_fusion = bf16[4,16,196,196]{2,3,1,0:T(8,128)(2,1)} fusion(f32[4,16,196,196]{2,3,1,0:T(8,128)} %get-tuple-element.153, f32[4,16,196,196]{2,3,1,0:T(8,128)S(1)} %bitcast.432, f32[4,16,196]{2,1,0:T(8,128)S(1)} %get-tuple-element.152, f32[4,16,196]{2,1,0:T(8,128)S(1)} %log_add_fusion), kind=kLoop, calls=%fused_computation.4 | loop fusion | flops 12293120 | bytes 24686592 | tf_op jit(solution)/shard_map/convert_element_type | solution.py:794
  329.1 4.1 multiply_bitcast_fusion.1
  333.2 6.1 multiply_bitcast_fusion
  360.9 4.9 copy.87
  365.8 5.6 fusion.34
  376.8 4.5 fusion.16
  396.4 4.9 convert_element_type.254
  404.9 6.9 %fusion.95 = f32[768,3072,1]{1,0,2:T(8,128)} fusion(bf16[4,64,3072]{2,1,0:T(8,128)(2,1)} %copy-done.123, f32[4,64,768]{2,1,0:T(8,128)} %copy-done.40, f32[768]{0:T(1024)} %copy-done.114, f32[768]{0:T(1024)} %copy-done.109, f32[4,64]{1,0:T(4,128)} %copy-done.110, f32[4,64]{1,0:T(4,128)} %copy-done.97), kind=kOutput, calls=%fused_computation.254 | convolution fusion | flops 1208942592 | bytes 11804672 | tf_op jit(solution)/shard_map/bsi,bsj->ij/dot_general | solution.py:680
  429.3 4.1 constant_dynamic-update-slice_fusion.8
  456.9 154.2 %reduce_scatter.1 = (f32[3072,128]{1,0:T(8,128)}, f32[4,4,3072,128]{3,2,1,0:T(8,128)}) custom-call(f32[90904,128]{1,0:T(8,128)} %broadcast_dynamic-update-slice_fusion.grad_ref), custom_call_target="tpu_custom_call" | custom-call | tf_op jit(solution)/shard_map/reduce_scatter/pallas_call | solution.py:599
  619.4 10.2 %share_all.1 = f32[32,8,128]{2,1,0:T(8,128)} custom-call(f32[8,128]{1,0:T(8,128)} %scatter.9.in_ref), custom_call_target="tpu_custom_call" | custom-call | tf_op jit(solution)/shard_map/share_all/pallas_call | solution.py:652
  634.1 5.9 multiply_subtract_fusion
  (436 shorter events, 176.2 us)
Async XLA Ops:
  145.4 20.8 %copy-start.96 = (s32[4,196]{1,0:T(4,128)S(1)}, s32[4,196]{1,0:T(4,128)}, u32[]{:S(2)}) copy-start(s32[4,196]{1,0:T(4,128)} %param.14) | copy-start | bytes 9412
  166.7 207.2 %copy-start.111 = (pred[4,64]{1,0:T(4,128)(4,1)}, pred[4,64]{1,0:T(4,128)(4,1)S(1)}, u32[]{:S(2)}) copy-start(pred[4,64]{1,0:T(4,128)(4,1)S(1)} %get-tuple-element.164) | copy-start | bytes 772
  172.2 16.6 %copy-start.114 = (f32[768]{0:T(1024)}, f32[768]{0:T(1024)S(1)}, u32[]{:S(2)}) copy-start(f32[768]{0:T(1024)S(1)} %get-tuple-element.112) | copy-start | bytes 9220
  172.2 31.0 %copy-start.105 = (f32[768]{0:T(1024)}, f32[768]{0:T(1024)S(1)}, u32[]{:S(2)}) copy-start(f32[768]{0:T(1024)S(1)} %get-tuple-element.111) | copy-start | bytes 9220
  172.2 204.2 %copy-start.84 = (f32[768]{0:T(1024)}, f32[768]{0:T(1024)S(1)}, u32[]{:S(2)}) copy-start(f32[768]{0:T(1024)S(1)} %get-tuple-element.110) | copy-start | bytes 9220
  172.2 211.3 %copy-start.109 = (f32[768]{0:T(1024)}, f32[768]{0:T(1024)S(1)}, u32[]{:S(2)}) copy-start(f32[768]{0:T(1024)S(1)} %get-tuple-element.113) | copy-start | bytes 9220
  188.5 195.0 %copy-start.97 = (f32[4,64]{1,0:T(4,128)}, f32[4,64]{1,0:T(4,128)S(1)}, u32[]{:S(2)}) copy-start(f32[4,64]{1,0:T(4,128)S(1)} %broadcast_multiply_fusion.17) | copy-start | bytes 3076
  188.8 194.8 %copy-start.110 = (f32[4,64]{1,0:T(4,128)}, f32[4,64]{1,0:T(4,128)S(1)}, u32[]{:S(2)}) copy-start(f32[4,64]{1,0:T(4,128)S(1)} %add_rsqrt_fusion.5) | copy-start | bytes 3076
  203.0 173.5 %copy-start.94 = (f32[4,64]{1,0:T(4,128)}, f32[4,64]{1,0:T(4,128)S(1)}, u32[]{:S(2)}) copy-start(f32[4,64]{1,0:T(4,128)S(1)} %broadcast_multiply_fusion.16) | copy-start | bytes 3076
  203.2 173.2 %copy-start.101 = (f32[4,64]{1,0:T(4,128)}, f32[4,64]{1,0:T(4,128)S(1)}, u32[]{:S(2)}) copy-start(f32[4,64]{1,0:T(4,128)S(1)} %add_rsqrt_fusion.4) | copy-start | bytes 3076
  227.8 35.8 %copy-start.82 = (f32[1,512]{1,0:T(1,128)}, f32[1,512]{1,0:T(1,128)S(1)}, u32[]{:S(2)}) copy-start(f32[1,512]{1,0:T(1,128)S(1)} %get-tuple-element.118) | copy-start | bytes 6148
  227.8 60.5 %copy-start.120 = (f32[1,512]{1,0:T(1,128)}, f32[1,512]{1,0:T(1,128)S(1)}, u32[]{:S(2)}) copy-start(f32[1,512]{1,0:T(1,128)S(1)} %get-tuple-element.117) | copy-start | bytes 6148
  227.8 122.6 %copy-start.103 = (f32[1,512]{1,0:T(1,128)}, f32[1,512]{1,0:T(1,128)S(1)}, u32[]{:S(2)}) copy-start(f32[1,512]{1,0:T(1,128)S(1)} %get-tuple-element.116) | copy-start | bytes 6148
  263.2 37.2 %copy-start.20 = (f32[4,196,512]{2,1,0:T(8,128)}, f32[4,196,512]{2,1,0:T(8,128)S(1)}, u32[]{:S(2)}) copy-start(f32[4,196,512]{2,1,0:T(8,128)S(1)} %get-tuple-element.101) | copy-start | bytes 4816900
  267.2 15.2 %copy-start.8 = (bf16[1024,8,128]{2,1,0:T(8,128)(2,1)S(1)}, bf16[1024,8,128]{2,1,0:T(8,128)(2,1)}, u32[]{:S(2)}) copy-start(bf16[1024,8,128]{2,1,0:T(8,128)(2,1)} %copy-done.7) | copy-start | bytes 6291460
  285.6 64.8 %copy-start.79 = (f32[4,196]{1,0:T(4,128)}, f32[4,196]{1,0:T(4,128)S(1)}, u32[]{:S(2)}) copy-start(f32[4,196]{1,0:T(4,128)S(1)} %broadcast_multiply_fusion.7) | copy-start | bytes 9412
  286.0 64.4 %copy-start.89 = (f32[4,196]{1,0:T(4,128)}, f32[4,196]{1,0:T(4,128)S(1)}, u32[]{:S(2)}) copy-start(f32[4,196]{1,0:T(4,128)S(1)} %add_rsqrt_fusion.1) | copy-start | bytes 9412
  306.6 13.5 %slice-start = ((s8[13107200]{0:T(1024)(128)(4,1)}), s8[4194304]{0:T(1024)(128)(4,1)S(1)}, s32[]{:S(2)}) async-start(s8[13107200]{0:T(1024)(128)(4,1)} %bitcast.431), calls=%async_computation | async-start | bytes 8388608
  306.6 13.5 %slice-start.1 = ((s8[13107200]{0:T(1024)(128)(4,1)}), s8[4194304]{0:T(1024)(128)(4,1)S(1)}, s32[]{:S(2)}) async-start(s8[13107200]{0:T(1024)(128)(4,1)} %bitcast.431), calls=%async_computation.1 | async-start | bytes 8388608
  306.6 13.5 %slice-start.2 = ((s8[13107200]{0:T(1024)(128)(4,1)}), s8[4194304]{0:T(1024)(128)(4,1)S(1)}, s32[]{:S(2)}) async-start(s8[13107200]{0:T(1024)(128)(4,1)} %bitcast.431), calls=%async_computation.2 | async-start | bytes 8388608
  306.6 13.5 %slice-start.3 = ((s8[13107200]{0:T(1024)(128)(4,1)}), s8[524288]{0:T(1024)(128)(4,1)S(1)}, s32[]{:S(2)}) async-start(s8[13107200]{0:T(1024)(128)(4,1)} %bitcast.431), calls=%async_computation.3 | async-start | bytes 1048576
  611.1 22.4 %copy-start.122 = (f32[2]{0:T(128)S(1)}, f32[2]{0:T(128)}, u32[]{:S(2)}) copy-start(f32[2]{0:T(128)} %param.19) | copy-start | bytes 28
  611.1 23.0 %copy-start.52 = (f32[362752]{0:T(1024)S(1)}, f32[362752]{0:T(1024)}, u32[]{:S(2)}) copy-start(f32[362752]{0:T(1024)} %param.16) | copy-start | bytes 4353028
  614.4 19.7 %copy-start.29 = (f32[2834,128]{1,0:T(8,128)S(1)}, f32[2834,128]{1,0:T(8,128)}, u32[]{:S(2)}) copy-start(f32[2834,128]{1,0:T(8,128)} %to_lines.1) | copy-start | bytes 4353028
  (113 other events, 376.8 us)

commit v2 on v1

--- a/solution.py
+++ b/solution.py
@@ -661,40 +661,478 @@
 
 
 NORM_EPS = 1e-06
-ADAM_EPS = 1e-08
-BETA_ONE = 0.9
-BETA_TWO = 0.95
-DECAY = 0.05
 NEG_FILL = -1000000000.0
-
-
-def mult(left, right):
-    return jnp.einsum("bsi,ij->bsj", left, right, preferred_element_type=jnp.float32)
-
-
-def mult_back(grad, right):
-    return jnp.einsum("bsj,ij->bsi", grad, right, preferred_element_type=jnp.float32)
-
-
-def outer(left, grad):
-    return jnp.einsum("bsi,bsj->ij", left, grad, preferred_element_type=jnp.float32)
-
-
-def layer_norm(x, gain, shift):
+P_ROWS = 208
+BF = jnp.bfloat16
+F32 = jnp.float32
+
+
+def dot_nn(left, right):
+    return lax.dot_general(left, right, (((1,), (0,)), ((), ())), preferred_element_type=F32)
+
+
+def dot_nt(left, right):
+    return lax.dot_general(left, right, (((1,), (1,)), ((), ())), preferred_element_type=F32)
+
+
+def loop(count, body, unroll=1):
+    def step(i, _):
+        body(i)
+        return 0
+
+    lax.fori_loop(0, count, step, 0, unroll=unroll)
+
+
+def rows_at(i, size):
+    return pl.ds(pl.multiple_of(i * size, size), size)
+
+
+def norm(x):
     centered = x - jnp.mean(x, axis=-1, keepdims=True)
     scale = lax.rsqrt(jnp.mean(centered * centered, axis=-1, keepdims=True) + NORM_EPS)
-    normed = centered * scale
-    return (normed * gain + shift, normed, scale)
-
-
-def norm_back(grad, normed, scale, gain):
+    return centered * scale, scale
+
+
+def norm_grad(grad, plain, scale, gain):
     inner = grad * gain
-    back = scale * (
-        inner
-        - jnp.mean(inner, axis=-1, keepdims=True)
-        - normed * jnp.mean(inner * normed, axis=-1, keepdims=True)
-    )
-    return (back, jnp.sum(grad * normed, axis=(0, 1)), jnp.sum(grad, axis=(0, 1)))
+    back = scale * (inner - jnp.mean(inner, axis=-1, keepdims=True) - plain * jnp.mean(inner * plain, axis=-1, keepdims=True))
+    return back, jnp.sum(grad * plain, axis=0, keepdims=True), jnp.sum(grad, axis=0, keepdims=True)
+
+
+def gelu_pair(h):
+    cumulative = 0.5 * (1.0 + lax.erf(h * 0.7071067811865476))
+    density = jnp.exp(-0.5 * h * h) * 0.3989422804014327
+    return h * cumulative, cumulative + h * density
+
+
+def head_masks(size):
+    lane = lax.broadcasted_iota(jnp.int32, (1, LANES), 1)
+    shift = size.bit_length() - 1
+    return [jnp.where((lane >> shift) == h, 1.0, 0.0).astype(BF) for h in range(LANES // size)]
+
+
+def three(value):
+    top = value.astype(BF)
+    rest = value - top.astype(F32)
+    mid = rest.astype(BF)
+    return top, mid, (rest - mid.astype(F32)).astype(BF)
+
+
+def block_forward(x, rows, images, length, heads, weights, norms, key_bias, saved):
+    triple_w, proj_w, up_w, down_w = weights
+    entry, plain1, scale1, triple, probs, mixed, plain2, scale2, inner, act, slope = saved
+    width = x.shape[1]
+    size = width // heads
+    per = LANES // size
+    groups = width // LANES
+    hidden = up_w.shape[1]
+
+    def first(i):
+        at = rows_at(i, rows)
+        plain, scale = norm(x[at, :])
+        plain1[at, :] = plain
+        scale1[at, :] = scale
+        entry[at, :] = (plain * norms[0:1, :] + norms[1:2, :]).astype(BF)
+
+    loop(images, first)
+
+    def project(j):
+        at = rows_at(j, 256)
+        triple[:, at] = dot_nn(entry[...], triple_w[:, at]).astype(BF)
+
+    loop(3 * width // 256, project)
+    masks = head_masks(size)
+
+    def attend(i):
+        at = rows_at(i, rows)
+        bias = key_bias(i)
+        for g in range(groups):
+            q = triple[at, g * LANES : (g + 1) * LANES]
+            k = triple[at, width + g * LANES : width + (g + 1) * LANES]
+            v = triple[at, 2 * width + g * LANES : 2 * width + (g + 1) * LANES]
+            v_side = v.T
+            parts = []
+            for h in range(per):
+                s = dot_nt(k * masks[h], q) * size ** (-0.5) + bias
+                e = jnp.exp(s - jnp.max(s, axis=0, keepdims=True))
+                p = e * (1.0 / jnp.sum(e, axis=0, keepdims=True))
+                probs[i * groups + g, h * rows : (h + 1) * rows, :] = p
+                parts.append(dot_nn(v_side[h * size : (h + 1) * size, :], p.astype(BF)))
+            mixed[at, g * LANES : (g + 1) * LANES] = jnp.concatenate(parts, axis=0).T.astype(BF)
+
+    loop(images, attend)
+
+    def middle(j):
+        at = rows_at(j, 256)
+        x[:, at] += dot_nn(mixed[...], proj_w[:, at])
+
+    loop(width // 256, middle)
+
+    def second(i):
+        at = rows_at(i, rows)
+        plain, scale = norm(x[at, :])
+        plain2[at, :] = plain
+        scale2[at, :] = scale
+        inner[at, :] = (plain * norms[2:3, :] + norms[3:4, :]).astype(BF)
+
+    loop(images, second)
+
+    def up(j):
+        at = rows_at(j, 256)
+        value, gradient = gelu_pair(dot_nn(inner[...], up_w[:, at]))
+        act[:, at] = value.astype(BF)
+        slope[:, at] = gradient
+
+    loop(hidden // 256, up)
+
+    def down(j):
+        at = rows_at(j, 256)
+        x[:, at] += dot_nn(act[...], down_w[:, at])
+
+    loop(width // 256, down)
+
+
+class Writer:
+    def __init__(self, flat, stage, sem):
+        self.flat, self.stage, self.sem = flat, stage, sem
+
+    def outer(self, number, left, right, chunk=256):
+        _, _, cols, tile, _ = ENTRIES[number]
+        rows = left.shape[1]
+        count = rows // chunk
+        tall = chunk // 8
+
+        def copy(i, s):
+            return pltpu.make_async_copy(
+                self.stage.at[s, pl.ds(0, tall * cols)], self.flat.at[pl.ds(tile + i * tall * cols, tall * cols)], self.sem.at[s]
+            )
+
+        def body(i):
+            s = lax.rem(i, 2)
+
+            @pl.when(i >= 2)
+            def _():
+                copy(i - 2, s).wait()
+
+            side = left[:, rows_at(i, chunk)].T
+            for c in range(0, cols, 2):
+                value = dot_nn(side, right[:, c * LANES : (c + 2) * LANES])
+                for d in range(2):
+                    self.stage[s, pl.ds(c + d, tall, stride=cols)] = value[:, d * LANES : (d + 1) * LANES].reshape(tall, 8, LANES)
+            copy(i, s).start()
+
+        loop(count, body)
+        for i in range(max(0, count - 2), count):
+            copy(i, i % 2).wait()
+
+
+def block_backward(grad, rows, images, length, heads, weights, norms, norm_sums, saved, extra, writer, numbers):
+    triple_w, proj_w, up_w, down_w = weights
+    entry, plain1, scale1, triple, probs, mixed, plain2, scale2, inner, act, slope = saved
+    low, grad_hidden, side, low_mixed, grad_triple = extra
+    width = grad.shape[1]
+    size = width // heads
+    per = LANES // size
+    groups = width // LANES
+    hidden = up_w.shape[1]
+    low[...] = grad[...].astype(BF)
+
+    def back_up(j):
+        at = rows_at(j, 256)
+        grad_hidden[:, at] = (dot_nt(low[...], down_w[at, :]) * slope[:, at]).astype(BF)
+
+    loop(hidden // 256, back_up)
+    writer.outer(numbers[3], act, low)
+    writer.outer(numbers[2], inner, grad_hidden)
+
+    def back_inner(j):
+        at = rows_at(j, 256)
+        side[:, at] = dot_nt(grad_hidden[...], up_w[at, :])
+
+    loop(width // 256, back_inner)
+
+    def second(i):
+        at = rows_at(i, rows)
+        back, gain, shift = norm_grad(side[at, :], plain2[at, :], scale2[at, :], norms[2:3, :])
+        norm_sums[2:3, :] += gain
+        norm_sums[3:4, :] += shift
+        total = grad[at, :] + back
+        grad[at, :] = total
+        low[at, :] = total.astype(BF)
+
+    loop(images, second)
+    writer.outer(numbers[1], mixed, low)
+
+    def back_mixed(j):
+        at = rows_at(j, 256)
+        low_mixed[:, at] = dot_nt(low[...], proj_w[at, :]).astype(BF)
+
+    loop(width // 256, back_mixed)
+    masks = head_masks(size)
+
+    def attend(i):
+        at = rows_at(i, rows)
+        for g in range(groups):
+            lanes = [slice(t * width + g * LANES, t * width + (g + 1) * LANES) for t in range(3)]
+            q, k, v = (triple[at, lane] for lane in lanes)
+            dm = low_mixed[at, g * LANES : (g + 1) * LANES]
+            k_side = k.T
+            parts, dk, dv = [], 0.0, 0.0
+            for h in range(per):
+                p = probs[i * groups + g, h * rows : (h + 1) * rows, :]
+                dp = dot_nt(v * masks[h], dm)
+                ds = (p * (dp - jnp.sum(p * dp, axis=0, keepdims=True))).astype(BF)
+                dv = dv + dot_nn(p.astype(BF), dm * masks[h])
+                dk = dk + dot_nn(ds, q * masks[h])
+                parts.append(dot_nn(k_side[h * size : (h + 1) * size, :], ds))
+            dq = jnp.concatenate(parts, axis=0).T
+            grad_triple[at, lanes[0]] = (dq * size ** (-0.5)).astype(BF)
+            grad_triple[at, lanes[1]] = (dk * size ** (-0.5)).astype(BF)
+            grad_triple[at, lanes[2]] = dv.astype(BF)
+
+    loop(images, attend)
+    writer.outer(numbers[0], entry, grad_triple)
+
+    def back_entry(j):
+        at = rows_at(j, 256)
+        side[:, at] = dot_nt(grad_triple[...], triple_w[at, :])
+
+    loop(width // 256, back_entry)
+
+    def first(i):
+        at = rows_at(i, rows)
+        back, gain, shift = norm_grad(side[at, :], plain1[at, :], scale1[at, :], norms[0:1, :])
+        norm_sums[0:1, :] += gain
+        norm_sums[1:2, :] += shift
+        grad[at, :] += back
+
+    loop(images, first)
+
+
+def write_small(number, norm_sums, count, flat, stage, sem):
+    _, lines, _, tile, groups = ENTRIES[number]
+    per = SHAPES[number][1] // LANES
+    stage[0, 0:groups] = jnp.zeros((groups, 8, LANES), F32)
+    for r in range(count):
+        for c in range(per):
+            line = r * per + c
+            stage[0, line // 8, line % 8 : line % 8 + 1, :] = norm_sums[r : r + 1, c * LANES : (c + 1) * LANES]
+    copy = pltpu.make_async_copy(stage.at[0, pl.ds(0, groups)], flat.at[pl.ds(tile, groups)], sem.at[0])
+    copy.start()
+    copy.wait()
+
+
+def encoder_kernel(images, counts_ref, patches_ref, cols_ref, pos_ref, embed_ref, triple_ref, proj_ref, up_ref, down_ref, norms_ref, dec_embed_ref,
+                   seen, entry, plain1, scale1, triple, probs, mixed, plain2, scale2, inner, act, slope, plain3, scale3, encoded, entering, x, place, pos_split):
+    spots = lax.broadcasted_iota(jnp.int32, (KEEP, P_ROWS), 1)
+    for t, part in enumerate(three(pos_ref[...])):
+        pos_split[t] = part
+
+    def select(i):
+        at = rows_at(i, KEEP)
+        pick = jnp.where(spots == cols_ref[i], 1.0, 0.0).astype(BF)
+        seen[at, :] = dot_nn(pick, patches_ref[rows_at(i, P_ROWS), :]).astype(BF)
+        place[at, :] = dot_nn(pick, pos_split[0]) + dot_nn(pick, pos_split[1]) + dot_nn(pick, pos_split[2])
+
+    loop(images, select)
+
+    def embed(j):
+        at = rows_at(j, 256)
+        x[:, at] = dot_nn(seen[...], embed_ref[:, at]) + place[:, at]
+
+    loop(D // 256, embed)
+    slot = lax.broadcasted_iota(jnp.int32, (KEEP, 1), 0)
+
+    def key_bias(i):
+        return jnp.where(slot < counts_ref[i], 0.0, NEG_FILL)
+
+    block_forward(x, KEEP, images, KEEP, HEADS, (triple_ref, proj_ref, up_ref, down_ref), norms_ref, key_bias,
+                  (entry, plain1, scale1, triple, probs, mixed, plain2, scale2, inner, act, slope))
+
+    def last(i):
+        at = rows_at(i, KEEP)
+        plain, scale = norm(x[at, :])
+        plain3[at, :] = plain
+        scale3[at, :] = scale
+        encoded[at, :] = (plain * norms_ref[4:5, :] + norms_ref[5:6, :]).astype(BF)
+
+    loop(images, last)
+    entering[...] = dot_nn(encoded[...], dec_embed_ref[...])
+
+
+def encoder(counts, patches, cols, pos, weights, norms, dec_embed):
+    images = counts.shape[0]
+    rows = images * KEEP
+    vmem = pl.BlockSpec(memory_space=pltpu.VMEM)
+
+    def s(shape, kind):
+        return jax.ShapeDtypeStruct(shape, kind)
+
+    return pl.pallas_call(
+        functools.partial(encoder_kernel, images),
+        name="encoder",
+        out_shape=[
+            s((rows, D), BF), s((rows, D), BF), s((rows, D), F32), s((rows, 1), F32), s((rows, 3 * D), BF),
+            s((images * D // LANES, LANES, KEEP), F32), s((rows, D), BF), s((rows, D), F32), s((rows, 1), F32), s((rows, D), BF),
+            s((rows, F), BF), s((rows, F), F32), s((rows, D), F32), s((rows, 1), F32), s((rows, D), BF), s((rows, DD), F32),
+        ],
+        in_specs=[pl.BlockSpec(memory_space=pltpu.SMEM)] + [vmem] * 10,
+        out_specs=[vmem] * 16,
+        scratch_shapes=[pltpu.VMEM((rows, D), F32), pltpu.VMEM((rows, D), F32), pltpu.VMEM((3, P_ROWS, D), BF)],
+        compiler_params=pltpu.CompilerParams(vmem_limit_bytes=60 * MB),
+    )(counts, patches, cols, pos, *weights, norms, dec_embed)
+
+
+def decoder_kernel(images, counts_ref, masked_ref, patches_ref, cols_ref, rows_ref, pos_ref, entering_ref, triple_ref, proj_ref, up_ref, down_ref, head_ref, norms_ref,
+                   flat, grad_entering, loss_ref,
+                   x, hide, entry, plain1, scale1, triple, probs, mixed, plain2, scale2, inner, act, slope, plain3, scale3, final, grad_pred,
+                   low, grad_hidden, side, low_mixed, grad_triple, norm_sums, stage, sem):
+    lane = lax.broadcasted_iota(jnp.int32, (P_ROWS, KEEP), 1)
+    spot = lax.broadcasted_iota(jnp.int32, (P_ROWS, KEEP), 0)
+    line = lax.broadcasted_iota(jnp.int32, (P_ROWS, 1), 0)
+
+    def start(i):
+        at = rows_at(i, P_ROWS)
+        hit = jnp.where(jnp.logical_and(spot == rows_ref[pl.ds(i, 1), 0:KEEP], lane < counts_ref[i]), 1.0, 0.0)
+        shown = jnp.max(hit, axis=1, keepdims=True)
+        pick = hit.astype(BF)
+        top, mid, end = three(entering_ref[rows_at(i, KEEP), :])
+        picked = dot_nn(pick, top) + dot_nn(pick, mid) + dot_nn(pick, end)
+        x[at, :] = jnp.where(shown > 0.0, picked, norms_ref[6:7, :]) + pos_ref[...]
+        hide[at, :] = jnp.where(jnp.logical_and(line < PATCHES, shown == 0.0), 1.0, 0.0)
+
+    loop(images, start)
+    bias = jnp.where(line < PATCHES, 0.0, NEG_FILL)
+    weights = (triple_ref, proj_ref, up_ref, down_ref)
+    saved = (entry, plain1, scale1, triple, probs, mixed, plain2, scale2, inner, act, slope)
+    block_forward(x, P_ROWS, images, PATCHES, DHEADS, weights, norms_ref, lambda i: bias, saved)
+
+    def last(i):
+        at = rows_at(i, P_ROWS)
+        plain, scale = norm(x[at, :])
+        plain3[at, :] = plain
+        scale3[at, :] = scale
+        final[at, :] = (plain * norms_ref[4:5, :] + norms_ref[5:6, :]).astype(BF)
+
+    loop(images, last)
+    loss_ref[...] = jnp.zeros_like(loss_ref)
+    masked = masked_ref[0:1, 0:1]
+
+    def score(i):
+        at = rows_at(i, P_ROWS)
+        target, _ = norm(patches_ref[at, :].astype(F32))
+        diff = dot_nn(final[at, :], head_ref[...]) - target
+        hidden = hide[at, :]
+        loss_ref[...] += jnp.sum(jnp.mean(diff * diff, axis=-1, keepdims=True) * hidden, axis=0, keepdims=True)
+        grad_pred[at, :] = (diff * (hidden * (2.0 / PIX)) / masked).astype(BF)
+
+    loop(images, score)
+    writer = Writer(flat, stage, sem)
+    writer.outer(11, final, grad_pred)
+    norm_sums[...] = jnp.zeros_like(norm_sums)
+
+    def back_final(i):
+        at = rows_at(i, P_ROWS)
+        back, gain, shift = norm_grad(dot_nt(grad_pred[at, :], head_ref[...]), plain3[at, :], scale3[at, :], norms_ref[4:5, :])
+        norm_sums[4:5, :] += gain
+        norm_sums[5:6, :] += shift
+        x[at, :] = back
+
+    loop(images, back_final)
+    block_backward(x, P_ROWS, images, PATCHES, DHEADS, weights, norms_ref, norm_sums, saved, (low, grad_hidden, side, low_mixed, grad_triple), writer, (7, 8, 9, 10))
+    spots = lax.broadcasted_iota(jnp.int32, (KEEP, P_ROWS), 1)
+    slot = lax.broadcasted_iota(jnp.int32, (KEEP, P_ROWS), 0)
+
+    def finish(i):
+        at = rows_at(i, P_ROWS)
+        grad = x[at, :]
+        norm_sums[6:7, :] += jnp.sum(grad * hide[at, :], axis=0, keepdims=True)
+        pick = jnp.where(jnp.logical_and(spots == cols_ref[i], slot < counts_ref[i]), 1.0, 0.0).astype(BF)
+        grad_entering[rows_at(i, KEEP), :] = dot_nn(pick, grad.astype(BF)).astype(BF)
+
+    loop(images, finish)
+    write_small(12, norm_sums, 7, flat, stage, sem)
+    extra = flat.shape[0] - TILES
+    if extra > 0:
+        stage[0, 0:extra] = jnp.zeros((extra, 8, LANES), F32)
+        copy = pltpu.make_async_copy(stage.at[0, pl.ds(0, extra)], flat.at[pl.ds(TILES, extra)], sem.at[0])
+        copy.start()
+        copy.wait()
+
+
+def decoder(total, counts, masked, patches, cols, order, pos, entering, weights, head, norms):
+    images = counts.shape[0]
+    rows = images * P_ROWS
+    vmem = pl.BlockSpec(memory_space=pltpu.VMEM)
+
+    def v(shape, kind=F32):
+        return pltpu.VMEM(shape, kind)
+
+    return pl.pallas_call(
+        functools.partial(decoder_kernel, images),
+        name="decoder",
+        out_shape=[
+            jax.ShapeDtypeStruct((total, 8, LANES), F32),
+            jax.ShapeDtypeStruct((images * KEEP, DD), BF),
+            jax.ShapeDtypeStruct((1, 1), F32),
+        ],
+        in_specs=[pl.BlockSpec(memory_space=pltpu.SMEM)] + [vmem] * 12,
+        out_specs=[pl.BlockSpec(memory_space=pl.ANY), vmem, vmem],
+        scratch_shapes=[
+            v((rows, DD)), v((rows, 1)), v((rows, DD), BF), v((rows, DD)), v((rows, 1)), v((rows, 3 * DD), BF),
+            v((images * DD // LANES, 4 * P_ROWS, P_ROWS)), v((rows, DD), BF), v((rows, DD)), v((rows, 1)), v((rows, DD), BF),
+            v((rows, FD), BF), v((rows, FD)), v((rows, DD)), v((rows, 1)), v((rows, DD), BF), v((rows, PIX), BF),
+            v((rows, DD), BF), v((rows, FD), BF), v((rows, DD)), v((rows, DD), BF), v((rows, 3 * DD), BF),
+            v((8, DD)), v((2, 32 * 16, 8, LANES)), pltpu.SemaphoreType.DMA((2,)),
+        ],
+        compiler_params=pltpu.CompilerParams(vmem_limit_bytes=63 * MB),
+    )(counts, masked, patches, cols, order, pos, entering, *weights, head, norms)
+
+
+def encoder_back_kernel(images, flat_in, grad_entering, seen, entry, plain1, scale1, triple, probs, mixed, plain2, scale2, inner, act, slope, plain3, scale3, encoded,
+                        triple_ref, proj_ref, up_ref, down_ref, norms_ref, dec_embed_ref, flat, x, low, grad_hidden, side, low_mixed, grad_triple, norm_sums, stage, sem):
+    writer = Writer(flat, stage, sem)
+    writer.outer(6, encoded, grad_entering)
+    norm_sums[...] = jnp.zeros_like(norm_sums)
+    side[...] = dot_nt(grad_entering[...], dec_embed_ref[...])
+
+    def last(i):
+        at = rows_at(i, KEEP)
+        back, gain, shift = norm_grad(side[at, :], plain3[at, :], scale3[at, :], norms_ref[4:5, :])
+        norm_sums[4:5, :] += gain
+        norm_sums[5:6, :] += shift
+        x[at, :] = back
+
+    loop(images, last)
+    block_backward(x, KEEP, images, KEEP, HEADS, (triple_ref, proj_ref, up_ref, down_ref), norms_ref, norm_sums,
+                   (entry, plain1, scale1, triple, probs, mixed, plain2, scale2, inner, act, slope), (low, grad_hidden, side, low_mixed, grad_triple), writer, (1, 2, 3, 4))
+    low[...] = x[...].astype(BF)
+    writer.outer(0, seen, low)
+    write_small(5, norm_sums, 6, flat, stage, sem)
+
+
+def encoder_back(flat, grad_entering, saved, weights, norms, dec_embed):
+    rows = grad_entering.shape[0]
+    images = rows // KEEP
+    vmem = pl.BlockSpec(memory_space=pltpu.VMEM)
+    anyspec = pl.BlockSpec(memory_space=pl.ANY)
+
+    def v(shape, kind=F32):
+        return pltpu.VMEM(shape, kind)
+
+    return pl.pallas_call(
+        functools.partial(encoder_back_kernel, images),
+        name="encoder_back",
+        out_shape=jax.ShapeDtypeStruct(flat.shape, flat.dtype),
+        in_specs=[anyspec] + [vmem] * (1 + len(saved) + 6),
+        out_specs=anyspec,
+        scratch_shapes=[
+            v((rows, D)), v((rows, D), BF), v((rows, F), BF), v((rows, D)), v((rows, D), BF), v((rows, 3 * D), BF),
+            v((8, D)), v((2, 32 * 24, 8, LANES)), pltpu.SemaphoreType.DMA((2,)),
+        ],
+        input_output_aliases={0: 0},
+        compiler_params=pltpu.CompilerParams(vmem_limit_bytes=60 * MB),
+    )(flat, grad_entering, *saved, *weights, norms, dec_embed)
 
 
 def positions(width):
@@ -706,107 +1144,10 @@
     return jnp.concatenate([jnp.sin(row), jnp.cos(row), jnp.sin(column), jnp.cos(column)], axis=1)
 
 
-def attention_scores(query, keys, bias, size):
-    scores = jnp.einsum("bqhd,bkhd->bhqk", query, keys, preferred_element_type=jnp.float32)
-    return scores * size ** (-0.5) + bias[:, None, None, :]
-
-
-def block_forward(x, weights, gains, heads, bias):
-    triple_w, proj_w, up_w, down_w = weights
-    batch, length, width = x.shape
-    size = width // heads
-    normed_one, plain_one, scale_one = layer_norm(x, gains[0], gains[1])
-    entry = normed_one.astype(jnp.bfloat16)
-    triple = mult(entry, triple_w).astype(jnp.bfloat16).reshape(batch, length, 3, heads, size)
-    query, keys, values = (triple[:, :, 0], triple[:, :, 1], triple[:, :, 2])
-    scores = attention_scores(query, keys, bias, size)
-    top = jnp.max(scores, axis=-1, keepdims=True)
-    log_total = top + jnp.log(jnp.sum(jnp.exp(scores - top), axis=-1, keepdims=True))
-    attend = jnp.exp(scores - log_total).astype(jnp.bfloat16)
-    mixed = jnp.einsum("bhqk,bkhd->bqhd", attend, values, preferred_element_type=jnp.float32)
-    mixed = mixed.astype(jnp.bfloat16).reshape(batch, length, width)
-    middle = x + mult(mixed, proj_w)
-    normed_two, plain_two, scale_two = layer_norm(middle, gains[2], gains[3])
-    inner = normed_two.astype(jnp.bfloat16)
-    hidden = mult(inner, up_w)
-    activated = jax.nn.gelu(hidden, approximate=False).astype(jnp.bfloat16)
-    result = middle + mult(activated, down_w)
-    saved = (
-        entry,
-        plain_one,
-        scale_one,
-        query,
-        keys,
-        values,
-        log_total,
-        mixed,
-        plain_two,
-        scale_two,
-        inner,
-        hidden,
-        activated,
-    )
-    return (result, saved)
-
-
-def block_backward(grad, weights, gains, heads, bias, saved):
-    triple_w, proj_w, up_w, down_w = weights
-    (
-        entry,
-        plain_one,
-        scale_one,
-        query,
-        keys,
-        values,
-        log_total,
-        mixed,
-        plain_two,
-        scale_two,
-        inner,
-        hidden,
-        activated,
-    ) = saved
-    batch, length, width = grad.shape
-    size = width // heads
-    low_grad = grad.astype(jnp.bfloat16)
-    grad_down = outer(activated, low_grad)
-    grad_act = mult_back(low_grad, down_w)
-    density = jnp.exp(-0.5 * hidden * hidden) * 0.3989422804014327
-    cumulative = 0.5 * (1.0 + lax.erf(hidden * 0.7071067811865476))
-    grad_hidden = (grad_act * (cumulative + hidden * density)).astype(jnp.bfloat16)
-    grad_up = outer(inner, grad_hidden)
-    back_two, gain_two, shift_two = norm_back(
-        mult_back(grad_hidden, up_w), plain_two, scale_two, gains[2]
-    )
-    grad_mid = grad + back_two
-    mid_low = grad_mid.astype(jnp.bfloat16)
-    grad_proj = outer(mixed, mid_low)
-    grad_mixed = mult_back(mid_low, proj_w).astype(jnp.bfloat16).reshape(batch, length, heads, size)
-    attend = jnp.exp(attention_scores(query, keys, bias, size) - log_total)
-    grad_att = jnp.einsum("bqhd,bkhd->bhqk", grad_mixed, values, preferred_element_type=jnp.float32)
-    grad_values = jnp.einsum(
-        "bhqk,bqhd->bkhd",
-        attend.astype(jnp.bfloat16),
-        grad_mixed,
-        preferred_element_type=jnp.float32,
-    )
-    grad_scores = attend * (grad_att - jnp.sum(attend * grad_att, axis=-1, keepdims=True))
-    grad_scores = grad_scores.astype(jnp.bfloat16)
-    grad_query = jnp.einsum(
-        "bhqk,bkhd->bqhd", grad_scores, keys, preferred_element_type=jnp.float32
-    ) * size ** (-0.5)
-    grad_keys = jnp.einsum(
-        "bhqk,bqhd->bkhd", grad_scores, query, preferred_element_type=jnp.float32
-    ) * size ** (-0.5)
-    grad_triple = jnp.stack([grad_query, grad_keys, grad_values], axis=2)
-    grad_triple = grad_triple.astype(jnp.bfloat16).reshape(batch, length, 3 * width)
-    grad_triple_w = outer(entry, grad_triple)
-    back_one, gain_one, shift_one = norm_back(
-        mult_back(grad_triple, triple_w), plain_one, scale_one, gains[0]
-    )
-    grad_in = grad_mid + back_one
-    gain_grads = jnp.stack([gain_one, shift_one, gain_two, shift_two])
-    return (grad_in, (grad_triple_w, grad_proj, grad_up, grad_down), gain_grads)
+ADAM_EPS = 1e-08
+BETA_ONE = 0.9
+BETA_TWO = 0.95
+DECAY = 0.05
 
 
 def own_lines(flat, share, index):
@@ -822,127 +1163,51 @@
     return lax.dynamic_slice(lines.reshape(-1), (share * index % LANES,), (share,))
 
 
-def body(
-    n_dp, n_pair, patches, patch_order, counts, master, moment1, moment2, block_rates, clip_limit, step_count
-):
+def body(n_dp, n_pair, patches, patch_order, counts, master, moment1, moment2, block_rates, clip_limit, step_count):
     n = n_dp * n_pair
     share = master.shape[0]
+    images = counts.shape[0]
     index = lax.axis_index("dp") * n_pair + lax.axis_index("pair")
-    extra = jnp.zeros((8, LANES), jnp.float32).at[0, : counts.shape[0]].set((PATCHES - counts).astype(jnp.float32))
+    extra = jnp.zeros((8, LANES), F32).at[0, :images].set((PATCHES - counts).astype(F32))
     slab = to_tiles(own_lines(master, share, index), extra, share, n, n_pair)
     slots = gather(slab, n_dp, n_pair)
-    masked = jnp.sum(slots[:, slab.shape[0] - 2, 0, :].astype(jnp.float32))
+    masked = jnp.sum(slots[:, slab.shape[0] - 2, 0, :].astype(F32))
     held = assemble(slots, share)
-    parts = [held[i].reshape(-1)[: SHAPES[i][0] * SHAPES[i][1]].reshape(SHAPES[i]) if i in SMALL else matrix(held[i], i) for i in range(len(SHAPES))]
-    enc_gains = parts[5].astype(jnp.float32)
-    dec_gains = parts[12].astype(jnp.float32)
-    slots = patch_order[:, :KEEP]
-    live = jnp.arange(KEEP)[None, :] < counts[:, None]
-    enc_bias = jnp.where(live, 0.0, NEG_FILL).astype(jnp.float32)
-    seen = jnp.take_along_axis(patches, slots[:, :, None], axis=1)
-    x_start = mult(seen, parts[0]) + jnp.take(positions(D), slots, axis=0)
-    x_end, enc_saved = block_forward(x_start, tuple(parts[1:5]), enc_gains, HEADS, enc_bias)
-    enc_normed, enc_plain, enc_scale = layer_norm(x_end, enc_gains[4], enc_gains[5])
-    encoded = enc_normed.astype(jnp.bfloat16)
-    entering = mult(encoded, parts[6])
-    rank = jnp.argsort(patch_order, axis=1)
-    shown = rank < counts[:, None]
-    picked = jnp.take_along_axis(entering, jnp.minimum(rank, KEEP - 1)[:, :, None], axis=1)
-    token = parts[12][6].astype(jnp.float32)
-    y_start = jnp.where(shown[:, :, None], picked, token) + positions(DD)[None]
-    dec_bias = jnp.zeros(shown.shape, jnp.float32)
-    y_end, dec_saved = block_forward(y_start, tuple(parts[7:11]), dec_gains, DHEADS, dec_bias)
-    final_normed, final_plain, final_scale = layer_norm(y_end, dec_gains[4], dec_gains[5])
-    final = final_normed.astype(jnp.bfloat16)
-    pred = mult(final, parts[11])
-    pixels = patches.astype(jnp.float32)
-    centered = pixels - jnp.mean(pixels, axis=-1, keepdims=True)
-    target = centered * lax.rsqrt(jnp.mean(centered * centered, axis=-1, keepdims=True) + NORM_EPS)
-    diff = pred - target
-    hidden_mask = jnp.where(shown, 0.0, 1.0).astype(jnp.float32)
-    loss_local = jnp.sum(jnp.mean(diff * diff, axis=-1) * hidden_mask)
-    grad_pred = (diff * (hidden_mask[:, :, None] * (2.0 / PIX)) / masked).astype(jnp.bfloat16)
-    again = parts
-    enc_back_gains = again[5].astype(jnp.float32)
-    dec_back_gains = again[12].astype(jnp.float32)
-    grad_head = outer(final, grad_pred)
-    back_final, gain_final, shift_final = norm_back(
-        mult_back(grad_pred, again[11]), final_plain, final_scale, dec_back_gains[4]
+    parts = [held[i].reshape(-1)[: SHAPES[i][0] * SHAPES[i][1]].reshape(SHAPES[i]).astype(F32) if i in SMALL else matrix(held[i], i) for i in range(len(SHAPES))]
+    padded = jnp.pad(patches, ((0, 0), (0, P_ROWS - PATCHES), (0, 0))).reshape(images * P_ROWS, PIX)
+    slots_at = patch_order[:, :KEEP]
+    cols = slots_at[:, :, None]
+    pos_e = jnp.pad(positions(D), ((0, P_ROWS - PATCHES), (0, 0)))
+    pos_d = jnp.pad(positions(DD), ((0, P_ROWS - PATCHES), (0, 0)))
+    enc_weights = parts[1:5]
+    *saved, entering = encoder(counts, padded, cols, pos_e, [parts[0]] + enc_weights, parts[5], parts[6])
+    total = max(a for a, _ in ranges(share, n)) + slab_tiles(share, n)
+    flat, grad_entering, loss_local = decoder(
+        total, counts, masked.reshape(1, 1), padded, cols, slots_at, pos_d, entering, parts[7:11], parts[11], parts[12]
     )
-    grad_y, dec_grads, dec_gain_grads = block_backward(
-        back_final, tuple(again[7:11]), dec_back_gains, DHEADS, dec_bias, dec_saved
-    )
-    grad_token = jnp.sum(grad_y * hidden_mask[:, :, None], axis=(0, 1))
-    grad_entering = jnp.take_along_axis(grad_y, slots[:, :, None], axis=1)
-    grad_entering = jnp.where(live[:, :, None], grad_entering, 0.0).astype(jnp.bfloat16)
-    grad_dec_embed = outer(encoded, grad_entering)
-    back_enc, gain_enc, shift_enc = norm_back(
-        mult_back(grad_entering, again[6]), enc_plain, enc_scale, enc_back_gains[4]
-    )
-    grad_x, enc_grads, enc_gain_grads = block_backward(
-        back_enc, tuple(again[1:5]), enc_back_gains, HEADS, enc_bias, enc_saved
-    )
-    grad_embed = outer(seen, grad_x.astype(jnp.bfloat16))
-    enc_norm_grads = jnp.concatenate([enc_gain_grads, jnp.stack([gain_enc, shift_enc])])
-    dec_norm_grads = jnp.concatenate([dec_gain_grads, jnp.stack([gain_final, shift_final])])
-    grads = [
-        grad_embed,
-        enc_grads[0],
-        enc_grads[1],
-        enc_grads[2],
-        enc_grads[3],
-        enc_norm_grads,
-        grad_dec_embed,
-        dec_grads[0],
-        dec_grads[1],
-        dec_grads[2],
-        dec_grads[3],
-        grad_head,
-        jnp.concatenate([dec_norm_grads, grad_token[None]]),
-    ]
-    total = max(a for a, _ in ranges(share, n)) + slab_tiles(share, n)
-    pieces_ = []
-    for i, grad in enumerate(grads):
-        if i in SMALL:
-            lines = grad.reshape(-1, LANES)
-            pieces_.append(jnp.pad(lines, ((0, ENTRIES[i][4] * 8 - lines.shape[0]), (0, 0))))
-        else:
-            pieces_.append(matrix_tiles(grad))
-    pieces_.append(jnp.zeros(((total - TILES) * 8, LANES), jnp.float32))
-    slab_sum = reduce(jnp.concatenate(pieces_), share, n_dp, n_pair)
+    flat = encoder_back(flat, grad_entering, saved, enc_weights, parts[5], parts[6])
+    slab_sum = reduce(flat.reshape(-1, LANES), share, n_dp, n_pair)
     rows = share // LANES if share % LANES == 0 else (share + LANES - 1) // LANES + 1
     grad_share = own_flat(to_lines(slab_sum, rows, share, n_pair), share, index)
-    scalars = jnp.stack([jnp.sum(grad_share * grad_share), loss_local])
-    shared = share_all(jnp.zeros((8, LANES), jnp.float32).at[0, :2].set(scalars), n_dp, n_pair, 2)
+    scalars = jnp.stack([jnp.sum(grad_share * grad_share), loss_local[0, 0]])
+    shared = share_all(jnp.zeros((8, LANES), F32).at[0, :2].set(scalars), n_dp, n_pair, 2)
     squares, loss_sum = jnp.sum(shared[:, 0, 0]), jnp.sum(shared[:, 0, 1])
     grad_norm = jnp.sqrt(squares)
     loss = loss_sum / masked
     clipped = grad_share * (clip_limit[0] / (grad_norm + NORM_EPS))
     first = BETA_ONE * moment1 + (1.0 - BETA_ONE) * clipped
     second = BETA_TWO * moment2 + (1.0 - BETA_TWO) * clipped * clipped
-    steps_done = step_count[0].astype(jnp.float32)
+    steps_done = step_count[0].astype(F32)
     position = index * share + jnp.arange(share)
     rate = jnp.where(position < ENC_PARAMS, block_rates[0], block_rates[1])
-    update = (
-        first
-        / (1.0 - BETA_ONE**steps_done)
-        / (jnp.sqrt(second / (1.0 - BETA_TWO**steps_done)) + ADAM_EPS)
-    )
+    update = first / (1.0 - BETA_ONE**steps_done) / (jnp.sqrt(second / (1.0 - BETA_TWO**steps_done)) + ADAM_EPS)
     master_new = master - rate * (update + DECAY * master)
     return (loss.reshape(1), grad_norm.reshape(1), first, second, master_new)
 
 
 def solution(mesh):
-    in_specs = (
-        P(("dp", "pair"), None, None),
-        P(("dp", "pair"), None),
-        P(("dp", "pair")),
-        P(("dp", "pair")),
-        P(("dp", "pair")),
-        P(("dp", "pair")),
-        P(),
-        P(),
-        P(),
-    )
-    out_specs = (P(), P(), P(("dp", "pair")), P(("dp", "pair")), P(("dp", "pair")))
-    return jax.shard_map(functools.partial(body, mesh.shape["dp"], mesh.shape["pair"]), mesh=mesh, in_specs=in_specs, out_specs=out_specs, check_vma=False)
+    whole = P(("dp", "pair"))
+    in_specs = (P(("dp", "pair"), None, None), P(("dp", "pair"), None), whole, whole, whole, whole, P(), P(), P())
+    out_specs = (P(), P(), whole, whole, whole)
+    step = functools.partial(body, mesh.shape["dp"], mesh.shape["pair"])
+    return jax.shard_map(step, mesh=mesh, in_specs=in_specs, out_specs=out_specs, check_vma=False)

time: 649 us -> 530 us (0.82)
  Pallas kernels: 321 us -> 490 us
  matrix products: 126 us -> 0 us
  local copies, waits for them, and re-layouts: 112 us -> 15.2 us
  other arithmetic: 75.9 us -> 18.5 us
    pallas_call x0 -> x3, Pallas kernels: none -> 169 us  [the longest x1 83.2 us: decoder(): pl.pallas_call(functools.partial(decoder_kernel, images), name='decoder',...]
    dot_general x44 -> x0, matrix products: 126 us -> none  [the longest x11 27.3 us: outer(): jnp.einsum('bsi,bsj->ij', left, grad, preferred_element_type=jnp.float32)]
    unnamed x288 -> x29, local copies, waits for them, and re-layouts: 52.7 us -> 10.4 us
    convert_element_type x11 -> x2, other arithmetic: 38 us -> 0.6 us  [body(): held[i].reshape(-1)[:SHAPES[i][0] * SHAPES[i][1]].reshape(SHAPES[i])]
    gather x7 -> x0, local copies, waits for them, and re-layouts: 24.4 us -> none  [the longest x3 17.2 us: body(): jnp.take_along_axis(entering, jnp.minimum(rank, KEEP - 1)[:, :, None], ax...]
    convert_element_type x7 -> x1, local copies, waits for them, and re-layouts: 17.5 us -> 0.61 us  [body(): held[i].reshape(-1)[:SHAPES[i][0] * SHAPES[i][1]].reshape(SHAPES[i])]
    reduce_sum x16 -> x2, other arithmetic: 18.2 us -> 3.94 us  [the longest x1 2.46 us: body(): scalars = jnp.stack([jnp.sum(grad_share * grad_share), loss_local[0, 0]])]
where the time goes in v2:
time: 530 us
  Pallas kernels  490 us (92%)
  other arithmetic  18.5 us (3%)
  local copies, waits for them, and re-layouts  15.2 us (3%)
  between operations  6.49 us (1%)
    pallas_call x1, Pallas kernels, reduce(): pl.pallas_call(functools.partial(reduce_kernel, n_z, share), name='reduce...  154 us
    pallas_call x1, Pallas kernels, gather(): pl.pallas_call(functools.partial(gather_kernel, n_z), name='gather', out_...  137 us
    pallas_call x1, Pallas kernels, decoder(): pl.pallas_call(functools.partial(decoder_kernel, images), name='decoder',...  83.2 us
    pallas_call x1, Pallas kernels, encoder_back(): pl.pallas_call(functools.partial(encoder_back_kernel, images), name='enco...  51.6 us
    pallas_call x1, Pallas kernels, encoder(): pl.pallas_call(functools.partial(encoder_kernel, images), name='encoder',...  34.6 us
    pallas_call x1, Pallas kernels, assemble(): pl.pallas_call(functools.partial(assemble_kernel, share, n), name='assemb...  12.9 us

profile of v2, /device:TPU:0, one launch (start us, length us, event | category | flops | bytes accessed | tf_op | source)
XLA Modules:
  0.0 529.9 jit_solution(15882564308593361985)
XLA Ops:
  1.9 2.9 to_tiles.1.slab_ref
  4.8 136.7 %gather.1.slots_ref = bf16[32,386,8,128]{3,2,1,0:T(8,128)(2,1)} custom-call(bf16[386,8,128]{2,1,0:T(8,128)(2,1)} %to_tiles.1.slab_ref), custom_call_target="tpu_custom_call" | custom-call | tf_op jit(solution)/shard_map/gather/pallas_call | solution.py:149
  141.5 1.5 convert_reduce_fusion
  143.1 1.1 pad.21.clone
  147.2 1.5 multiply_sine_fusion.1
  148.7 1.1 select_maximum_fusion.pos_ref
  149.8 12.9 %assemble.1 = (bf16[576,8,128]{2,1,0:T(8,128)(2,1)S(1)}, bf16[1728,8,128]{2,1,0:T(8,128)(2,1)S(1)}, bf16[576,8,128]{2,1,0:T(8,128)(2,1)S(1)}, bf16[2304,8,128]{2...) custom-call(bf16[32,386,8,128]{3,2,1,0:T(8,128)(2,1)} %gather.1.slot, ...), custom_call_target="tpu_custom_call" | custom-call | tf_op jit(solution)/shard_map/assemble/pallas_call | solution.py:351
  162.7 1.8 copy-done
  164.5 1.0 copy-done.1
  166.4 1.4 copy-done.3
  167.8 1.3 copy-done.4
  169.1 1.1 copy-done.5
  170.3 1.0 copy-done.6
  171.3 0.9 copy-done.7
  173.6 34.6 %encoder.1 = (bf16[256,768]{1,0:T(8,128)(2,1)}, bf16[256,768]{1,0:T(8,128)(2,1)}, f32[256,768]{1,0:T(8,128)}, f32[256,1]{1,0:T(8,128)}, bf16[256,2304]{1,0:T(8,1...) custom-call(s32[4]{0:T(128)} %counts_ref.3, ...), custom_call_target="tpu_custom_call" | custom-call | tf_op jit(solution)/shard_map/encoder/pallas_call | solution.py:971
  208.8 83.2 %decoder.1 = (f32[11363,8,128]{2,1,0:T(8,128)}, bf16[256,512]{1,0:T(8,128)(2,1)}, f32[1,1]{1,0:T(1,128)}) custom-call(s32[4]{0:T(128)} %counts_ref.3, f32[1,1]{1,0:T(1,128)} %bitcast.2.masked_ref, bf16[832,768]{1,0:T(8,128)(2,1)} %bitcast.102, s32[4,64,1]{2,1,0:T(8,128)} %copy.17.cols_ref, s32[4,64]{1,0:T(4,128)} %get-tuple-element.100.rows_ref, ...), custom_call_target="tpu_custom_call" | custom-call | tf_op jit(solution)/shard_map/decoder/pallas_call | solution.py:1071
  292.0 51.6 %encoder_back.1 = f32[11363,8,128]{2,1,0:T(8,128)} custom-call(f32[11363,8,128]{2,1,0:T(8,128)} %get-tuple-element.76.flat_in, bf16[256,512]{1,0:T(8,128)(2,1)} %get-tuple-element.77.grad_entering, bf16[256,768]{1,0:T(8,128)(2,1)} %get-tuple-element.78.seen, bf16[256,768]{1,0:T(8,128)(2,1)} %get-tuple-element.79.entry, ...), custom_call_target="tpu_custom_call", output_to_operand_aliasing={{}: (0, {})} | custom-call | tf_op jit(solution)/shard_map/encoder_back/pallas_call | solution.py:1123
  343.6 154.4 %reduce_scatter.1 = (f32[3072,128]{1,0:T(8,128)}, f32[4,4,3072,128]{3,2,1,0:T(8,128)}) custom-call(f32[90904,128]{1,0:T(8,128)} %bitcast.96), custom_call_target="tpu_custom_call" | custom-call | tf_op jit(solution)/shard_map/reduce_scatter/pallas_call | solution.py:599
  498.0 3.2 to_lines.1
  501.2 2.5 multiply_reduce_fusion
  503.7 1.4 maximum_bitcast_fusion
  505.7 10.2 %share_all.1 = f32[32,8,128]{2,1,0:T(8,128)} custom-call(f32[8,128]{1,0:T(8,128)} %scatter.9.in_ref), custom_call_target="tpu_custom_call" | custom-call | tf_op jit(solution)/shard_map/share_all/pallas_call | solution.py:652
  515.9 1.7 slice_reduce_fusion
  521.7 6.0 %multiply_subtract_fusion = (f32[362752]{0:T(1024)}, f32[362752]{0:T(1024)}, f32[362752]{0:T(1024)}) fusion(f32[362752]{0:T(1024)S(1)} %copy-done.10, f32[]{:T(128)} %bitcast.50, f32[]{:T(128)} %bitcast.49, f32[]{:T(128)} %bitcast.48, f32[]{:T(128)} %bitcast.47, s32[]{:T(128)S(6)} %mul.148, f32[2834,128]{1,0:T(8,128)S(1)} %copy-done.9, f32[]{:T(128)S(6)} %div.67, ...), kind=kLoop, calls=%fused_computation.4 | loop fusion | flops 6892288 | bytes 10157080 | tf_op jit(solution)/shard_map/sub | solution.py:1204
  (37 shorter events, 8.5 us)
Async XLA Ops:
  4.8 138.2 %copy-start.11 = (bf16[4,196,768]{2,0,1:T(4,128)(2,1)S(1)}, bf16[4,196,768]{2,0,1:T(4,128)(2,1)}, u32[]{:S(2)}) copy-start(bf16[4,196,768]{2,0,1:T(4,128)(2,1)} %param.13) | copy-start | bytes 3612676
  143.1 1.1 copy-start.13
  162.7 1.8 copy-start
  164.5 1.0 copy-start.1
  165.5 0.9 copy-start.2
  166.4 1.4 copy-start.3
  167.8 1.3 copy-start.4
  169.1 1.2 copy-start.5
  170.2 1.0 copy-start.6
  171.3 0.9 copy-start.7
  172.2 0.8 copy-start.8
  498.0 23.6 %copy-start.10 = (f32[362752]{0:T(1024)S(1)}, f32[362752]{0:T(1024)}, u32[]{:S(2)}) copy-start(f32[362752]{0:T(1024)} %param.16) | copy-start | bytes 4353028
  501.2 19.1 %copy-start.12 = (f32[2]{0:T(128)S(1)}, f32[2]{0:T(128)}, u32[]{:S(2)}) copy-start(f32[2]{0:T(128)} %param.19) | copy-start | bytes 28
  501.2 20.4 %copy-start.9 = (f32[2834,128]{1,0:T(8,128)S(1)}, f32[2834,128]{1,0:T(8,128)}, u32[]{:S(2)}) copy-start(f32[2834,128]{1,0:T(8,128)} %to_lines.1) | copy-start | bytes 4353028

commit v3 on v2

--- a/solution.py
+++ b/solution.py
@@ -2,6 +2,7 @@
 
 import jax
 import jax.numpy as jnp
+import numpy as np
 from jax import lax
 from jax.experimental import pallas as pl
 from jax.experimental.pallas import tpu as pltpu
@@ -47,8 +48,15 @@
     pl.semaphore_wait(barrier, 3 + jnp.where(z < n_z - 1, 1, 0) + jnp.where(z > 0, 1, 0))
 
 
-def gather_kernel(n_z, slab_ref, out_ref, own_sem, send_sem, recv_sem):
-    half = slab_ref.shape[0] // 2
+def both(*conditions):
+    total = conditions[0]
+    for one in conditions[1:]:
+        total = jnp.logical_and(total, one)
+    return total
+
+
+def gather_kernel(n_z, chunks, slab_ref, out_ref, own_sem, z_sem, plane_sem, second_sem, third_sem, recv_sem):
+    piece = slab_ref.shape[0] // (2 * chunks)
     z, x, y, c = place()
     to = partners(z, x, y, c)
     me = slot_of(z, x, y, c)
@@ -56,107 +64,119 @@
     local.start()
     greet(n_z, z, to)
     local.wait()
-    pending = []
-
-    def copy(slot, part, name, index):
-        rows = pl.ds(part * half, half)
+    steps = n_z * chunks
+
+    def copy(slot, chunk, part, name, sem):
+        rows = pl.ds((chunk * 2 + part) * piece, piece)
         return pltpu.make_async_remote_copy(
             out_ref.at[slot, rows],
             out_ref.at[slot, rows],
-            send_sem.at[index],
-            recv_sem.at[slot, part],
+            sem,
+            recv_sem.at[slot, chunk, part],
             device_id=to[name],
             device_id_type=MESH,
         )
 
-    def send(slot, part, name, where):
-        index = len(pending)
-        pending.append((slot, part, name, index, where))
-        if where is None:
-            copy(slot, part, name, index).start()
-        else:
-            pl.when(where)(lambda: copy(slot, part, name, index).start())
-
-    def arrived(slot, part, where):
-        if where is None:
-            copy(slot, part, "c", 0).wait_recv()
-        else:
-            pl.when(where)(lambda: copy(slot, part, "c", 0).wait_recv())
-
-    def both(one, two):
-        return two if one is None else jnp.logical_and(one, two)
-
-    levels = [[(z, None, None)]]
-    for t in range(1, n_z):
-        levels.append([(z - t, z >= t, "up"), (z + t, z + t < n_z, "down")])
-
-    def first(level):
-        for zz, where, onward in level:
-            slot = slot_of(zz, x, y, c)
-            for part in (0, 1):
-                if onward is None:
-                    send(slot, part, "up", z < n_z - 1)
-                    send(slot, part, "down", z > 0)
-                else:
-                    arrived(slot, part, where)
-                    more = z < n_z - 1 if onward == "up" else z > 0
-                    send(slot, part, onward, both(where, more))
-            for part in (0, 1):
-                send(slot, part, ("x", "y")[part], where)
-            for part in (0, 1):
-                send(slot, part, ("y", "x")[part], where)
-            for part in (0, 1):
-                send(slot, part, "c", where)
-
-    def second(level):
-        for zz, where, _ in level:
-            for part, slot in ((0, slot_of(zz, 1 - x, y, c)), (1, slot_of(zz, x, 1 - y, c))):
-                arrived(slot, part, where)
-                send(slot, part, ("y", "x")[part], where)
-                send(slot, part, "c", where)
-
-    def third(level):
-        for zz, where, _ in level:
-            for part, ox, oy in ((0, x, 1 - y), (1, 1 - x, y), (0, 1 - x, 1 - y), (1, 1 - x, 1 - y)):
-                slot = slot_of(zz, ox, oy, c)
-                arrived(slot, part, where)
-                send(slot, part, "c", where)
-
-    for t in range(n_z + 2):
-        if t < n_z:
-            first(levels[t])
-        if 1 <= t < n_z + 1:
-            second(levels[t - 1])
-        if t >= 2:
-            third(levels[t - 2])
-    for level in levels:
-        for zz, where, _ in level:
-            for ox in (0, 1):
-                for oy in (0, 1):
-                    for part in (0, 1):
-                        arrived(slot_of(zz, ox, oy, 1 - c), part, where)
-    for slot, part, name, index, where in pending:
-        if where is None:
-            copy(slot, part, name, index).wait_send()
-        else:
-            pl.when(where)(lambda s=slot, p=part, n=name, i=index: copy(s, p, n, i).wait_send())
-
-
-def gather(slab, n_dp, n_pair):
+    def arrived(slot, chunk, part):
+        copy(slot, chunk, part, "c", own_sem).wait_recv()
+
+    def lines(s):
+        t, chunk = s // chunks, lax.rem(s, chunks)
+        for d in (0, 1):
+            zz = z - t if d == 0 else z + t
+            inside = zz >= 0 if d == 0 else zz < n_z
+            more = z < n_z - 1 if d == 0 else z > 0
+            fresh = both(t > 0, inside)
+            held = jnp.logical_or(fresh, t == 0) if d == 0 else fresh
+            onward = both(jnp.logical_or(fresh, t == 0), more)
+            yield d, zz, chunk, fresh, held, onward
+
+    def first_sends(d, zz, chunk, held, onward, s, act):
+        slot = slot_of(zz, x, y, c)
+        for part in (0, 1):
+            pl.when(onward)(lambda part=part: act(copy(slot, chunk, part, ("up", "down")[d], z_sem.at[s, d, part])))
+
+        @pl.when(held)
+        def _():
+            for i, (part, name) in enumerate(((0, "x"), (1, "y"), (0, "y"), (1, "x"), (0, "c"), (1, "c"))):
+                act(copy(slot, chunk, part, name, plane_sem.at[s, d, i]))
+
+    def first(s):
+        for d, zz, chunk, fresh, held, onward in lines(s):
+
+            @pl.when(fresh)
+            def _():
+                for part in (0, 1):
+                    arrived(slot_of(zz, x, y, c), chunk, part)
+
+            first_sends(d, zz, chunk, held, onward, s, lambda one: one.start())
+
+    def second_items(zz):
+        return ((0, slot_of(zz, 1 - x, y, c), "y"), (1, slot_of(zz, x, 1 - y, c), "x"))
+
+    def second(s):
+        for d, zz, chunk, _, held, _ in lines(s):
+
+            @pl.when(held)
+            def _():
+                for part, slot, name in second_items(zz):
+                    arrived(slot, chunk, part)
+                    copy(slot, chunk, part, name, second_sem.at[s, d, part, 0]).start()
+                    copy(slot, chunk, part, "c", second_sem.at[s, d, part, 1]).start()
+
+    def third_items(zz):
+        return ((0, slot_of(zz, x, 1 - y, c)), (1, slot_of(zz, 1 - x, y, c)), (0, slot_of(zz, 1 - x, 1 - y, c)), (1, slot_of(zz, 1 - x, 1 - y, c)))
+
+    def third(s):
+        for d, zz, chunk, _, held, _ in lines(s):
+
+            @pl.when(held)
+            def _():
+                for i, (part, slot) in enumerate(third_items(zz)):
+                    arrived(slot, chunk, part)
+                    copy(slot, chunk, part, "c", third_sem.at[s, d, i]).start()
+
+    def turn(s, _):
+        pl.when(s < steps)(lambda: first(s))
+        pl.when(both(s >= 1, s < steps + 1))(lambda: second(s - 1))
+        pl.when(s >= 2)(lambda: third(s - 2))
+        return 0
+
+    lax.fori_loop(0, steps + 2, turn, 0)
+
+    def finish(s, _):
+        for d, zz, chunk, _, held, onward in lines(s):
+            first_sends(d, zz, chunk, held, onward, s, lambda one: one.wait_send())
+
+            @pl.when(held)
+            def _():
+                for part, slot, name in second_items(zz):
+                    copy(slot, chunk, part, name, second_sem.at[s, d, part, 0]).wait_send()
+                    copy(slot, chunk, part, "c", second_sem.at[s, d, part, 1]).wait_send()
+                for i, (part, slot) in enumerate(third_items(zz)):
+                    copy(slot, chunk, part, "c", third_sem.at[s, d, i]).wait_send()
+                for ox in (0, 1):
+                    for oy in (0, 1):
+                        for part in (0, 1):
+                            arrived(slot_of(zz, ox, oy, 1 - c), chunk, part)
+
+        return 0
+
+    lax.fori_loop(0, steps, finish, 0)
+
+
+def gather(slab, n_dp, n_pair, chunks):
     n_z = n_dp // 2
     n = n_dp * n_pair
-    sends = (2 * n_z - 1) * 16 + 8
+    steps = n_z * chunks
+    dma = pltpu.SemaphoreType.DMA
     return pl.pallas_call(
-        functools.partial(gather_kernel, n_z),
+        functools.partial(gather_kernel, n_z, chunks),
         name="gather",
         out_shape=jax.ShapeDtypeStruct((n,) + slab.shape, slab.dtype),
-        in_specs=[pl.BlockSpec(memory_space=pl.ANY)],
+        in_specs=[pl.BlockSpec(memory_space=pltpu.VMEM)],
         out_specs=pl.BlockSpec(memory_space=pl.ANY),
-        scratch_shapes=[
-            pltpu.SemaphoreType.DMA,
-            pltpu.SemaphoreType.DMA((sends,)),
-            pltpu.SemaphoreType.DMA((n, 2)),
-        ],
+        scratch_shapes=[dma, dma((steps, 2, 2)), dma((steps, 2, 6)), dma((steps, 2, 2, 2)), dma((steps, 2, 4)), dma((n, chunks, 2))],
         compiler_params=pltpu.CompilerParams(collective_id=0, has_side_effects=True),
     )(slab)
 
@@ -362,7 +382,7 @@
             dma((len(seams),)),
             dma((len(ENTRIES),)),
         ],
-        compiler_params=pltpu.CompilerParams(vmem_limit_bytes=40 * MB),
+        compiler_params=pltpu.CompilerParams(vmem_limit_bytes=60 * MB),
     )(slots)
 
 
@@ -378,11 +398,12 @@
     return value.reshape(rows // 8, 8, cols, LANES).transpose(0, 2, 1, 3).reshape(rows * cols, LANES)
 
 
-def reduce_kernel(n_z, share, grad_ref, out_ref, sib_ref, gbuf, rbuf, keep, q1s, q1r, q2s, q2r, zs, zr, t1s, t1r, t2s, t2r, tzs, tzr, sib_sem, load_sem, s1_sem, s2_sem, z_sem):
+def reduce_kernel(n_z, chunks, share, grad_ref, out_ref, sib_ref, gbuf, rbuf, keep, q1s, q1r, q2s, q2r, zs, zr, t1s, t1r, t2s, t2r, tzs, tzr, sib_sem, load_sem, s1_sem, s2_sem, z_sem):
     z, x, y, c = place()
     to = partners(z, x, y, c)
-    rows = out_ref.shape[0]
+    rows = out_ref.shape[0] // chunks
     half = rows // 2
+    steps = n_z * chunks
     count = half // BLOCK
 
     def start_of(k):
@@ -394,21 +415,26 @@
         moved = jnp.where(low, jnp.where(far > z, far, far - 1), jnp.where(far < z, far, far + 1))
         return jnp.where(j == n_z - 1, z, moved)
 
-    def sibling(j, xx, yy, core):
-        k = slot_of(order(j), xx, yy, core)
+    def lines_of(s, xx, yy, core):
+        k = slot_of(order(s // chunks), xx, yy, core)
+        return pl.ds(pl.multiple_of(start_of(k) + lax.rem(s, chunks) * rows, 8), rows)
+
+    def kept(s, part, b):
+        return s // chunks, pl.ds(pl.multiple_of(lax.rem(s, chunks) * rows + part * half + b * BLOCK, BLOCK), BLOCK)
+
+    def sibling(s, xx, yy, core):
         return pltpu.make_async_remote_copy(
-            grad_ref.at[pl.ds(start_of(k), rows)],
-            sib_ref.at[j, xx * 2 + yy],
-            sib_sem.at[0, j, xx * 2 + yy],
-            sib_sem.at[1, j, xx * 2 + yy],
+            grad_ref.at[lines_of(s, xx, yy, core)],
+            sib_ref.at[s, xx * 2 + yy],
+            sib_sem.at[0, s, xx * 2 + yy],
+            sib_sem.at[1, s, xx * 2 + yy],
             device_id=to["c"],
             device_id_type=MESH,
         )
 
     def loads(j, s, q):
-        k = slot_of(order(j), q // 2, q % 2, c)
         return (
-            pltpu.make_async_copy(grad_ref.at[pl.ds(start_of(k), rows)], gbuf.at[s, q], load_sem.at[0, s, q]),
+            pltpu.make_async_copy(grad_ref.at[lines_of(j, q // 2, q % 2, c)], gbuf.at[s, q], load_sem.at[0, s, q]),
             pltpu.make_async_copy(sib_ref.at[j, q], rbuf.at[s, q], load_sem.at[1, s, q]),
         )
 
@@ -492,15 +518,15 @@
             k = part * 2 + here
 
             def store(b, part=part, k=k):
-                at = pl.ds(pl.multiple_of(part * half + b * BLOCK, BLOCK), BLOCK)
-                keep[j, at, :] = own(s, mine, part, b) + unpack(q1r.at[j, k], t1r.at[j, k], b)
+                group, at = kept(j, part, b)
+                keep[group, at, :] = own(s, mine, part, b) + unpack(q1r.at[j, k], t1r.at[j, k], b)
 
             each(store)
 
     def add_to_keep(j, part, q_ref, t_ref):
         def body(b):
-            at = pl.ds(pl.multiple_of(part * half + b * BLOCK, BLOCK), BLOCK)
-            keep[j, at, :] += unpack(q_ref, t_ref, b)
+            group, at = kept(j, part, b)
+            keep[group, at, :] += unpack(q_ref, t_ref, b)
 
         each(body)
 
@@ -512,28 +538,29 @@
 
     def pass_on(j, zz, part, name):
         def body(b):
-            at = pl.ds(pl.multiple_of(part * half + b * BLOCK, BLOCK), BLOCK)
-            pack(keep[j, at, :], zs.at[zz, part], tzs.at[zz, part], b)
+            group, at = kept(j, part, b)
+            pack(keep[group, at, :], zs.at[zz, part], tzs.at[zz, part], b)
 
         each(body)
         for one in z_message(zz, part, name):
             one.start()
 
     def stage_four(j):
-        zz = order(j)
+        zz = order(j // chunks)
+        zc = zz * chunks + lax.rem(j, chunks)
         for part in (0, 1):
             for d, name, has, onward in ((0, "up", z > 0, zz > z), (1, "down", z < n_z - 1, zz < z)):
                 back = zz >= z if d == 0 else zz <= z
 
                 @pl.when(jnp.logical_and(has, back))
                 def _():
-                    for one in z_message(zz, part, name):
+                    for one in z_message(zc, part, name):
                         one.wait_recv()
-                    add_to_keep(j, part, zr.at[d, zz, part], tzr.at[d, zz, part])
+                    add_to_keep(j, part, zr.at[d, zc, part], tzr.at[d, zc, part])
 
                 @pl.when(onward)
                 def _():
-                    pass_on(j, zz, part, name)
+                    pass_on(j, zc, part, name)
 
     greet(n_z, z, to)
 
@@ -542,22 +569,23 @@
             sibling(j, q // 2, q % 2, 1 - c).start()
         return 0
 
-    lax.fori_loop(0, n_z, begin, 0)
+    lax.fori_loop(0, steps, begin, 0)
     load(0)
 
     def turn(t, _):
-        pl.when(t < n_z)(lambda: stage_one(t))
-        pl.when(jnp.logical_and(t >= 1, t <= n_z))(lambda: stage_two(t - 1))
-        pl.when(t + 1 < n_z)(lambda: load(t + 1))
-        pl.when(jnp.logical_and(t >= 2, t <= n_z + 1))(lambda: stage_three(t - 2))
+        pl.when(t < steps)(lambda: stage_one(t))
+        pl.when(jnp.logical_and(t >= 1, t <= steps))(lambda: stage_two(t - 1))
+        pl.when(t + 1 < steps)(lambda: load(t + 1))
+        pl.when(jnp.logical_and(t >= 2, t <= steps + 1))(lambda: stage_three(t - 2))
         pl.when(t >= 3)(lambda: stage_four(t - 3))
         return 0
 
-    lax.fori_loop(0, n_z + 3, turn, 0)
+    lax.fori_loop(0, steps + 3, turn, 0)
     out_ref[...] = keep[n_z - 1]
 
     def finish(j, _):
-        zz = order(j)
+        zz = order(j // chunks)
+        zc = zz * chunks + lax.rem(j, chunks)
         for q in range(4):
             sibling(j, q // 2, q % 2, 1 - c).wait_send()
         for part in (0, 1):
@@ -569,23 +597,31 @@
 
             @pl.when(zz > z)
             def _():
-                for one in z_message(zz, part, "up"):
+                for one in z_message(zc, part, "up"):
                     one.wait_send()
 
             @pl.when(zz < z)
             def _():
-                for one in z_message(zz, part, "down"):
+                for one in z_message(zc, part, "down"):
                     one.wait_send()
 
         return 0
 
-    lax.fori_loop(0, n_z, finish, 0)
+    lax.fori_loop(0, steps, finish, 0)
+
+
+def reduce_chunks(share, n):
+    rows = slab_tiles(share, n) * 8
+    return max(d for d in (1, 2, 4) if rows % (2 * BLOCK * d) == 0)
 
 
 def reduce(flat, share, n_dp, n_pair):
+    chunks = reduce_chunks(share, n_dp * n_pair)
     n_z, n = n_dp // 2, n_dp * n_pair
     rows = slab_tiles(share, n) * 8
-    half = rows // 2
+    part = rows // chunks
+    half = part // 2
+    steps = n_z * chunks
     marks = (half // BLOCK + 7) // 8 * 8
     anyspec = pl.BlockSpec(memory_space=pl.ANY)
 
@@ -597,18 +633,18 @@
 
     dma = pltpu.SemaphoreType.DMA
     return pl.pallas_call(
-        functools.partial(reduce_kernel, n_z, share),
+        functools.partial(reduce_kernel, n_z, chunks, share),
         name="reduce_scatter",
-        out_shape=[jax.ShapeDtypeStruct((rows, LANES), jnp.float32), jax.ShapeDtypeStruct((n_z, 4, rows, LANES), jnp.float32)],
+        out_shape=[jax.ShapeDtypeStruct((rows, LANES), jnp.float32), jax.ShapeDtypeStruct((steps, 4, part, LANES), jnp.float32)],
         in_specs=[anyspec],
         out_specs=[pl.BlockSpec(memory_space=pltpu.VMEM), anyspec],
         scratch_shapes=[
-            pltpu.VMEM((2, 4, rows, LANES), jnp.float32),
-            pltpu.VMEM((2, 4, rows, LANES), jnp.float32),
+            pltpu.VMEM((2, 4, part, LANES), jnp.float32),
+            pltpu.VMEM((2, 4, part, LANES), jnp.float32),
             pltpu.VMEM((n_z, rows, LANES), jnp.float32),
-            q(n_z, 4), q(n_z, 4), q(n_z, 2), q(n_z, 2), q(n_z, 2), q(2, n_z, 2),
-            t(n_z, 4), t(n_z, 4), t(n_z, 2), t(n_z, 2), t(n_z, 2), t(2, n_z, 2),
-            dma((2, n_z, 4)), dma((2, 2, 4)), dma((n_z, 4, 2, 2)), dma((n_z, 2, 2, 2)), dma((2, n_z, 2, 2, 2)),
+            q(steps, 4), q(steps, 4), q(steps, 2), q(steps, 2), q(steps, 2), q(2, steps, 2),
+            t(steps, 4), t(steps, 4), t(steps, 2), t(steps, 2), t(steps, 2), t(2, steps, 2),
+            dma((2, steps, 4)), dma((2, 2, 4)), dma((steps, 4, 2, 2)), dma((steps, 2, 2, 2)), dma((2, steps, 2, 2, 2)),
         ],
         compiler_params=pltpu.CompilerParams(collective_id=1, has_side_effects=True, vmem_limit_bytes=60 * MB),
     )(flat)[0]
@@ -718,14 +754,73 @@
     return top, mid, (rest - mid.astype(F32)).astype(BF)
 
 
-def block_forward(x, rows, images, length, heads, weights, norms, key_bias, saved):
-    triple_w, proj_w, up_w, down_w = weights
+class Moves:
+    def __init__(self, names, sources, targets, sems):
+        self.targets = dict(zip(names, targets))
+        self.copies = {name: pltpu.make_async_copy(a, b, sems.at[i]) for i, (name, a, b) in enumerate(zip(names, sources, targets))}
+        self.open = []
+
+    def start(self, *names):
+        for name in names or self.copies:
+            self.copies[name].start()
+            self.open.append(name)
+
+    def __call__(self, name):
+        if name in self.open:
+            self.copies[name].wait()
+            self.open.remove(name)
+        return self.targets[name]
+
+    def close(self):
+        for name in list(self.open):
+            self(name)
+
+
+def wide_attention(width, heads, rows, triple, bias, probs, mixed):
+    size = width // heads
+    per = LANES // size
+    masks = head_masks(size)
+    for g in range(width // LANES):
+        q, k, v = (triple[:, t * width + g * LANES : t * width + (g + 1) * LANES] for t in range(3))
+        v_side = v.T
+        parts = []
+        for h in range(per):
+            s = dot_nt(k * masks[h], q) * size ** (-0.5) + bias[...]
+            e = jnp.exp(s - jnp.max(s, axis=0, keepdims=True))
+            p = e * (1.0 / jnp.sum(e, axis=0, keepdims=True))
+            probs[g * per + h] = p
+            parts.append(dot_nn(v_side[h * size : (h + 1) * size, :], p.astype(BF)))
+        mixed[:, g * LANES : (g + 1) * LANES] = jnp.concatenate(parts, axis=0).T.astype(BF)
+
+
+def wide_attention_back(width, heads, triple, probs, low_mixed, grad_triple):
+    size = width // heads
+    per = LANES // size
+    masks = head_masks(size)
+    for g in range(width // LANES):
+        lanes = [slice(t * width + g * LANES, t * width + (g + 1) * LANES) for t in range(3)]
+        q, k, v = (triple[:, lane] for lane in lanes)
+        dm = low_mixed[:, g * LANES : (g + 1) * LANES]
+        k_side = k.T
+        parts, dk, dv = [], 0.0, 0.0
+        for h in range(per):
+            p = probs[g * per + h]
+            dp = dot_nt(v * masks[h], dm)
+            ds = (p * (dp - jnp.sum(p * dp, axis=0, keepdims=True))).astype(BF)
+            dv = dv + dot_nn(p.astype(BF), dm * masks[h])
+            dk = dk + dot_nn(ds, q * masks[h])
+            parts.append(dot_nn(k_side[h * size : (h + 1) * size, :], ds))
+        grad_triple[:, lanes[0]] = (jnp.concatenate(parts, axis=0).T * size ** (-0.5)).astype(BF)
+        grad_triple[:, lanes[1]] = (dk * size ** (-0.5)).astype(BF)
+        grad_triple[:, lanes[2]] = dv.astype(BF)
+
+
+def block_forward(x, rows, images, heads, need, norms, key_bias, saved, done=lambda *names: None):
     entry, plain1, scale1, triple, probs, mixed, plain2, scale2, inner, act, slope = saved
     width = x.shape[1]
     size = width // heads
     per = LANES // size
     groups = width // LANES
-    hidden = up_w.shape[1]
 
     def first(i):
         at = rows_at(i, rows)
@@ -736,11 +831,15 @@
 
     loop(images, first)
 
+    done("entry", "plain1", "scale1")
+    triple_w = need("triple_w")
+
     def project(j):
         at = rows_at(j, 256)
         triple[:, at] = dot_nn(entry[...], triple_w[:, at]).astype(BF)
 
     loop(3 * width // 256, project)
+    done("triple")
     masks = head_masks(size)
 
     def attend(i):
@@ -760,7 +859,12 @@
                 parts.append(dot_nn(v_side[h * size : (h + 1) * size, :], p.astype(BF)))
             mixed[at, g * LANES : (g + 1) * LANES] = jnp.concatenate(parts, axis=0).T.astype(BF)
 
-    loop(images, attend)
+    if callable(key_bias):
+        loop(images, attend)
+    else:
+        wide_attention(width, heads, rows, triple, key_bias, probs, mixed)
+    done("probs", "mixed")
+    proj_w = need("proj_w")
 
     def middle(j):
         at = rows_at(j, 256)
@@ -776,6 +880,9 @@
         inner[at, :] = (plain * norms[2:3, :] + norms[3:4, :]).astype(BF)
 
     loop(images, second)
+    done("plain2", "scale2", "inner")
+    up_w = need("up_w")
+    hidden = up_w.shape[1]
 
     def up(j):
         at = rows_at(j, 256)
@@ -784,6 +891,8 @@
         slope[:, at] = gradient
 
     loop(hidden // 256, up)
+    done("act", "slope")
+    down_w = need("down_w")
 
     def down(j):
         at = rows_at(j, 256)
@@ -795,12 +904,18 @@
 class Writer:
     def __init__(self, flat, stage, sem):
         self.flat, self.stage, self.sem = flat, stage, sem
+        self.pending = {}
+
+    def settle(self, s):
+        if s in self.pending:
+            self.pending.pop(s).wait()
 
     def outer(self, number, left, right, chunk=256):
         _, _, cols, tile, _ = ENTRIES[number]
         rows = left.shape[1]
         count = rows // chunk
         tall = chunk // 8
+        before = dict(self.pending)
 
         def copy(i, s):
             return pltpu.make_async_copy(
@@ -809,6 +924,8 @@
 
         def body(i):
             s = lax.rem(i, 2)
+            for early in before:
+                pl.when(i == early)(before[early].wait)
 
             @pl.when(i >= 2)
             def _():
@@ -822,34 +939,48 @@
             copy(i, s).start()
 
         loop(count, body)
-        for i in range(max(0, count - 2), count):
-            copy(i, i % 2).wait()
-
-
-def block_backward(grad, rows, images, length, heads, weights, norms, norm_sums, saved, extra, writer, numbers):
-    triple_w, proj_w, up_w, down_w = weights
-    entry, plain1, scale1, triple, probs, mixed, plain2, scale2, inner, act, slope = saved
+        self.pending = {(count - 2) % 2: copy(count - 2, (count - 2) % 2), (count - 1) % 2: copy(count - 1, (count - 1) % 2)}
+
+    def small(self, number, norm_sums, count, extra=0):
+        _, _, _, tile, groups = ENTRIES[number]
+        per = SHAPES[number][1] // LANES
+        self.settle(0)
+        self.stage[0, 0 : groups + extra] = jnp.zeros((groups + extra, 8, LANES), F32)
+        for r in range(count):
+            for c in range(per):
+                line = r * per + c
+                self.stage[0, line // 8, line % 8 : line % 8 + 1, :] = norm_sums[r : r + 1, c * LANES : (c + 1) * LANES]
+        copy = pltpu.make_async_copy(self.stage.at[0, pl.ds(0, groups + extra)], self.flat.at[pl.ds(tile, groups + extra)], self.sem.at[0])
+        copy.start()
+        copy.wait()
+        self.settle(1)
+
+
+def block_backward(grad, rows, images, heads, need, norms, norm_sums, extra, writer, numbers):
     low, grad_hidden, side, low_mixed, grad_triple = extra
     width = grad.shape[1]
     size = width // heads
     per = LANES // size
     groups = width // LANES
-    hidden = up_w.shape[1]
     low[...] = grad[...].astype(BF)
+    down_w, slope = need("down_w"), need("slope")
+    hidden = down_w.shape[0]
 
     def back_up(j):
         at = rows_at(j, 256)
         grad_hidden[:, at] = (dot_nt(low[...], down_w[at, :]) * slope[:, at]).astype(BF)
 
     loop(hidden // 256, back_up)
-    writer.outer(numbers[3], act, low)
-    writer.outer(numbers[2], inner, grad_hidden)
+    writer.outer(numbers[3], need("act"), low)
+    writer.outer(numbers[2], need("inner"), grad_hidden)
+    up_w = need("up_w")
 
     def back_inner(j):
         at = rows_at(j, 256)
         side[:, at] = dot_nt(grad_hidden[...], up_w[at, :])
 
     loop(width // 256, back_inner)
+    plain2, scale2 = need("plain2"), need("scale2")
 
     def second(i):
         at = rows_at(i, rows)
@@ -861,13 +992,15 @@
         low[at, :] = total.astype(BF)
 
     loop(images, second)
-    writer.outer(numbers[1], mixed, low)
+    writer.outer(numbers[1], need("mixed"), low)
+    proj_w = need("proj_w")
 
     def back_mixed(j):
         at = rows_at(j, 256)
         low_mixed[:, at] = dot_nt(low[...], proj_w[at, :]).astype(BF)
 
     loop(width // 256, back_mixed)
+    triple, probs = need("triple"), need("probs")
     masks = head_masks(size)
 
     def attend(i):
@@ -890,14 +1023,19 @@
             grad_triple[at, lanes[1]] = (dk * size ** (-0.5)).astype(BF)
             grad_triple[at, lanes[2]] = dv.astype(BF)
 
-    loop(images, attend)
-    writer.outer(numbers[0], entry, grad_triple)
+    if probs.shape[1] == probs.shape[2] and probs.shape[0] == heads:
+        wide_attention_back(width, heads, triple, probs, low_mixed, grad_triple)
+    else:
+        loop(images, attend)
+    writer.outer(numbers[0], need("entry"), grad_triple)
+    triple_w = need("triple_w")
 
     def back_entry(j):
         at = rows_at(j, 256)
         side[:, at] = dot_nt(grad_triple[...], triple_w[at, :])
 
     loop(width // 256, back_entry)
+    plain1, scale1 = need("plain1"), need("scale1")
 
     def first(i):
         at = rows_at(i, rows)
@@ -909,45 +1047,70 @@
     loop(images, first)
 
 
-def write_small(number, norm_sums, count, flat, stage, sem):
-    _, lines, _, tile, groups = ENTRIES[number]
-    per = SHAPES[number][1] // LANES
-    stage[0, 0:groups] = jnp.zeros((groups, 8, LANES), F32)
-    for r in range(count):
-        for c in range(per):
-            line = r * per + c
-            stage[0, line // 8, line % 8 : line % 8 + 1, :] = norm_sums[r : r + 1, c * LANES : (c + 1) * LANES]
-    copy = pltpu.make_async_copy(stage.at[0, pl.ds(0, groups)], flat.at[pl.ds(tile, groups)], sem.at[0])
-    copy.start()
-    copy.wait()
-
-
-def encoder_kernel(images, counts_ref, patches_ref, cols_ref, pos_ref, embed_ref, triple_ref, proj_ref, up_ref, down_ref, norms_ref, dec_embed_ref,
-                   seen, entry, plain1, scale1, triple, probs, mixed, plain2, scale2, inner, act, slope, plain3, scale3, encoded, entering, x, place, pos_split):
+SAVED = ("seen", "entry", "plain1", "scale1", "triple", "probs", "mixed", "plain2", "scale2", "inner", "act", "slope", "plain3", "scale3", "encoded")
+ENC_NAMES = ("embed_w", "triple_w", "proj_w", "up_w", "down_w", "dec_embed_w")
+DEC_NAMES = ("triple_w", "proj_w", "up_w", "down_w", "head_w")
+
+
+def saved_shapes(rows):
+    s = jax.ShapeDtypeStruct
+    return [
+        s((rows, D), BF), s((rows, D), BF), s((rows, D), F32), s((rows, 1), F32), s((rows, 3 * D), BF),
+        s((HEADS, rows, rows), F32), s((rows, D), BF), s((rows, D), F32), s((rows, 1), F32), s((rows, D), BF),
+        s((rows, F), BF), s((rows, F), F32), s((rows, D), F32), s((rows, 1), F32), s((rows, D), BF),
+    ]
+
+
+def like(shape):
+    return pltpu.VMEM(shape.shape, shape.dtype)
+
+
+def pad_patches(patches, padded, images):
+    padded[...] = jnp.zeros_like(padded)
+    for i in range(images):
+        padded[i * P_ROWS : i * P_ROWS + PATCHES, :] = patches[i]
+
+
+def encoder_kernel(images, counts_ref, cols_ref, norms_ref, *refs):
+    pos_hbm, patches_hbm, *weights_hbm = refs[:8]
+    outs = refs[8:23]
+    entering = refs[23]
+    pos, patches, *weights = refs[24:32]
+    saved = dict(zip(SAVED, refs[32:47]))
+    x, place_, pos_split, padded, bias, in_sem, out_sem = refs[47:]
+    need = Moves(("pos", "patches") + ENC_NAMES, [pos_hbm, patches_hbm] + weights_hbm, [pos, patches] + weights, in_sem)
+    need.start()
+    put = Moves(SAVED, [saved[name] for name in SAVED], outs, out_sem)
+    rows = images * KEEP
+    key = lax.broadcasted_iota(jnp.int32, (KEEP, rows), 0)
+    query = lax.broadcasted_iota(jnp.int32, (KEEP, rows), 1)
+    for i in range(images):
+        inside = jnp.logical_and(jnp.logical_and(query >= i * KEEP, query < (i + 1) * KEEP), key < counts_ref[i])
+        bias[i * KEEP : (i + 1) * KEEP, :] = jnp.where(inside, 0.0, NEG_FILL)
+    need("pos")
+    for t, part in enumerate(three(pos[...])):
+        pos_split[t] = part
+    pad_patches(need("patches"), padded, images)
     spots = lax.broadcasted_iota(jnp.int32, (KEEP, P_ROWS), 1)
-    for t, part in enumerate(three(pos_ref[...])):
-        pos_split[t] = part
+    seen = saved["seen"]
 
     def select(i):
         at = rows_at(i, KEEP)
         pick = jnp.where(spots == cols_ref[i], 1.0, 0.0).astype(BF)
-        seen[at, :] = dot_nn(pick, patches_ref[rows_at(i, P_ROWS), :]).astype(BF)
-        place[at, :] = dot_nn(pick, pos_split[0]) + dot_nn(pick, pos_split[1]) + dot_nn(pick, pos_split[2])
+        seen[at, :] = dot_nn(pick, padded[rows_at(i, P_ROWS), :]).astype(BF)
+        place_[at, :] = dot_nn(pick, pos_split[0]) + dot_nn(pick, pos_split[1]) + dot_nn(pick, pos_split[2])
 
     loop(images, select)
+    put.start("seen")
+    embed_w = need("embed_w")
 
     def embed(j):
         at = rows_at(j, 256)
-        x[:, at] = dot_nn(seen[...], embed_ref[:, at]) + place[:, at]
+        x[:, at] = dot_nn(seen[...], embed_w[:, at]) + place_[:, at]
 
     loop(D // 256, embed)
-    slot = lax.broadcasted_iota(jnp.int32, (KEEP, 1), 0)
-
-    def key_bias(i):
-        return jnp.where(slot < counts_ref[i], 0.0, NEG_FILL)
-
-    block_forward(x, KEEP, images, KEEP, HEADS, (triple_ref, proj_ref, up_ref, down_ref), norms_ref, key_bias,
-                  (entry, plain1, scale1, triple, probs, mixed, plain2, scale2, inner, act, slope))
+    block_forward(x, KEEP, images, HEADS, need, norms_ref, bias, [saved[name] for name in SAVED[1:12]], put.start)
+    plain3, scale3, encoded = (saved[name] for name in SAVED[12:])
 
     def last(i):
         at = rows_at(i, KEEP)
@@ -957,39 +1120,46 @@
         encoded[at, :] = (plain * norms_ref[4:5, :] + norms_ref[5:6, :]).astype(BF)
 
     loop(images, last)
-    entering[...] = dot_nn(encoded[...], dec_embed_ref[...])
-
-
-def encoder(counts, patches, cols, pos, weights, norms, dec_embed):
+    put.start("plain3", "scale3", "encoded")
+    entering[...] = dot_nn(encoded[...], need("dec_embed_w")[...])
+    put.close()
+
+
+def encoder(counts, patches, cols, pos, weights, norms):
     images = counts.shape[0]
     rows = images * KEEP
     vmem = pl.BlockSpec(memory_space=pltpu.VMEM)
-
-    def s(shape, kind):
-        return jax.ShapeDtypeStruct(shape, kind)
-
+    anyspec = pl.BlockSpec(memory_space=pl.ANY)
+    shapes = saved_shapes(rows)
     return pl.pallas_call(
         functools.partial(encoder_kernel, images),
         name="encoder",
-        out_shape=[
-            s((rows, D), BF), s((rows, D), BF), s((rows, D), F32), s((rows, 1), F32), s((rows, 3 * D), BF),
-            s((images * D // LANES, LANES, KEEP), F32), s((rows, D), BF), s((rows, D), F32), s((rows, 1), F32), s((rows, D), BF),
-            s((rows, F), BF), s((rows, F), F32), s((rows, D), F32), s((rows, 1), F32), s((rows, D), BF), s((rows, DD), F32),
+        out_shape=shapes + [jax.ShapeDtypeStruct((rows, DD), F32)],
+        in_specs=[pl.BlockSpec(memory_space=pltpu.SMEM), vmem, vmem] + [anyspec] * 8,
+        out_specs=[anyspec] * 15 + [vmem],
+        scratch_shapes=[like(one) for one in [pos, patches] + weights + shapes]
+        + [
+            pltpu.VMEM((rows, D), F32), pltpu.VMEM((rows, D), F32), pltpu.VMEM((3, P_ROWS, D), BF), pltpu.VMEM((images * P_ROWS, PIX), BF),
+            pltpu.VMEM((rows, rows), F32), pltpu.SemaphoreType.DMA((8,)), pltpu.SemaphoreType.DMA((15,)),
         ],
-        in_specs=[pl.BlockSpec(memory_space=pltpu.SMEM)] + [vmem] * 10,
-        out_specs=[vmem] * 16,
-        scratch_shapes=[pltpu.VMEM((rows, D), F32), pltpu.VMEM((rows, D), F32), pltpu.VMEM((3, P_ROWS, D), BF)],
         compiler_params=pltpu.CompilerParams(vmem_limit_bytes=60 * MB),
-    )(counts, patches, cols, pos, *weights, norms, dec_embed)
-
-
-def decoder_kernel(images, counts_ref, masked_ref, patches_ref, cols_ref, rows_ref, pos_ref, entering_ref, triple_ref, proj_ref, up_ref, down_ref, head_ref, norms_ref,
-                   flat, grad_entering, loss_ref,
-                   x, hide, entry, plain1, scale1, triple, probs, mixed, plain2, scale2, inner, act, slope, plain3, scale3, final, grad_pred,
-                   low, grad_hidden, side, low_mixed, grad_triple, norm_sums, stage, sem):
+    )(counts, cols, norms, pos, patches, *weights)
+
+
+def decoder_kernel(images, counts_ref, masked_ref, cols_ref, rows_ref, entering_ref, norms_ref, *refs):
+    pos_hbm, patches_hbm, *weights_hbm = refs[:7]
+    flat, grad_entering, loss_ref = refs[7:10]
+    pos, patches, *weights = refs[10:17]
+    (x, hide, entry, plain1, scale1, triple, probs, mixed, plain2, scale2, inner, act, slope, plain3, scale3, final, grad_pred,
+     low, grad_hidden, side, low_mixed, grad_triple, norm_sums, padded, stage, sem, in_sem) = refs[17:]
+    need = Moves(("pos", "patches") + DEC_NAMES, [pos_hbm, patches_hbm] + weights_hbm, [pos, patches] + weights, in_sem)
+    need.start()
+    saved = (entry, plain1, scale1, triple, probs, mixed, plain2, scale2, inner, act, slope)
+    need.targets.update(zip(SAVED[1:12], saved))
     lane = lax.broadcasted_iota(jnp.int32, (P_ROWS, KEEP), 1)
     spot = lax.broadcasted_iota(jnp.int32, (P_ROWS, KEEP), 0)
     line = lax.broadcasted_iota(jnp.int32, (P_ROWS, 1), 0)
+    need("pos")
 
     def start(i):
         at = rows_at(i, P_ROWS)
@@ -998,14 +1168,12 @@
         pick = hit.astype(BF)
         top, mid, end = three(entering_ref[rows_at(i, KEEP), :])
         picked = dot_nn(pick, top) + dot_nn(pick, mid) + dot_nn(pick, end)
-        x[at, :] = jnp.where(shown > 0.0, picked, norms_ref[6:7, :]) + pos_ref[...]
+        x[at, :] = jnp.where(shown > 0.0, picked, norms_ref[6:7, :]) + pos[...]
         hide[at, :] = jnp.where(jnp.logical_and(line < PATCHES, shown == 0.0), 1.0, 0.0)
 
     loop(images, start)
     bias = jnp.where(line < PATCHES, 0.0, NEG_FILL)
-    weights = (triple_ref, proj_ref, up_ref, down_ref)
-    saved = (entry, plain1, scale1, triple, probs, mixed, plain2, scale2, inner, act, slope)
-    block_forward(x, P_ROWS, images, PATCHES, DHEADS, weights, norms_ref, lambda i: bias, saved)
+    block_forward(x, P_ROWS, images, DHEADS, need, norms_ref, lambda i: bias, saved)
 
     def last(i):
         at = rows_at(i, P_ROWS)
@@ -1017,11 +1185,13 @@
     loop(images, last)
     loss_ref[...] = jnp.zeros_like(loss_ref)
     masked = masked_ref[0:1, 0:1]
+    head_w = need("head_w")
+    pad_patches(need("patches"), padded, images)
 
     def score(i):
         at = rows_at(i, P_ROWS)
-        target, _ = norm(patches_ref[at, :].astype(F32))
-        diff = dot_nn(final[at, :], head_ref[...]) - target
+        target, _ = norm(padded[at, :].astype(F32))
+        diff = dot_nn(final[at, :], head_w[...]) - target
         hidden = hide[at, :]
         loss_ref[...] += jnp.sum(jnp.mean(diff * diff, axis=-1, keepdims=True) * hidden, axis=0, keepdims=True)
         grad_pred[at, :] = (diff * (hidden * (2.0 / PIX)) / masked).astype(BF)
@@ -1033,13 +1203,13 @@
 
     def back_final(i):
         at = rows_at(i, P_ROWS)
-        back, gain, shift = norm_grad(dot_nt(grad_pred[at, :], head_ref[...]), plain3[at, :], scale3[at, :], norms_ref[4:5, :])
+        back, gain, shift = norm_grad(dot_nt(grad_pred[at, :], head_w[...]), plain3[at, :], scale3[at, :], norms_ref[4:5, :])
         norm_sums[4:5, :] += gain
         norm_sums[5:6, :] += shift
         x[at, :] = back
 
     loop(images, back_final)
-    block_backward(x, P_ROWS, images, PATCHES, DHEADS, weights, norms_ref, norm_sums, saved, (low, grad_hidden, side, low_mixed, grad_triple), writer, (7, 8, 9, 10))
+    block_backward(x, P_ROWS, images, DHEADS, need, norms_ref, norm_sums, (low, grad_hidden, side, low_mixed, grad_triple), writer, (7, 8, 9, 10))
     spots = lax.broadcasted_iota(jnp.int32, (KEEP, P_ROWS), 1)
     slot = lax.broadcasted_iota(jnp.int32, (KEEP, P_ROWS), 0)
 
@@ -1051,19 +1221,14 @@
         grad_entering[rows_at(i, KEEP), :] = dot_nn(pick, grad.astype(BF)).astype(BF)
 
     loop(images, finish)
-    write_small(12, norm_sums, 7, flat, stage, sem)
-    extra = flat.shape[0] - TILES
-    if extra > 0:
-        stage[0, 0:extra] = jnp.zeros((extra, 8, LANES), F32)
-        copy = pltpu.make_async_copy(stage.at[0, pl.ds(0, extra)], flat.at[pl.ds(TILES, extra)], sem.at[0])
-        copy.start()
-        copy.wait()
-
-
-def decoder(total, counts, masked, patches, cols, order, pos, entering, weights, head, norms):
+    writer.small(12, norm_sums, 7, flat.shape[0] - TILES)
+
+
+def decoder(total, counts, masked, patches, cols, order, pos, entering, weights, norms):
     images = counts.shape[0]
     rows = images * P_ROWS
     vmem = pl.BlockSpec(memory_space=pltpu.VMEM)
+    anyspec = pl.BlockSpec(memory_space=pl.ANY)
 
     def v(shape, kind=F32):
         return pltpu.VMEM(shape, kind)
@@ -1076,25 +1241,36 @@
             jax.ShapeDtypeStruct((images * KEEP, DD), BF),
             jax.ShapeDtypeStruct((1, 1), F32),
         ],
-        in_specs=[pl.BlockSpec(memory_space=pltpu.SMEM)] + [vmem] * 12,
-        out_specs=[pl.BlockSpec(memory_space=pl.ANY), vmem, vmem],
-        scratch_shapes=[
+        in_specs=[pl.BlockSpec(memory_space=pltpu.SMEM)] + [vmem] * 5 + [anyspec] * 7,
+        out_specs=[anyspec, vmem, vmem],
+        scratch_shapes=[like(one) for one in [pos, patches] + weights]
+        + [
             v((rows, DD)), v((rows, 1)), v((rows, DD), BF), v((rows, DD)), v((rows, 1)), v((rows, 3 * DD), BF),
             v((images * DD // LANES, 4 * P_ROWS, P_ROWS)), v((rows, DD), BF), v((rows, DD)), v((rows, 1)), v((rows, DD), BF),
             v((rows, FD), BF), v((rows, FD)), v((rows, DD)), v((rows, 1)), v((rows, DD), BF), v((rows, PIX), BF),
             v((rows, DD), BF), v((rows, FD), BF), v((rows, DD)), v((rows, DD), BF), v((rows, 3 * DD), BF),
-            v((8, DD)), v((2, 32 * 16, 8, LANES)), pltpu.SemaphoreType.DMA((2,)),
+            v((8, DD)), v((rows, PIX), BF), v((2, 32 * 16, 8, LANES)), pltpu.SemaphoreType.DMA((2,)), pltpu.SemaphoreType.DMA((7,)),
         ],
         compiler_params=pltpu.CompilerParams(vmem_limit_bytes=63 * MB),
-    )(counts, masked, patches, cols, order, pos, entering, *weights, head, norms)
-
-
-def encoder_back_kernel(images, flat_in, grad_entering, seen, entry, plain1, scale1, triple, probs, mixed, plain2, scale2, inner, act, slope, plain3, scale3, encoded,
-                        triple_ref, proj_ref, up_ref, down_ref, norms_ref, dec_embed_ref, flat, x, low, grad_hidden, side, low_mixed, grad_triple, norm_sums, stage, sem):
+    )(counts, masked, cols, order, entering, norms, pos, patches, *weights)
+
+
+def encoder_back_kernel(images, flat_in, grad_entering, norms_ref, *refs):
+    names = SAVED + ENC_NAMES[1:]
+    sources = refs[:20]
+    flat = refs[20]
+    targets = refs[21:41]
+    x, low, grad_hidden, side, low_mixed, grad_triple, norm_sums, stage, sem, in_sem = refs[41:]
+    need = Moves(names, sources, targets, in_sem)
+    need.start(
+        "encoded", "dec_embed_w", "plain3", "scale3", "down_w", "slope", "act", "inner", "up_w", "plain2", "scale2",
+        "mixed", "proj_w", "triple", "probs", "entry", "triple_w", "plain1", "scale1", "seen",
+    )
     writer = Writer(flat, stage, sem)
-    writer.outer(6, encoded, grad_entering)
+    writer.outer(6, need("encoded"), grad_entering)
     norm_sums[...] = jnp.zeros_like(norm_sums)
-    side[...] = dot_nt(grad_entering[...], dec_embed_ref[...])
+    side[...] = dot_nt(grad_entering[...], need("dec_embed_w")[...])
+    plain3, scale3 = need("plain3"), need("scale3")
 
     def last(i):
         at = rows_at(i, KEEP)
@@ -1104,14 +1280,13 @@
         x[at, :] = back
 
     loop(images, last)
-    block_backward(x, KEEP, images, KEEP, HEADS, (triple_ref, proj_ref, up_ref, down_ref), norms_ref, norm_sums,
-                   (entry, plain1, scale1, triple, probs, mixed, plain2, scale2, inner, act, slope), (low, grad_hidden, side, low_mixed, grad_triple), writer, (1, 2, 3, 4))
+    block_backward(x, KEEP, images, HEADS, need, norms_ref, norm_sums, (low, grad_hidden, side, low_mixed, grad_triple), writer, (1, 2, 3, 4))
     low[...] = x[...].astype(BF)
-    writer.outer(0, seen, low)
-    write_small(5, norm_sums, 6, flat, stage, sem)
-
-
-def encoder_back(flat, grad_entering, saved, weights, norms, dec_embed):
+    writer.outer(0, need("seen"), low)
+    writer.small(5, norm_sums, 6)
+
+
+def encoder_back(flat, grad_entering, saved, weights, norms):
     rows = grad_entering.shape[0]
     images = rows // KEEP
     vmem = pl.BlockSpec(memory_space=pltpu.VMEM)
@@ -1124,24 +1299,26 @@
         functools.partial(encoder_back_kernel, images),
         name="encoder_back",
         out_shape=jax.ShapeDtypeStruct(flat.shape, flat.dtype),
-        in_specs=[anyspec] + [vmem] * (1 + len(saved) + 6),
+        in_specs=[anyspec, vmem, vmem] + [anyspec] * 20,
         out_specs=anyspec,
-        scratch_shapes=[
+        scratch_shapes=[like(one) for one in saved + weights]
+        + [
             v((rows, D)), v((rows, D), BF), v((rows, F), BF), v((rows, D)), v((rows, D), BF), v((rows, 3 * D), BF),
-            v((8, D)), v((2, 32 * 24, 8, LANES)), pltpu.SemaphoreType.DMA((2,)),
+            v((8, D)), v((2, 32 * 24, 8, LANES)), pltpu.SemaphoreType.DMA((2,)), pltpu.SemaphoreType.DMA((20,)),
         ],
         input_output_aliases={0: 0},
         compiler_params=pltpu.CompilerParams(vmem_limit_bytes=60 * MB),
-    )(flat, grad_entering, *saved, *weights, norms, dec_embed)
+    )(flat, grad_entering, norms, *saved, *weights)
 
 
 def positions(width):
-    index = jnp.arange(PATCHES)
+    index = np.arange(PATCHES)
     quarter = width // 4
-    freq = 10000.0 ** (-jnp.arange(quarter).astype(jnp.float32) / quarter)
-    row = (index // GRID).astype(jnp.float32)[:, None] * freq[None, :]
-    column = (index % GRID).astype(jnp.float32)[:, None] * freq[None, :]
-    return jnp.concatenate([jnp.sin(row), jnp.cos(row), jnp.sin(column), jnp.cos(column)], axis=1)
+    freq = 10000.0 ** (-np.arange(quarter).astype(np.float32) / np.float32(quarter))
+    row = (index // GRID).astype(np.float32)[:, None] * freq[None, :].astype(np.float32)
+    column = (index % GRID).astype(np.float32)[:, None] * freq[None, :].astype(np.float32)
+    table = np.concatenate([np.sin(row), np.cos(row), np.sin(column), np.cos(column)], axis=1).astype(np.float32)
+    return jnp.asarray(np.pad(table, ((0, P_ROWS - PATCHES), (0, 0))))
 
 
 ADAM_EPS = 1e-08
@@ -1170,22 +1347,19 @@
     index = lax.axis_index("dp") * n_pair + lax.axis_index("pair")
     extra = jnp.zeros((8, LANES), F32).at[0, :images].set((PATCHES - counts).astype(F32))
     slab = to_tiles(own_lines(master, share, index), extra, share, n, n_pair)
-    slots = gather(slab, n_dp, n_pair)
+    slots = gather(slab, n_dp, n_pair, 1)
     masked = jnp.sum(slots[:, slab.shape[0] - 2, 0, :].astype(F32))
     held = assemble(slots, share)
     parts = [held[i].reshape(-1)[: SHAPES[i][0] * SHAPES[i][1]].reshape(SHAPES[i]).astype(F32) if i in SMALL else matrix(held[i], i) for i in range(len(SHAPES))]
-    padded = jnp.pad(patches, ((0, 0), (0, P_ROWS - PATCHES), (0, 0))).reshape(images * P_ROWS, PIX)
     slots_at = patch_order[:, :KEEP]
     cols = slots_at[:, :, None]
-    pos_e = jnp.pad(positions(D), ((0, P_ROWS - PATCHES), (0, 0)))
-    pos_d = jnp.pad(positions(DD), ((0, P_ROWS - PATCHES), (0, 0)))
-    enc_weights = parts[1:5]
-    *saved, entering = encoder(counts, padded, cols, pos_e, [parts[0]] + enc_weights, parts[5], parts[6])
+    enc_weights = parts[1:5] + [parts[6]]
+    *saved, entering = encoder(counts, patches, cols, positions(D), [parts[0]] + enc_weights, parts[5])
     total = max(a for a, _ in ranges(share, n)) + slab_tiles(share, n)
     flat, grad_entering, loss_local = decoder(
-        total, counts, masked.reshape(1, 1), padded, cols, slots_at, pos_d, entering, parts[7:11], parts[11], parts[12]
+        total, counts, masked.reshape(1, 1), patches, cols, slots_at, positions(DD), entering, parts[7:12], parts[12]
     )
-    flat = encoder_back(flat, grad_entering, saved, enc_weights, parts[5], parts[6])
+    flat = encoder_back(flat, grad_entering, saved, enc_weights, parts[5])
     slab_sum = reduce(flat.reshape(-1, LANES), share, n_dp, n_pair)
     rows = share // LANES if share % LANES == 0 else (share + LANES - 1) // LANES + 1
     grad_share = own_flat(to_lines(slab_sum, rows, share, n_pair), share, index)

time: 530 us -> 436 us (0.82)
  Pallas kernels: 490 us -> 409 us
  local copies, waits for them, and re-layouts: 15.2 us -> 4.95 us
    pallas_call x2, Pallas kernels: 291 us -> 240 us  [the longest x1 126 us: reduce(): pl.pallas_call(functools.partial(reduce_kernel, n_z, chunks, share), name...]
    pallas_call x1, Pallas kernels: 51.6 us -> 36.1 us  [encoder_back(): pl.pallas_call(functools.partial(encoder_back_kernel, images), name='enco...]
    pallas_call x1, Pallas kernels: 34.6 us -> 22.8 us  [encoder(): pl.pallas_call(functools.partial(encoder_kernel, images), name='encoder',...]
    unnamed x29 -> x13, local copies, waits for them, and re-layouts: 10.4 us -> 1.18 us
    pallas_call x1, Pallas kernels: 83.2 us -> 76.5 us  [decoder(): pl.pallas_call(functools.partial(decoder_kernel, images), name='decoder',...]
where the time goes in v3:
time: 436 us; the launch traced here: 435 us
  Pallas kernels  409 us (94%)
  other arithmetic  14.9 us (3%)
  between operations  6.46 us (1%)
  local copies, waits for them, and re-layouts  4.95 us (1%)
    pallas_call x1, Pallas kernels, reduce(): pl.pallas_call(functools.partial(reduce_kernel, n_z, chunks, share), name...  126 us
    pallas_call x1, Pallas kernels, gather(): pl.pallas_call(functools.partial(gather_kernel, n_z, chunks), name='gathe...  114 us
    pallas_call x1, Pallas kernels, decoder(): pl.pallas_call(functools.partial(decoder_kernel, images), name='decoder',...  76.5 us
    pallas_call x1, Pallas kernels, encoder_back(): pl.pallas_call(functools.partial(encoder_back_kernel, images), name='enco...  36.1 us
    pallas_call x1, Pallas kernels, encoder(): pl.pallas_call(functools.partial(encoder_kernel, images), name='encoder',...  22.8 us
    pallas_call x1, Pallas kernels, assemble(): pl.pallas_call(functools.partial(assemble_kernel, share, n), name='assemb...  16.1 us
    pallas_call x1, Pallas kernels, share_all(): pl.pallas_call(functools.partial(share_kernel, n_dp, n_pair), name='share...  11.4 us

profile of v3, /device:TPU:0, one launch (start us, length us, event | category | flops | bytes accessed | tf_op | source)
XLA Modules:
  0.0 435.3 jit_solution(6007387177309847963)
XLA Ops:
  0.6 0.7 convert_bitcast_fusion
  1.3 0.6 scatter.6.extra_ref
  1.9 2.9 to_tiles.1.slab_ref
  4.8 114.0 %gather.1.slots_ref = bf16[32,386,8,128]{3,2,1,0:T(8,128)(2,1)} custom-call(bf16[386,8,128]{2,1,0:T(8,128)(2,1)} %to_tiles.1.slab_ref), custom_call_target="tpu_custom_call" | custom-call | tf_op jit(solution)/shard_map/gather/pallas_call | solution.py:173
  118.8 1.5 convert_reduce_fusion
  120.3 0.6 fusion.4
  120.9 0.8 copy.19.cols_ref
  121.6 16.1 %assemble.1 = (bf16[576,8,128]{2,1,0:T(8,128)(2,1)}, bf16[1728,8,128]{2,1,0:T(8,128)(2,1)}, bf16[576,8,128]{2,1,0:T(8,128)(2,1)}, bf16[2304,8,128]{2,1,0:T(8,128...) custom-call(bf16[32,386,8,128]{3,2,1,0:T(8,128)(2,1)} %gather.1.slot, ...), custom_call_target="tpu_custom_call" | custom-call | tf_op jit(solution)/shard_map/assemble/pallas_call | solution.py:371
  137.7 0.7 slice_convert_fusion
  138.5 0.6 reshape.200.norms_ref
  139.1 1.2 copy.18.refs_1_
  140.2 22.8 %encoder.1 = (bf16[256,768]{1,0:T(8,128)(2,1)}, bf16[256,768]{1,0:T(8,128)(2,1)}, f32[256,768]{1,0:T(8,128)}, f32[256,1]{1,0:T(8,128)}, bf16[256,2304]{1,0:T(8,1...) custom-call(s32[4]{0:T(128)} %counts_ref.3, ...), custom_call_target="tpu_custom_call" | custom-call | tf_op jit(solution)/shard_map/encoder/pallas_call | solution.py:1134
  163.1 0.6 slice_convert_fusion.1.norms_ref
  163.7 76.5 %decoder.1 = (f32[11363,8,128]{2,1,0:T(8,128)}, bf16[256,512]{1,0:T(8,128)(2,1)}, f32[1,1]{1,0:T(1,128)}) custom-call(s32[4]{0:T(128)} %counts_ref.3, f32[1,1]{1,0:T(1,128)} %bitcast.2.masked_ref, s32[4,64,1]{2,1,0:T(8,128)} %copy.19.cols_ref, s32[4,64]{1,0:T(4,128)} %get-tuple-element.100.rows_ref, f32[256,512]{1,0:T(8,128)} %get-tuple-element.69.entering_ref, ...), custom_call_target="tpu_custom_call" | custom-call | tf_op jit(solution)/shard_map/decoder/pallas_call | solution.py:1236
  240.2 36.1 %encoder_back.1 = f32[11363,8,128]{2,1,0:T(8,128)} custom-call(f32[11363,8,128]{2,1,0:T(8,128)} %get-tuple-element.76.flat_in, bf16[256,512]{1,0:T(8,128)(2,1)} %get-tuple-element.77.grad_entering, f32[6,768]{1,0:T(8,128)} %reshape.200.norms_ref, bf16[256,768]{1,0:T(8,128)(2,1)} %get-tuple-element.78.refs_0_, ...), custom_call_target="tpu_custom_call", output_to_operand_aliasing={{}: (0, {})} | custom-call | tf_op jit(solution)/shard_map/encoder_back/pallas_call | solution.py:1298
  276.3 126.0 %reduce_scatter.1 = (f32[3072,128]{1,0:T(8,128)}, f32[16,4,768,128]{3,2,1,0:T(8,128)}) custom-call(f32[90904,128]{1,0:T(8,128)} %bitcast.82), custom_call_target="tpu_custom_call" | custom-call | tf_op jit(solution)/shard_map/reduce_scatter/pallas_call | solution.py:635
  402.3 3.2 to_lines.1
  405.5 2.5 multiply_reduce_fusion
  408.0 1.4 maximum_bitcast_fusion
  409.4 0.6 scatter.9.in_ref
  410.0 11.4 %share_all.1 = f32[32,8,128]{2,1,0:T(8,128)} custom-call(f32[8,128]{1,0:T(8,128)} %scatter.9.in_ref), custom_call_target="tpu_custom_call" | custom-call | tf_op jit(solution)/shard_map/share_all/pallas_call | solution.py:688
  421.3 1.7 slice_reduce_fusion
  425.8 0.6 fusion.5
  427.1 5.9 %multiply_subtract_fusion = (f32[362752]{0:T(1024)}, f32[362752]{0:T(1024)}, f32[362752]{0:T(1024)}) fusion(f32[362752]{0:T(1024)S(1)} %copy-done.1, f32[]{:T(128)} %bitcast.49, f32[]{:T(128)} %bitcast.48, f32[]{:T(128)} %bitcast.47, f32[]{:T(128)} %bitcast.46, s32[]{:T(128)S(6)} %mul.62, f32[2834,128]{1,0:T(8,128)S(1)} %copy-done, f32[]{:T(128)S(6)} %div.20, ...), kind=kLoop, calls=%fused_computation.4 | loop fusion | flops 6892288 | bytes 10157080 | tf_op jit(solution)/shard_map/sub | solution.py:1378
  (13 shorter events, 0.0 us)
Async XLA Ops:
  4.8 115.4 %copy-start.5 = (s32[4,196]{1,0:T(4,128)S(1)}, s32[4,196]{1,0:T(4,128)}, u32[]{:S(2)}) copy-start(s32[4,196]{1,0:T(4,128)} %param.16) | copy-start | bytes 9412
  121.6 17.4 %copy-start.2 = (bf16[4,196,768]{2,0,1:T(4,128)(2,1)S(1)}, bf16[4,196,768]{2,0,1:T(4,128)(2,1)}, u32[]{:S(2)}) copy-start(bf16[4,196,768]{2,0,1:T(4,128)(2,1)} %param.15) | copy-start | bytes 3612676
  140.2 22.8 %copy-start.3 = (bf16[4,8,128]{2,1,0:T(8,128)(2,1)S(1)}, bf16[4,8,128]{2,1,0:T(8,128)(2,1)}, u32[]{:S(2)}) copy-start(bf16[4,8,128]{2,1,0:T(8,128)(2,1)} %get-tuple-element.70) | copy-start | bytes 24580
  402.3 24.8 %copy-start.1 = (f32[362752]{0:T(1024)S(1)}, f32[362752]{0:T(1024)}, u32[]{:S(2)}) copy-start(f32[362752]{0:T(1024)} %param.18) | copy-start | bytes 4353028
  405.5 20.3 %copy-start.4 = (f32[2]{0:T(128)S(1)}, f32[2]{0:T(128)}, u32[]{:S(2)}) copy-start(f32[2]{0:T(128)} %param.21) | copy-start | bytes 28
  405.5 21.5 %copy-start = (f32[2834,128]{1,0:T(8,128)S(1)}, f32[2834,128]{1,0:T(8,128)}, u32[]{:S(2)}) copy-start(f32[2834,128]{1,0:T(8,128)} %to_lines.1) | copy-start | bytes 4353028

commit v4 on v3

--- a/solution.py
+++ b/solution.py
@@ -55,136 +55,15 @@
     return total
 
 
-def gather_kernel(n_z, chunks, slab_ref, out_ref, own_sem, z_sem, plane_sem, second_sem, third_sem, recv_sem):
-    piece = slab_ref.shape[0] // (2 * chunks)
-    z, x, y, c = place()
-    to = partners(z, x, y, c)
-    me = slot_of(z, x, y, c)
-    local = pltpu.make_async_copy(slab_ref, out_ref.at[me], own_sem)
-    local.start()
-    greet(n_z, z, to)
-    local.wait()
-    steps = n_z * chunks
-
-    def copy(slot, chunk, part, name, sem):
-        rows = pl.ds((chunk * 2 + part) * piece, piece)
-        return pltpu.make_async_remote_copy(
-            out_ref.at[slot, rows],
-            out_ref.at[slot, rows],
-            sem,
-            recv_sem.at[slot, chunk, part],
-            device_id=to[name],
-            device_id_type=MESH,
-        )
-
-    def arrived(slot, chunk, part):
-        copy(slot, chunk, part, "c", own_sem).wait_recv()
-
-    def lines(s):
-        t, chunk = s // chunks, lax.rem(s, chunks)
-        for d in (0, 1):
-            zz = z - t if d == 0 else z + t
-            inside = zz >= 0 if d == 0 else zz < n_z
-            more = z < n_z - 1 if d == 0 else z > 0
-            fresh = both(t > 0, inside)
-            held = jnp.logical_or(fresh, t == 0) if d == 0 else fresh
-            onward = both(jnp.logical_or(fresh, t == 0), more)
-            yield d, zz, chunk, fresh, held, onward
-
-    def first_sends(d, zz, chunk, held, onward, s, act):
-        slot = slot_of(zz, x, y, c)
-        for part in (0, 1):
-            pl.when(onward)(lambda part=part: act(copy(slot, chunk, part, ("up", "down")[d], z_sem.at[s, d, part])))
-
-        @pl.when(held)
-        def _():
-            for i, (part, name) in enumerate(((0, "x"), (1, "y"), (0, "y"), (1, "x"), (0, "c"), (1, "c"))):
-                act(copy(slot, chunk, part, name, plane_sem.at[s, d, i]))
-
-    def first(s):
-        for d, zz, chunk, fresh, held, onward in lines(s):
-
-            @pl.when(fresh)
-            def _():
-                for part in (0, 1):
-                    arrived(slot_of(zz, x, y, c), chunk, part)
-
-            first_sends(d, zz, chunk, held, onward, s, lambda one: one.start())
-
-    def second_items(zz):
-        return ((0, slot_of(zz, 1 - x, y, c), "y"), (1, slot_of(zz, x, 1 - y, c), "x"))
-
-    def second(s):
-        for d, zz, chunk, _, held, _ in lines(s):
-
-            @pl.when(held)
-            def _():
-                for part, slot, name in second_items(zz):
-                    arrived(slot, chunk, part)
-                    copy(slot, chunk, part, name, second_sem.at[s, d, part, 0]).start()
-                    copy(slot, chunk, part, "c", second_sem.at[s, d, part, 1]).start()
-
-    def third_items(zz):
-        return ((0, slot_of(zz, x, 1 - y, c)), (1, slot_of(zz, 1 - x, y, c)), (0, slot_of(zz, 1 - x, 1 - y, c)), (1, slot_of(zz, 1 - x, 1 - y, c)))
-
-    def third(s):
-        for d, zz, chunk, _, held, _ in lines(s):
-
-            @pl.when(held)
-            def _():
-                for i, (part, slot) in enumerate(third_items(zz)):
-                    arrived(slot, chunk, part)
-                    copy(slot, chunk, part, "c", third_sem.at[s, d, i]).start()
-
-    def turn(s, _):
-        pl.when(s < steps)(lambda: first(s))
-        pl.when(both(s >= 1, s < steps + 1))(lambda: second(s - 1))
-        pl.when(s >= 2)(lambda: third(s - 2))
-        return 0
-
-    lax.fori_loop(0, steps + 2, turn, 0)
-
-    def finish(s, _):
-        for d, zz, chunk, _, held, onward in lines(s):
-            first_sends(d, zz, chunk, held, onward, s, lambda one: one.wait_send())
-
-            @pl.when(held)
-            def _():
-                for part, slot, name in second_items(zz):
-                    copy(slot, chunk, part, name, second_sem.at[s, d, part, 0]).wait_send()
-                    copy(slot, chunk, part, "c", second_sem.at[s, d, part, 1]).wait_send()
-                for i, (part, slot) in enumerate(third_items(zz)):
-                    copy(slot, chunk, part, "c", third_sem.at[s, d, i]).wait_send()
-                for ox in (0, 1):
-                    for oy in (0, 1):
-                        for part in (0, 1):
-                            arrived(slot_of(zz, ox, oy, 1 - c), chunk, part)
-
-        return 0
-
-    lax.fori_loop(0, steps, finish, 0)
-
-
-def gather(slab, n_dp, n_pair, chunks):
-    n_z = n_dp // 2
-    n = n_dp * n_pair
-    steps = n_z * chunks
-    dma = pltpu.SemaphoreType.DMA
-    return pl.pallas_call(
-        functools.partial(gather_kernel, n_z, chunks),
-        name="gather",
-        out_shape=jax.ShapeDtypeStruct((n,) + slab.shape, slab.dtype),
-        in_specs=[pl.BlockSpec(memory_space=pltpu.VMEM)],
-        out_specs=pl.BlockSpec(memory_space=pl.ANY),
-        scratch_shapes=[dma, dma((steps, 2, 2)), dma((steps, 2, 6)), dma((steps, 2, 2, 2)), dma((steps, 2, 4)), dma((n, chunks, 2))],
-        compiler_params=pltpu.CompilerParams(collective_id=0, has_side_effects=True),
-    )(slab)
-
-
 PIX, HEADS, F, DHEADS, FD, GRID, KEEP, D, DD, PATCHES = 768, 12, 3072, 16, 2048, 14, 64, 768, 512, 196
 SHAPES = [(PIX, D), (D, 3 * D), (D, D), (D, F), (F, D), (6, D), (D, DD), (DD, 3 * DD), (DD, DD), (DD, FD), (FD, DD), (DD, PIX), (7, DD)]
 SMALL = (5, 12)
 ENC_PARAMS = 7672320
+NORM_EPS = 1e-06
+ADAM_EPS = 1e-08
+BETA_ONE = 0.9
+BETA_TWO = 0.95
+DECAY = 0.05
 MB = 1 << 20
 CELL = 8 * LANES
 BLOCK = 96
@@ -203,6 +82,7 @@
 
 
 ENTRIES, ROWS, TILES = make_entries()
+BIG = tuple(i for i in range(len(SHAPES)) if i not in SMALL)
 MARGIN = 8 * max(cols for _, _, cols, _, _ in ENTRIES)
 
 
@@ -254,60 +134,8 @@
         lax.fori_loop(jnp.where(low < high, low // size, 0), jnp.where(low < high, (high + size - 1) // size, 0), group, 0)
 
 
-def tile_kernel(share, n_pair, lines_ref, extra_ref, out_ref, wide):
-    k = lax.axis_index("dp") * n_pair + lax.axis_index("pair")
-    rows = lines_ref.shape[0]
-    wide[0:MARGIN, :] = jnp.zeros((MARGIN, LANES), jnp.float32)
-    wide[MARGIN + rows :, :] = jnp.zeros((wide.shape[0] - MARGIN - rows, LANES), jnp.float32)
-    wide[MARGIN : MARGIN + rows, :] = lines_ref[...]
-
-    def body(line, tile, cols):
-        for col in range(cols):
-            out_ref[tile + col] = wide[pl.ds(line + col, 8, stride=cols), :].astype(out_ref.dtype)
-
-    tiled(share, k, body)
-    out_ref[out_ref.shape[0] - 2] = extra_ref[...].astype(out_ref.dtype)
-
-
 def wide_rows(rows):
     return -(-(rows + 2 * MARGIN) // 8) * 8
-
-
-def to_tiles(lines, extra, share, n, n_pair):
-    rows = lines.shape[0]
-    count = slab_tiles(share, n) + 2
-    spec = pl.BlockSpec(memory_space=pltpu.VMEM)
-    return pl.pallas_call(
-        functools.partial(tile_kernel, share, n_pair),
-        name="to_tiles",
-        out_shape=jax.ShapeDtypeStruct((count, 8, LANES), jnp.bfloat16),
-        in_specs=[spec, spec],
-        out_specs=spec,
-        scratch_shapes=[pltpu.VMEM((wide_rows(rows), LANES), jnp.float32)],
-    )(lines, extra)
-
-
-def line_kernel(share, n_pair, slab_ref, out_ref, wide):
-    k = lax.axis_index("dp") * n_pair + lax.axis_index("pair")
-
-    def body(line, tile, cols):
-        for col in range(cols):
-            wide[pl.ds(line + col, 8, stride=cols), :] = slab_ref[pl.ds(pl.multiple_of((tile + col) * 8, 8), 8), :]
-
-    tiled(share, k, body)
-    out_ref[...] = wide[MARGIN : MARGIN + out_ref.shape[0], :]
-
-
-def to_lines(slab, rows, share, n_pair):
-    spec = pl.BlockSpec(memory_space=pltpu.VMEM)
-    return pl.pallas_call(
-        functools.partial(line_kernel, share, n_pair),
-        name="to_lines",
-        out_shape=jax.ShapeDtypeStruct((rows, LANES), jnp.float32),
-        in_specs=[spec],
-        out_specs=spec,
-        scratch_shapes=[pltpu.VMEM((wide_rows(rows), LANES), jnp.float32)],
-    )(slab)
 
 
 def pieces(share, n):
@@ -331,61 +159,6 @@
     return spans, plain, seams
 
 
-def assemble_kernel(share, n, slots_ref, *refs):
-    outs = refs[: len(ENTRIES)]
-    whole, right, plain_sem, left_sem, right_sem, out_sem = refs[len(ENTRIES) :]
-    spans, plain, seams = pieces(share, n)
-    waits = [[] for _ in ENTRIES]
-    for i, (number, k, low, high) in enumerate(plain):
-        copy = pltpu.make_async_copy(slots_ref.at[k, pl.ds(low - spans[k][0], high - low)], whole.at[pl.ds(low, high - low)], plain_sem.at[i])
-        copy.start()
-        waits[number].append(copy)
-    for i, (number, k, low, high) in enumerate(seams):
-        one = pltpu.make_async_copy(slots_ref.at[k, pl.ds(low - spans[k][0], high - low)], whole.at[pl.ds(low, high - low)], left_sem.at[i])
-        two = pltpu.make_async_copy(
-            slots_ref.at[k + 1, pl.ds(low - spans[k + 1][0], high - low)], right.at[i, pl.ds(0, high - low)], right_sem.at[i]
-        )
-        one.start()
-        two.start()
-        waits[number] += [one, two]
-    ended = []
-    for number, (_, _, cols, tile, groups) in enumerate(ENTRIES):
-        for copy in waits[number]:
-            copy.wait()
-        for i, (owner, k, low, high) in enumerate(seams):
-            if owner == number:
-                total = whole[low:high].astype(jnp.float32) + right[i, 0 : high - low].astype(jnp.float32)
-                whole[low:high] = total.astype(jnp.bfloat16)
-        copy = pltpu.make_async_copy(whole.at[pl.ds(tile, groups * cols)], outs[number], out_sem.at[number])
-        copy.start()
-        ended.append(copy)
-    for copy in ended:
-        copy.wait()
-
-
-def assemble(slots, share):
-    n = slots.shape[0]
-    _, plain, seams = pieces(share, n)
-    anyspec = pl.BlockSpec(memory_space=pl.ANY)
-    dma = pltpu.SemaphoreType.DMA
-    return pl.pallas_call(
-        functools.partial(assemble_kernel, share, n),
-        name="assemble",
-        out_shape=[jax.ShapeDtypeStruct((groups * cols, 8, LANES), jnp.bfloat16) for _, _, cols, _, groups in ENTRIES],
-        in_specs=[anyspec],
-        out_specs=[anyspec] * len(ENTRIES),
-        scratch_shapes=[
-            pltpu.VMEM((TILES, 8, LANES), jnp.bfloat16),
-            pltpu.VMEM((len(seams), MARGIN // 8, 8, LANES), jnp.bfloat16),
-            dma((len(plain),)),
-            dma((len(seams),)),
-            dma((len(seams),)),
-            dma((len(ENTRIES),)),
-        ],
-        compiler_params=pltpu.CompilerParams(vmem_limit_bytes=60 * MB),
-    )(slots)
-
-
 def matrix(tiles_, number):
     rows, width = SHAPES[number]
     cols = width // LANES
@@ -398,10 +171,203 @@
     return value.reshape(rows // 8, 8, cols, LANES).transpose(0, 2, 1, 3).reshape(rows * cols, LANES)
 
 
-def reduce_kernel(n_z, chunks, share, grad_ref, out_ref, sib_ref, gbuf, rbuf, keep, q1s, q1r, q2s, q2r, zs, zr, t1s, t1r, t2s, t2r, tzs, tzr, sib_sem, load_sem, s1_sem, s2_sem, z_sem):
+def gather_kernel(n_z, n_pair, chunks, share, lines_ref, extra_ref, *refs):
+    outs = dict(zip(BIG, refs[: len(BIG)]))
+    enc_norms, dec_norms, masked_ref = refs[len(BIG) : len(BIG) + 3]
+    wide, out_ref, own_sem, z_sem, plane_sem, second_sem, third_sem, recv_sem, put_sem = refs[len(BIG) + 3 :]
+    n = n_z * 2 * n_pair
+    piece = out_ref.shape[1] // (2 * chunks)
     z, x, y, c = place()
     to = partners(z, x, y, c)
-    rows = out_ref.shape[0] // chunks
+    me = slot_of(z, x, y, c)
+    rows = lines_ref.shape[0]
+    wide[0:MARGIN, :] = jnp.zeros((MARGIN, LANES), jnp.float32)
+    wide[MARGIN + rows :, :] = jnp.zeros((wide.shape[0] - MARGIN - rows, LANES), jnp.float32)
+    wide[MARGIN : MARGIN + rows, :] = lines_ref[...]
+
+    def fill(line, tile, cols):
+        for col in range(cols):
+            out_ref[me, tile + col] = wide[pl.ds(line + col, 8, stride=cols), :].astype(out_ref.dtype)
+
+    tiled(share, me, fill)
+    out_ref[me, out_ref.shape[1] - 2] = extra_ref[...].astype(out_ref.dtype)
+    greet(n_z, z, to)
+    steps = n_z * chunks
+
+    def copy(slot, chunk, part, name, sem):
+        rows = pl.ds((chunk * 2 + part) * piece, piece)
+        return pltpu.make_async_remote_copy(
+            out_ref.at[slot, rows],
+            out_ref.at[slot, rows],
+            sem,
+            recv_sem.at[slot, chunk, part],
+            device_id=to[name],
+            device_id_type=MESH,
+        )
+
+    def arrived(slot, chunk, part):
+        copy(slot, chunk, part, "c", own_sem).wait_recv()
+
+    def lines(s):
+        t, chunk = s // chunks, lax.rem(s, chunks)
+        for d in (0, 1):
+            zz = z - t if d == 0 else z + t
+            inside = zz >= 0 if d == 0 else zz < n_z
+            more = z < n_z - 1 if d == 0 else z > 0
+            fresh = both(t > 0, inside)
+            held = jnp.logical_or(fresh, t == 0) if d == 0 else fresh
+            onward = both(jnp.logical_or(fresh, t == 0), more)
+            yield d, zz, chunk, fresh, held, onward
+
+    def first_sends(d, zz, chunk, held, onward, s, act):
+        slot = slot_of(zz, x, y, c)
+        for part in (0, 1):
+            pl.when(onward)(lambda part=part: act(copy(slot, chunk, part, ("up", "down")[d], z_sem.at[s, d, part])))
+
+        @pl.when(held)
+        def _():
+            for i, (part, name) in enumerate(((0, "x"), (1, "y"), (0, "y"), (1, "x"), (0, "c"), (1, "c"))):
+                act(copy(slot, chunk, part, name, plane_sem.at[s, d, i]))
+
+    def first(s):
+        for d, zz, chunk, fresh, held, onward in lines(s):
+
+            @pl.when(fresh)
+            def _():
+                for part in (0, 1):
+                    arrived(slot_of(zz, x, y, c), chunk, part)
+
+            first_sends(d, zz, chunk, held, onward, s, lambda one: one.start())
+
+    def second_items(zz):
+        return ((0, slot_of(zz, 1 - x, y, c), "y"), (1, slot_of(zz, x, 1 - y, c), "x"))
+
+    def second(s):
+        for d, zz, chunk, _, held, _ in lines(s):
+
+            @pl.when(held)
+            def _():
+                for part, slot, name in second_items(zz):
+                    arrived(slot, chunk, part)
+                    copy(slot, chunk, part, name, second_sem.at[s, d, part, 0]).start()
+                    copy(slot, chunk, part, "c", second_sem.at[s, d, part, 1]).start()
+
+    def third_items(zz):
+        return ((0, slot_of(zz, x, 1 - y, c)), (1, slot_of(zz, 1 - x, y, c)), (0, slot_of(zz, 1 - x, 1 - y, c)), (1, slot_of(zz, 1 - x, 1 - y, c)))
+
+    def third(s):
+        for d, zz, chunk, _, held, _ in lines(s):
+
+            @pl.when(held)
+            def _():
+                for i, (part, slot) in enumerate(third_items(zz)):
+                    arrived(slot, chunk, part)
+                    copy(slot, chunk, part, "c", third_sem.at[s, d, i]).start()
+
+    def turn(s, _):
+        pl.when(s < steps)(lambda: first(s))
+        pl.when(both(s >= 1, s < steps + 1))(lambda: second(s - 1))
+        pl.when(s >= 2)(lambda: third(s - 2))
+        return 0
+
+    lax.fori_loop(0, steps + 2, turn, 0)
+
+    def finish(s, _):
+        for d, zz, chunk, _, held, onward in lines(s):
+            first_sends(d, zz, chunk, held, onward, s, lambda one: one.wait_send())
+
+            @pl.when(held)
+            def _():
+                for part, slot, name in second_items(zz):
+                    copy(slot, chunk, part, name, second_sem.at[s, d, part, 0]).wait_send()
+                    copy(slot, chunk, part, "c", second_sem.at[s, d, part, 1]).wait_send()
+                for i, (part, slot) in enumerate(third_items(zz)):
+                    copy(slot, chunk, part, "c", third_sem.at[s, d, i]).wait_send()
+                for ox in (0, 1):
+                    for oy in (0, 1):
+                        for part in (0, 1):
+                            arrived(slot_of(zz, ox, oy, 1 - c), chunk, part)
+
+        return 0
+
+    lax.fori_loop(0, steps, finish, 0)
+
+    spans, plain, seams = pieces(share, n)
+    puts = []
+
+    def put(number, k, low, high):
+        copy = pltpu.make_async_copy(
+            out_ref.at[k, pl.ds(low - spans[k][0], high - low)], outs[number].at[pl.ds(low - ENTRIES[number][3], high - low)], put_sem.at[len(puts)]
+        )
+        copy.start()
+        puts.append(copy)
+
+    home = {}
+    for number, k, low, high in plain + seams:
+        if number in SMALL:
+            home.update({tile: (k, tile - spans[k][0]) for tile in range(low, high)})
+        elif (number, k, low, high) in plain:
+            put(number, k, low, high)
+    for number, k, low, high in seams:
+        left = pl.ds(low - spans[k][0], high - low)
+        right = pl.ds(low - spans[k + 1][0], high - low)
+        total = out_ref[k, left].astype(jnp.float32) + out_ref[k + 1, right].astype(jnp.float32)
+        out_ref[k, left] = total.astype(out_ref.dtype)
+        if number not in SMALL:
+            put(number, k, low, high)
+    for number, target in zip(SMALL, (enc_norms, dec_norms)):
+        row, lines_, _, tile, groups = ENTRIES[number]
+        per = SHAPES[number][1] // LANES
+        for group in range(groups):
+            k, at = home[tile + group]
+            value = out_ref[k, at].astype(jnp.float32)
+            for line in range(group * 8, min(group * 8 + 8, lines_)):
+                target[line // per : line // per + 1, line % per * LANES : (line % per + 1) * LANES] = value[line % 8 : line % 8 + 1, :]
+    masked_ref[...] = jnp.zeros_like(masked_ref)
+
+    def count(k, _):
+        masked_ref[...] += jnp.sum(out_ref[k, out_ref.shape[1] - 2].astype(jnp.float32)[0:1, :], axis=1, keepdims=True)
+        return 0
+
+    lax.fori_loop(0, n, count, 0)
+    for copy in puts:
+        copy.wait()
+
+
+def gather(lines, extra, share, n_dp, n_pair, chunks):
+    n_z = n_dp // 2
+    n = n_dp * n_pair
+    steps = n_z * chunks
+    tiles_ = slab_tiles(share, n) + 2
+    _, plain, seams = pieces(share, n)
+    dma = pltpu.SemaphoreType.DMA
+    anyspec = pl.BlockSpec(memory_space=pl.ANY)
+    vmem = pl.BlockSpec(memory_space=pltpu.VMEM)
+
+    def s(shape, kind=jnp.float32):
+        return jax.ShapeDtypeStruct(shape, kind)
+
+    return pl.pallas_call(
+        functools.partial(gather_kernel, n_z, n_pair, chunks, share),
+        name="gather",
+        out_shape=[s((ENTRIES[i][4] * ENTRIES[i][2], 8, LANES), jnp.bfloat16) for i in BIG] + [s(SHAPES[5]), s(SHAPES[12]), s((1, 1))],
+        in_specs=[vmem, vmem],
+        out_specs=[anyspec] * len(BIG) + [vmem] * 3,
+        scratch_shapes=[
+            pltpu.VMEM((wide_rows(lines.shape[0]), LANES), jnp.float32),
+            pltpu.VMEM((n, tiles_, 8, LANES), jnp.bfloat16),
+            dma, dma((steps, 2, 2)), dma((steps, 2, 6)), dma((steps, 2, 2, 2)), dma((steps, 2, 4)), dma((n, chunks, 2)), dma((len(plain) + len(seams),)),
+        ],
+        compiler_params=pltpu.CompilerParams(collective_id=0, has_side_effects=True, vmem_limit_bytes=60 * MB),
+    )(lines, extra)
+
+
+def reduce_kernel(n_z, n_pair, chunks, share, grad_ref, loss_in, params, master, moment1, moment2, first_ref, second_ref, master_ref, total_ref, sib_ref, wide, mine, shared, send_sem, recv_sem, gbuf, rbuf, keep, q1s, q1r, q2s, q2r, zs, zr, t1s, t1r, t2s, t2r, tzs, tzr, sib_sem, load_sem, s1_sem, s2_sem, z_sem):
+    z, x, y, c = place()
+    to = partners(z, x, y, c)
+    n = n_z * 2 * n_pair
+    me = slot_of(z, x, y, c)
+    rows = keep.shape[1] // chunks
     half = rows // 2
     steps = n_z * chunks
     count = half // BLOCK
@@ -562,7 +528,90 @@
                 def _():
                     pass_on(j, zc, part, name)
 
-    greet(n_z, z, to)
+    def spread_lines(line, tile, cols):
+        for col in range(cols):
+            wide[pl.ds(line + col, 8, stride=cols), :] = keep[n_z - 1, pl.ds(pl.multiple_of((tile + col) * 8, 8), 8), :]
+
+    count_lines = master.shape[0]
+    tall = 128
+
+    def by_lines(body):
+        def one(i, _):
+            body(pl.multiple_of(i * tall, tall), tall)
+            return 0
+
+        lax.fori_loop(0, count_lines // tall, one, 0)
+        if count_lines % tall:
+            body(count_lines // tall * tall, count_lines % tall)
+
+    def send(d):
+        return pltpu.make_async_remote_copy(mine, shared.at[me], send_sem.at[d], recv_sem.at[d], device_id=peer(d), device_id_type=MESH)
+
+    def update():
+        tiled(share, me, spread_lines)
+        lo, _ = line_span(share, me)
+        mine[...] = jnp.zeros_like(mine)
+
+        def squares(start, size):
+            value = wide[pl.ds(MARGIN + start, size), :]
+            if share % LANES:
+                line = lax.broadcasted_iota(jnp.int32, (size, LANES), 0) + lo + start
+                spot = line * LANES + lax.broadcasted_iota(jnp.int32, (size, LANES), 1)
+                inside = jnp.logical_and(spot >= share * me, spot < share * (me + 1))
+                value = jnp.where(inside, value, 0.0)
+            mine[0:1, :] += jnp.sum(value * value, axis=0, keepdims=True)
+
+        by_lines(squares)
+        lane = lax.broadcasted_iota(jnp.int32, (1, LANES), 1)
+        mine[1:2, :] = jnp.where(lane == 0, loss_in[0:1, 0:1], 0.0)
+        shared[me] = mine[...]
+
+        def go(d, _):
+            send(d).start()
+            return 0
+
+        def stop(d, _):
+            send(d).wait()
+            return 0
+
+        lax.fori_loop(1, n, go, 0)
+        lax.fori_loop(1, n, stop, 0)
+
+        def add(k, total):
+            return total + shared[k]
+
+        total = lax.fori_loop(0, n, add, jnp.zeros((8, LANES), jnp.float32))
+        norm_ = jnp.sqrt(jnp.sum(total[0:1, :], axis=1, keepdims=True))
+        loss_sum = jnp.sum(total[1:2, :], axis=1, keepdims=True)
+        total_ref[...] = jnp.where(lax.broadcasted_iota(jnp.int32, (8, LANES), 0) == 0, norm_, loss_sum)
+        factor = params[2] / (norm_ + NORM_EPS)
+
+        def adam(start, size):
+            at = pl.ds(start, size)
+            clipped = wide[pl.ds(MARGIN + start, size), :] * factor
+            one = BETA_ONE * moment1[at, :] + (1.0 - BETA_ONE) * clipped
+            two = BETA_TWO * moment2[at, :] + (1.0 - BETA_TWO) * clipped * clipped
+            line = lax.broadcasted_iota(jnp.int32, (size, 1), 0) + lo + start
+            rate = jnp.where(line < ENC_PARAMS // LANES, params[0], params[1])
+            step = one / params[3] / (jnp.sqrt(two / params[4]) + ADAM_EPS)
+            first_ref[at, :] = one
+            second_ref[at, :] = two
+            master_ref[at, :] = master[at, :] - rate * (step + DECAY * master[at, :])
+
+        by_lines(adam)
+
+    barrier = pltpu.get_barrier_semaphore()
+
+    def peer(d):
+        k = lax.rem(me + d, n)
+        return {"dp": k // n_pair, "pair": lax.rem(k, n_pair)}
+
+    def hello(d, _):
+        pl.semaphore_signal(barrier, inc=1, device_id=peer(d), device_id_type=MESH)
+        return 0
+
+    lax.fori_loop(1, n, hello, 0)
+    pl.semaphore_wait(barrier, n - 1)
 
     def begin(j, _):
         for q in range(4):
@@ -581,7 +630,7 @@
         return 0
 
     lax.fori_loop(0, steps + 3, turn, 0)
-    out_ref[...] = keep[n_z - 1]
+    update()
 
     def finish(j, _):
         zz = order(j // chunks)
@@ -615,7 +664,7 @@
     return max(d for d in (1, 2, 4) if rows % (2 * BLOCK * d) == 0)
 
 
-def reduce(flat, share, n_dp, n_pair):
+def reduce(flat, loss, params, lines, share, n_dp, n_pair):
     chunks = reduce_chunks(share, n_dp * n_pair)
     n_z, n = n_dp // 2, n_dp * n_pair
     rows = slab_tiles(share, n) * 8
@@ -624,6 +673,8 @@
     steps = n_z * chunks
     marks = (half // BLOCK + 7) // 8 * 8
     anyspec = pl.BlockSpec(memory_space=pl.ANY)
+    vmem = pl.BlockSpec(memory_space=pltpu.VMEM)
+    line = jax.ShapeDtypeStruct(lines[0].shape, jnp.float32)
 
     def q(*lead):
         return pltpu.VMEM(lead + (half, LANES), jnp.int16)
@@ -633,12 +684,17 @@
 
     dma = pltpu.SemaphoreType.DMA
     return pl.pallas_call(
-        functools.partial(reduce_kernel, n_z, chunks, share),
+        functools.partial(reduce_kernel, n_z, n_pair, chunks, share),
         name="reduce_scatter",
-        out_shape=[jax.ShapeDtypeStruct((rows, LANES), jnp.float32), jax.ShapeDtypeStruct((steps, 4, part, LANES), jnp.float32)],
-        in_specs=[anyspec],
-        out_specs=[pl.BlockSpec(memory_space=pltpu.VMEM), anyspec],
+        out_shape=[line, line, line, jax.ShapeDtypeStruct((8, LANES), jnp.float32), jax.ShapeDtypeStruct((steps, 4, part, LANES), jnp.float32)],
+        in_specs=[anyspec, vmem, pl.BlockSpec(memory_space=pltpu.SMEM)] + [vmem] * 3,
+        out_specs=[vmem] * 4 + [anyspec],
         scratch_shapes=[
+            pltpu.VMEM((wide_rows(lines[0].shape[0]), LANES), jnp.float32),
+            pltpu.VMEM((8, LANES), jnp.float32),
+            pltpu.VMEM((n, 8, LANES), jnp.float32),
+            dma((n,)),
+            dma((n,)),
             pltpu.VMEM((2, 4, part, LANES), jnp.float32),
             pltpu.VMEM((2, 4, part, LANES), jnp.float32),
             pltpu.VMEM((n_z, rows, LANES), jnp.float32),
@@ -647,56 +703,9 @@
             dma((2, steps, 4)), dma((2, 2, 4)), dma((steps, 4, 2, 2)), dma((steps, 2, 2, 2)), dma((2, steps, 2, 2, 2)),
         ],
         compiler_params=pltpu.CompilerParams(collective_id=1, has_side_effects=True, vmem_limit_bytes=60 * MB),
-    )(flat)[0]
-
-
-def share_kernel(n_dp, n_pair, in_ref, out_ref, send_sem, recv_sem):
-    n = n_dp * n_pair
-    me = lax.axis_index("dp") * n_pair + lax.axis_index("pair")
-    barrier = pltpu.get_barrier_semaphore()
-
-    def other(d):
-        k = lax.rem(me + d, n)
-        return {"dp": k // n_pair, "pair": lax.rem(k, n_pair)}
-
-    def hello(d, _):
-        pl.semaphore_signal(barrier, inc=1, device_id=other(d), device_id_type=MESH)
-        return 0
-
-    lax.fori_loop(1, n, hello, 0)
-    pl.semaphore_wait(barrier, n - 1)
-    out_ref[me] = in_ref[...]
-
-    def copy(d):
-        return pltpu.make_async_remote_copy(in_ref, out_ref.at[me], send_sem.at[d], recv_sem.at[d], device_id=other(d), device_id_type=MESH)
-
-    def go(d, _):
-        copy(d).start()
-        return 0
-
-    def stop(d, _):
-        copy(d).wait()
-        return 0
-
-    lax.fori_loop(1, n, go, 0)
-    lax.fori_loop(1, n, stop, 0)
-
-
-def share_all(value, n_dp, n_pair, ident):
-    n = n_dp * n_pair
-    spec = pl.BlockSpec(memory_space=pltpu.VMEM)
-    return pl.pallas_call(
-        functools.partial(share_kernel, n_dp, n_pair),
-        name="share_all",
-        out_shape=jax.ShapeDtypeStruct((n,) + value.shape, value.dtype),
-        in_specs=[spec],
-        out_specs=spec,
-        scratch_shapes=[pltpu.SemaphoreType.DMA((n,)), pltpu.SemaphoreType.DMA((n,))],
-        compiler_params=pltpu.CompilerParams(collective_id=ident, has_side_effects=True),
-    )(value)
-
-
-NORM_EPS = 1e-06
+    )(flat, loss, params, *lines)[:4]
+
+
 NEG_FILL = -1000000000.0
 P_ROWS = 208
 BF = jnp.bfloat16
@@ -1321,12 +1330,6 @@
     return jnp.asarray(np.pad(table, ((0, P_ROWS - PATCHES), (0, 0))))
 
 
-ADAM_EPS = 1e-08
-BETA_ONE = 0.9
-BETA_TWO = 0.95
-DECAY = 0.05
-
-
 def own_lines(flat, share, index):
     if share % LANES == 0:
         return flat.reshape(-1, LANES)
@@ -1346,37 +1349,23 @@
     images = counts.shape[0]
     index = lax.axis_index("dp") * n_pair + lax.axis_index("pair")
     extra = jnp.zeros((8, LANES), F32).at[0, :images].set((PATCHES - counts).astype(F32))
-    slab = to_tiles(own_lines(master, share, index), extra, share, n, n_pair)
-    slots = gather(slab, n_dp, n_pair, 1)
-    masked = jnp.sum(slots[:, slab.shape[0] - 2, 0, :].astype(F32))
-    held = assemble(slots, share)
-    parts = [held[i].reshape(-1)[: SHAPES[i][0] * SHAPES[i][1]].reshape(SHAPES[i]).astype(F32) if i in SMALL else matrix(held[i], i) for i in range(len(SHAPES))]
+    lines = [own_lines(one, share, index) for one in (master, moment1, moment2)]
+    steps_done = step_count[0].astype(F32)
+    params = jnp.stack([block_rates[0], block_rates[1], clip_limit[0], 1.0 - BETA_ONE**steps_done, 1.0 - BETA_TWO**steps_done])
+    *held, enc_norms, dec_norms, masked = gather(lines[0], extra, share, n_dp, n_pair, 1)
+    parts = {i: matrix(one, i) for i, one in zip(BIG, held)}
     slots_at = patch_order[:, :KEEP]
     cols = slots_at[:, :, None]
-    enc_weights = parts[1:5] + [parts[6]]
-    *saved, entering = encoder(counts, patches, cols, positions(D), [parts[0]] + enc_weights, parts[5])
+    enc_weights = [parts[i] for i in (1, 2, 3, 4, 6)]
+    *saved, entering = encoder(counts, patches, cols, positions(D), [parts[0]] + enc_weights, enc_norms)
     total = max(a for a, _ in ranges(share, n)) + slab_tiles(share, n)
-    flat, grad_entering, loss_local = decoder(
-        total, counts, masked.reshape(1, 1), patches, cols, slots_at, positions(DD), entering, parts[7:12], parts[12]
-    )
-    flat = encoder_back(flat, grad_entering, saved, enc_weights, parts[5])
-    slab_sum = reduce(flat.reshape(-1, LANES), share, n_dp, n_pair)
-    rows = share // LANES if share % LANES == 0 else (share + LANES - 1) // LANES + 1
-    grad_share = own_flat(to_lines(slab_sum, rows, share, n_pair), share, index)
-    scalars = jnp.stack([jnp.sum(grad_share * grad_share), loss_local[0, 0]])
-    shared = share_all(jnp.zeros((8, LANES), F32).at[0, :2].set(scalars), n_dp, n_pair, 2)
-    squares, loss_sum = jnp.sum(shared[:, 0, 0]), jnp.sum(shared[:, 0, 1])
-    grad_norm = jnp.sqrt(squares)
-    loss = loss_sum / masked
-    clipped = grad_share * (clip_limit[0] / (grad_norm + NORM_EPS))
-    first = BETA_ONE * moment1 + (1.0 - BETA_ONE) * clipped
-    second = BETA_TWO * moment2 + (1.0 - BETA_TWO) * clipped * clipped
-    steps_done = step_count[0].astype(F32)
-    position = index * share + jnp.arange(share)
-    rate = jnp.where(position < ENC_PARAMS, block_rates[0], block_rates[1])
-    update = first / (1.0 - BETA_ONE**steps_done) / (jnp.sqrt(second / (1.0 - BETA_TWO**steps_done)) + ADAM_EPS)
-    master_new = master - rate * (update + DECAY * master)
-    return (loss.reshape(1), grad_norm.reshape(1), first, second, master_new)
+    dec_weights = [parts[i] for i in (7, 8, 9, 10, 11)]
+    flat, grad_entering, loss_local = decoder(total, counts, masked, patches, cols, slots_at, positions(DD), entering, dec_weights, dec_norms)
+    flat = encoder_back(flat, grad_entering, saved, enc_weights, enc_norms)
+    first, second, master_new, totals = reduce(flat.reshape(-1, LANES), loss_local, params, lines, share, n_dp, n_pair)
+    loss = totals[1, 0:1] / masked[0]
+    first, second, master_new = (own_flat(one, share, index) for one in (first, second, master_new))
+    return (loss, totals[0, 0:1], first, second, master_new)
 
 
 def solution(mesh):

time: 436 us -> 416 us (0.954)
  other arithmetic: 14.9 us -> 1.35 us
  Pallas kernels: 409 us -> 399 us
  local copies, waits for them, and re-layouts: 4.95 us -> 10.2 us
    pallas_call x6 -> x2, Pallas kernels: 274 us -> 264 us  [the longest x1 141 us: reduce(): pl.pallas_call(functools.partial(reduce_kernel, n_z, n_pair, chunks, shar...]
    sub x1 -> x0, other arithmetic: 5.93 us -> none  [body(): master_new = master - rate * (update + DECAY * master)]
    unnamed x13 -> x14, local copies, waits for them, and re-layouts: 1.18 us -> 6.94 us
    reduce_sum x3 -> x0, other arithmetic: 5.63 us -> none  [the longest x1 2.46 us: body(): scalars = jnp.stack([jnp.sum(grad_share * grad_share), loss_local[0, 0]])]
where the time goes in v4:
time: 416 us
  Pallas kernels  399 us (96%)
  local copies, waits for them, and re-layouts  10.2 us (2%)
  between operations  4.54 us (1%)
    pallas_call x1, Pallas kernels, reduce(): pl.pallas_call(functools.partial(reduce_kernel, n_z, n_pair, chunks, shar...  141 us
    pallas_call x1, Pallas kernels, gather(): pl.pallas_call(functools.partial(gather_kernel, n_z, n_pair, chunks, shar...  123 us
    pallas_call x1, Pallas kernels, decoder(): pl.pallas_call(functools.partial(decoder_kernel, images), name='decoder',...  76.4 us
    pallas_call x1, Pallas kernels, encoder_back(): pl.pallas_call(functools.partial(encoder_back_kernel, images), name='enco...  36 us
    pallas_call x1, Pallas kernels, encoder(): pl.pallas_call(functools.partial(encoder_kernel, images), name='encoder',...  22.9 us

profile of v4, /device:TPU:0, one launch (start us, length us, event | category | flops | bytes accessed | tf_op | source)
XLA Modules:
  0.0 415.5 jit_solution(14164618035134156763)
XLA Ops:
  0.6 0.0 copy-start.3
  0.6 0.0 copy-start.2
  0.7 0.8 convert_bitcast_fusion
  1.4 0.6 scatter.4.extra_ref
  2.0 122.8 %gather.1 = (bf16[576,8,128]{2,1,0:T(8,128)(2,1)}, bf16[1728,8,128]{2,1,0:T(8,128)(2,1)}, bf16[576,8,128]{2,1,0:T(8,128)(2,1)}, bf16[2304,8,128]{2,1,0:T(8,128)(...) custom-call(f32[2834,128]{1,0:T(8,128)} %bitcast.75, ...), custom_call_target="tpu_custom_call" | custom-call | tf_op jit(solution)/shard_map/gather/pallas_call | solution.py:350
  124.8 0.0 copy-done.3
  124.8 0.6 fusion.1
  125.4 0.8 copy.19.cols_ref
  126.2 0.0 copy-done.2
  126.2 1.2 copy.18.refs_1_
  127.4 22.9 %encoder.1 = (bf16[256,768]{1,0:T(8,128)(2,1)}, bf16[256,768]{1,0:T(8,128)(2,1)}, f32[256,768]{1,0:T(8,128)}, f32[256,1]{1,0:T(8,128)}, bf16[256,2304]{1,0:T(8,1...) custom-call(s32[4]{0:T(128)} %counts_ref.3, ...), custom_call_target="tpu_custom_call" | custom-call | tf_op jit(solution)/shard_map/encoder/pallas_call | solution.py:1143
  150.2 76.4 %decoder.1 = (f32[11363,8,128]{2,1,0:T(8,128)}, bf16[256,512]{1,0:T(8,128)(2,1)}, f32[1,1]{1,0:T(1,128)}) custom-call(s32[4]{0:T(128)} %counts_ref.3, f32[1,1]{1,0:T(1,128)} %get-tuple-element.54.masked_ref, s32[4,64,1]{2,1,0:T(8,128)} %copy.19.cols_ref, s32[4,64]{1,0:T(4,128)} %get-tuple-element.93.rows_ref, f32[256,512]{1,0:T(8,128)} %get-tuple-element.62.entering_ref, ...), custom_call_target="tpu_custom_call" | custom-call | tf_op jit(solution)/shard_map/decoder/pallas_call | solution.py:1245
  226.7 0.0 copy-start.4
  226.7 36.0 %encoder_back.1 = f32[11363,8,128]{2,1,0:T(8,128)} custom-call(f32[11363,8,128]{2,1,0:T(8,128)} %get-tuple-element.69.flat_in, bf16[256,512]{1,0:T(8,128)(2,1)} %get-tuple-element.70.grad_entering, f32[6,768]{1,0:T(8,128)} %get-tuple-element.55.norms_ref, bf16[256,768]{1,0:T(8,128)(2,1)} %get-tuple-element.71.refs_0_, ...), custom_call_target="tpu_custom_call", output_to_operand_aliasing={{}: (0, {})} | custom-call | tf_op jit(solution)/shard_map/encoder_back/pallas_call | solution.py:1307
  264.1 0.0 copy-done.4
  264.1 0.6 pad_maximum_fusion.params
  264.7 141.3 %reduce_scatter.1 = (f32[2834,128]{1,0:T(8,128)}, f32[2834,128]{1,0:T(8,128)}, f32[2834,128]{1,0:T(8,128)}, f32[8,128]{1,0:T(8,128)}, f32[16,4,768,128]{3,2,1,0:T(8,128)}) custom-call(f32[90904,128]{1,0:T(8,128)} %bitcast.68, f32[1,1]{1,0:T(1,128)} %get-tuple-element.86.loss_in, f32[5]{0:T(128)} %pad_maximum_fusion.params, f32[2834,128]{1,0:T(8,128)} %bitcast.76, ...), custom_call_target="tpu_custom_call" | custom-call | tf_op jit(solution)/shard_map/reduce_scatter/pallas_call | solution.py:686
  406.1 1.3 fusion
  408.6 0.0 copy-start.1
  408.6 2.7 copy.27
  411.3 0.0 copy-done.1
  411.3 1.2 copy.28
  412.5 0.7 copy-done
  413.2 1.2 copy.29
  (1 shorter events, 0.0 us)
Async XLA Ops:
  0.6 124.2 %copy-start.3 = (s32[4,196]{1,0:T(4,128)S(1)}, s32[4,196]{1,0:T(4,128)}, u32[]{:S(2)}) copy-start(s32[4,196]{1,0:T(4,128)} %param.14) | copy-start | bytes 9412
  0.6 125.6 %copy-start.2 = (bf16[4,196,768]{2,0,1:T(4,128)(2,1)S(1)}, bf16[4,196,768]{2,0,1:T(4,128)(2,1)}, u32[]{:S(2)}) copy-start(bf16[4,196,768]{2,0,1:T(4,128)(2,1)} %param.13) | copy-start | bytes 3612676
  226.7 37.4 %copy-start.4 = (f32[2]{0:T(128)S(1)}, f32[2]{0:T(128)}, u32[]{:S(2)}) copy-start(f32[2]{0:T(128)} %param.19) | copy-start | bytes 28
  408.6 2.7 copy-start.1
  411.3 1.9 copy-start
